TPU v7x, 32 devices: a whole 2x2x4 slice. The times are simulated.
32 devices in a mesh: grp: 16 (over z, y, x), node: 2 (over core).
Axes of the slice: x: 2, y: 2, z: 4, core: 2. Of those that a mesh axis runs over, the one named last changes fastest.
Arguments:
- tokens: bfloat16 [4096, 2048], P(('grp', 'node')), may hold values from -6 to 6
- codes: bfloat16 [768, 2048], P(('grp', 'node')), may hold values from -3 to 3
- scales: float32 [768, 16], P(('grp', 'node')), may hold values from 0.25 to 4, as said below
- cotangent: bfloat16 [4096, 768], P(('grp', 'node')), may hold values from -6 to 6
Outputs:
- values: bfloat16 [4096, 768], P(('grp', 'node'))
- input_grad: bfloat16 [4096, 2048], P(('grp', 'node'))
- weight_grad: float32 [768, 2048], P(('grp', 'node'))
Inputs may be any that keep to these rules, and one draw needn't show every extreme that they name: Positive block scales.
All inputs are finite; a program needn't handle non-finite values.
Results may differ from a plain program's by a relative error of at most 0.012.
Values may be sent and summed in bfloat16 or wider, within the bound.
No kernel may reach another device: no remote copies, remote signals or barrier semaphores. Data moves between devices by JAX's collectives and lax.ppermute only.
A program may use at most 64 MiB of HBM per device.

v0:
```python
import jax
import jax.numpy as jnp
from jax import lax
from jax.experimental import pallas as pl
from jax.experimental.pallas import tpu as pltpu
from jax.sharding import PartitionSpec as P


AXES = ("grp", "node")
F32 = jnp.float32
BF16 = jnp.bfloat16
VMEM = pl.BlockSpec(memory_space=pltpu.VMEM)
GRANT = 12 * 1024 * 1024


def dequantize(block_codes, block_scales):
    count, width = block_codes.shape
    blocks = block_scales.shape[1]
    floats = (
        block_codes.astype(F32).reshape(count, blocks, -1)
        * block_scales[:, :, None]
        * width ** (-0.5)
    )
    return floats.reshape(count, -1).astype(BF16)


def plain_body(tokens, codes, scales, cotangent):
    rows_here = tokens.shape[0]
    groups = lax.axis_size("grp")
    nodes = lax.axis_size("node")
    per_device = codes.shape[0]
    height = cotangent.shape[1]
    floats = tokens.astype(F32)
    power = jnp.mean(floats * floats, axis=-1, keepdims=True)
    normed = (floats * lax.rsqrt(power + 1e-05)).astype(BF16)
    weight = lax.all_gather(dequantize(codes, scales), AXES, axis=0, tiled=True)
    values = jnp.dot(normed, weight.T, preferred_element_type=F32).astype(BF16)
    input_grad = jnp.dot(cotangent, weight, preferred_element_type=F32).astype(BF16)
    reordered = (
        cotangent.reshape(rows_here, groups, nodes, per_device)
        .transpose(0, 2, 1, 3)
        .reshape(rows_here, height)
    )
    factor = (rows_here * groups * nodes) ** (-0.5)
    term = jnp.einsum("tr,td->rd", reordered, normed, preferred_element_type=F32) * factor
    node_sum = lax.psum_scatter(
        term.astype(BF16), "node", scatter_dimension=0, tiled=True
    ).astype(F32)
    weight_grad = lax.psum_scatter(node_sum, "grp", scatter_dimension=0, tiled=True)
    return (values, input_grad, weight_grad)


def swap_first():
    return [(g * 2 + c, (g ^ (1 + c)) * 2 + c) for g in range(16) for c in range(2)]


def swap_second():
    return [(g * 2 + c, (g ^ (2 - c)) * 2 + c) for g in range(16) for c in range(2)]


def swap_z(k):
    return [(g * 2 + c, (g ^ (4 * k)) * 2 + c) for g in range(16) for c in range(2)]


def swap_core():
    return [(g * 2 + c, g * 2 + 1 - c) for g in range(16) for c in range(2)]


def dequantize_kernel(codes, scales, out):
    width = codes.shape[1]
    blocks = scales.shape[0]
    block = width // blocks
    inv_root = width ** (-0.5)
    by_row = scales[...].T
    for j in range(blocks):
        part = slice(j * block, (j + 1) * block)
        out[:, part] = (codes[:, part].astype(F32) * by_row[:, j : j + 1] * inv_root).astype(BF16)


def place_of(g, core, first, second, k):
    return (g ^ (first * (1 + core) + second * (2 - core) + 4 * k)) * 2 + core


PAIRS = ((0, 0), (1, 0), (0, 1), (1, 1))


def term_kernel(per, factor, tok, tok2, cot, cot2, sent, kept_cot, normed, early, late, cot_t):
    rows = tok.shape[0]
    half = 8 * per
    g = lax.axis_index("grp")
    c = lax.axis_index("node")
    cot_t[:, :rows] = cot[...].astype(F32).T
    cot_t[:, rows:] = cot2[...].astype(F32).T

    def block(core, first, second, k):
        start = pl.multiple_of(place_of(g, core, first, second, k) * per, 8)
        return cot_t[pl.ds(start, per), :]

    def picked(core, first, second):
        return jnp.concatenate([block(core, first, second, k) for k in range(4)], axis=0)

    for i, source in enumerate((tok, tok2)):
        floats = source[...].astype(F32)
        power = jnp.mean(floats * floats, axis=-1, keepdims=True)
        normed[i * rows : (i + 1) * rows, :] = (floats * lax.rsqrt(power + 1e-05)).astype(BF16)
    mine = [picked(c, first, second).astype(BF16) for first, second in PAIRS]
    other = [picked(1 - c, first, second)[:, :rows].astype(BF16) for first, second in PAIRS]
    kept_cot[: half // 2, :] = mine[0]
    kept_cot[half // 2 :, :] = mine[2]
    sent[...] = (
        jnp.dot(
            jnp.concatenate([mine[1], mine[3]], axis=0), normed[...], preferred_element_type=F32
        )
        * factor
    ).astype(BF16)
    for i in range(3):
        early[i * 4 * per : (i + 1) * 4 * per, :] = mine[i][:, :rows]
        early[(i + 3) * 4 * per : (i + 4) * 4 * per, :] = other[i]
    late[: 4 * per, :] = mine[3][:, :rows]
    late[4 * per :, :] = other[3]


def kept_kernel(factor, kept_cot, normed, near, far):
    half = near.shape[0]
    both = jnp.dot(kept_cot[...], normed[...], preferred_element_type=F32) * factor
    near[...] = both[:half, :]
    far[...] = both[half:, :]


def second_kernel(far, got, sent):
    half = sent.shape[0]
    sent[...] = (far[...] + got[half:, :].astype(F32)).astype(BF16)


def spread_kernel(near, got, got2, own, s1, s2, s3):
    per = own.shape[0]
    for k, out in enumerate((own, s1, s2, s3)):
        part = slice(k * per, (k + 1) * per)
        total = near[part, :] + got[part, :].astype(F32) + got2[part, :].astype(F32)
        out[...] = total.astype(out.dtype)


def total_kernel(own, g1, g2, g3, out):
    out[...] = own[...] + g1[...].astype(F32) + g2[...].astype(F32) + g3[...].astype(F32)


def join_kernel(w0, w1, w2, w3, out):
    per = w0.shape[0]
    for k, piece in enumerate((w0, w1, w2, w3)):
        out[k * per : (k + 1) * per, :] = piece[...]


LAST = (((1,), (1,)), ((), ()))
FIRST = (((0,), (0,)), ((), ()))


def early_kernel(normed, cot, w0, w1, w2, w3, w4, w5, values_t, grad, joined):
    count = w0.shape[0]
    rows = grad.shape[0]
    for i, piece in enumerate((w0, w1, w2, w3, w4, w5)):
        joined[i * count : (i + 1) * count, :] = piece[...]
    values_t[...] = lax.dot_general(
        joined[...], normed[:rows, :], LAST, preferred_element_type=F32
    )
    grad[...] = lax.dot_general(cot[...], joined[...], FIRST, preferred_element_type=F32)


def late_kernel(per, normed, cot, w0, w1, values_t, grad, values, input_grad, joined, full_t):
    count = w0.shape[0]
    rows = grad.shape[0]
    g = lax.axis_index("grp")
    c = lax.axis_index("node")
    joined[:count, :] = w0[...]
    joined[count:, :] = w1[...]
    late_t = lax.dot_general(joined[...], normed[:rows, :], LAST, preferred_element_type=F32)
    for i in range(4):
        for j in range(2):
            core = c if j == 0 else 1 - c
            for k in range(4):
                start = pl.multiple_of(place_of(g, core, *PAIRS[i], k) * per, 8)
                if i < 3:
                    at = (i + 3 * j) * count + k * per
                    piece = values_t[at : at + per, :]
                else:
                    at = j * count + k * per
                    piece = late_t[at : at + per, :]
                full_t[pl.ds(start, per), :] = piece
    values[...] = full_t[...].T.astype(BF16)
    input_grad[...] = (
        grad[...] + lax.dot_general(cot[...], joined[...], FIRST, preferred_element_type=F32)
    ).astype(BF16)


def plain(rows, columns, dtype):
    return jax.ShapeDtypeStruct((rows, columns), dtype)


def held(rows, columns, dtype):
    return pltpu.VMEM((rows, columns), dtype)


def move(array, pairs):
    return lax.ppermute(array, AXES, pairs)


def call(kernel, outs, *args, scratch=(), hbm=()):
    args = [
        a if i in hbm else pltpu.with_memory_space_constraint(a, pltpu.VMEM)
        for i, a in enumerate(args)
    ]
    return pl.pallas_call(
        kernel,
        out_shape=outs,
        in_specs=[VMEM] * len(args),
        out_specs=jax.tree.map(lambda _: VMEM, outs),
        scratch_shapes=scratch,
        compiler_params=pltpu.CompilerParams(vmem_limit_bytes=GRANT),
    )(*args)


def block_body(tokens, codes, scales, cotangent):
    return block_steps(tokens, codes, scales, cotangent)


def block_steps(tokens, codes, scales, cotangent):
    rows, width = tokens.shape
    height = cotangent.shape[1]
    per = codes.shape[0]
    quarter = 4 * per
    factor = (rows * 32) ** (-0.5)

    tokens2 = move(tokens, swap_core())
    cotangent2 = move(cotangent, swap_core())
    own = call(dequantize_kernel, held(per, width, BF16), codes, scales.T, hbm=(0, 1))

    sent, kept_cot, normed, early, late = call(
        lambda *refs: term_kernel(per, factor, *refs),
        [
            held(2 * quarter, width, BF16),
            held(2 * quarter, 2 * rows, BF16),
            held(2 * rows, width, BF16),
            held(6 * quarter, rows, BF16),
            held(2 * quarter, rows, BF16),
        ],
        tokens,
        tokens2,
        cotangent,
        cotangent2,
        scratch=[pltpu.VMEM((height, 2 * rows), F32)],
        hbm=(0, 2),
    )
    got = move(sent, swap_first())
    by_z = [own] + [move(own, swap_z(k)) for k in (1, 2, 3)]
    near, far = call(
        lambda *refs: kept_kernel(factor, *refs), [held(quarter, width, F32)] * 2, kept_cot, normed
    )
    w00 = call(join_kernel, held(quarter, width, BF16), *by_z)
    sent2 = call(second_kernel, held(quarter, width, BF16), far, got)
    got2 = move(sent2, swap_second())
    w10 = move(w00, swap_first())
    w01 = move(w00, swap_second())
    v00 = move(w00, swap_core())
    w11 = move(w10, swap_second())
    v10 = move(w10, swap_core())
    v01 = move(w01, swap_core())

    mine, s1, s2, s3 = call(
        spread_kernel, [held(per, width, F32)] + [held(per, width, BF16)] * 3, near, got, got2
    )
    back = [move(s, swap_z(k)) for k, s in ((1, s1), (2, s2), (3, s3))]
    values_t, grad = call(
        early_kernel,
        [held(6 * quarter, rows, F32), held(rows, width, F32)],
        normed,
        early,
        w00,
        w10,
        w01,
        v00,
        v10,
        v01,
        scratch=[pltpu.VMEM((6 * quarter, width), BF16)],
    )
    v11 = move(w11, swap_core())
    values, input_grad = call(
        lambda *refs: late_kernel(per, *refs),
        [plain(rows, height, BF16), plain(rows, width, BF16)],
        normed,
        late,
        w11,
        v11,
        values_t,
        grad,
        scratch=[pltpu.VMEM((2 * quarter, width), BF16), pltpu.VMEM((height, rows), F32)],
    )
    weight_grad = call(total_kernel, plain(per, width, F32), mine, *back)
    return (values, input_grad, weight_grad)


def solution(mesh):
    sizes = dict(mesh.shape)
    blocked = (sizes["grp"], sizes["node"]) == (16, 2)
    split = P(AXES, None)
    return jax.shard_map(
        block_body if blocked else plain_body,
        mesh=mesh,
        in_specs=(split,) * 4,
        out_specs=(split,) * 3,
        check_vma=False,
    )
```

profile of v0, /device:TPU:0, one launch (start us, length us, event | category | flops | bytes accessed | tf_op | source)
XLA Modules:
  0.0 53.8 jit_solution(10881212098098983212)
XLA Ops:
  0.6 0.0 copy-start.1
  0.6 0.6 %collective-permute-start = (bf16[128,2048]{1,0:T(8,128)(2,1)}, bf16[128,2048]{1,0:T(8,128)(2,1)S(1)}, u32[]{:S(2)}, u32[]{:S(2)}) collective-permute-start(bf16[128,2048]{1,0:T(8,128)(2,1)} %refs_0_.1), channel_id=1, source_target_pairs={{0,1},{1,0},{2,3},{3,2},{4,5},{5,4},{6,7},{7,6},{8,9},{9,8},{10,11... | collective-permute-start | bytes 1572872 | tf_op jit(solution)/shard_map/ppermute | solution.py:203
  1.2 0.1 collective-permute-start.1
  1.3 0.0 copy-start.2
  1.3 0.9 %copy-done.2 = bf16[24,2048]{1,0:T(8,128)(2,1)S(1)} copy-done((bf16[24,2048]{1,0:T(8,128)(2,1)S(1)}, bf16[24,2048]{1,0:T(8,128)(2,1)}, u32[]{:S(2)}) %copy-start.2) | copy-done | bytes 98328
  2.2 0.0 copy-start.3
  2.2 0.7 %copy-done.3 = f32[24,16]{0,1:T(8,128)S(1)} copy-done((f32[24,16]{0,1:T(8,128)S(1)}, f32[24,16]{0,1:T(8,128)}, u32[]{:S(2)}) %copy-start.3) | copy-done | bytes 1560
  2.9 0.2 shard_map.68.w0
  3.1 3.1 %collective-permute-start.2 = (bf16[24,2048]{1,0:T(8,128)(2,1)S(1)}, bf16[24,2048]{1,0:T(8,128)(2,1)S(1)}, u32[]{:S(2)}, u32[]{:S(2)}) collective-permute-start(bf16[24,2048]{1,0:T(8,128)(2,1)S(1)} %shard_map.68.w0), channel_id=1, source_target_pairs={{0,8},{1,9},{2,10},{3,11},{4,12},{5,13},{6,14},{7,15},{8,0},{9,1},... | collective-permute-start | bytes 294920 | tf_op jit(solution)/shard_map/ppermute | solution.py:203
  6.2 0.0 collective-permute-done.1.refs_3_
  6.2 0.0 collective-permute-done.refs_1_
  6.2 0.0 copy-done.1
  6.2 0.0 copy-start
  6.2 1.0 %copy-done = bf16[128,2048]{1,0:T(8,128)(2,1)S(1)} copy-done((bf16[128,2048]{1,0:T(8,128)(2,1)S(1)}, bf16[128,2048]{1,0:T(8,128)(2,1)}, u32[]{:S(2)}) %copy-start) | copy-done | bytes 524312
  7.2 0.9 %shard_map.67 = (bf16[192,2048]{1,0:T(8,128)(2,1)S(1)}, bf16[192,256]{1,0:T(8,128)(2,1)S(1)}, bf16[256,2048]{1,0:T(8,128)(2,1)S(1)}, bf16[576,128]{1,0:T(8,128)(2,1)S(1)}, bf16[192,128]{1,0:T(8,128)(2,1)S(1)}) custom-call(bf16[128,2048]{1,0:T(8,128)(2,1)S(1)} %copy-done, bf16[128,2048]{1,0:T(8,128)(2,1)S(1)} %collective-permute-done.refs_1_, ...), custom_call_target="tpu_custom_call" | custom-call | tf_op jit(solution)/shard_map/pallas_call | solution.py:211
  8.1 1.6 %collective-permute-start.12 = (bf16[192,2048]{1,0:T(8,128)(2,1)S(1)}, bf16[192,2048]{1,0:T(8,128)(2,1)S(1)}, u32[]{:S(2)}, u32[]{:S(2)}) collective-permute-start(bf16[192,2048]{1,0:T(8,128)(2,1)S(1)} %get-tuple-element.27), channel_id=1, source_target_pairs={{0,2},{1,5},{2,0},{3,7},{4,6},{5,1},{6,4},{7,3},{8,10},{9,13},{10,... | collective-permute-start | bytes 2359304 | tf_op jit(solution)/shard_map/ppermute | solution.py:203
  9.6 2.6 %collective-permute-start.3 = (bf16[24,2048]{1,0:T(8,128)(2,1)S(1)}, bf16[24,2048]{1,0:T(8,128)(2,1)S(1)}, u32[]{:S(2)}, u32[]{:S(2)}) collective-permute-start(bf16[24,2048]{1,0:T(8,128)(2,1)S(1)} %shard_map.68.w0), channel_id=1, source_target_pairs={{0,16},{1,17},{2,18},{3,19},{4,20},{5,21},{6,22},{7,23},{8,24},{9,... | collective-permute-start | bytes 294920 | tf_op jit(solution)/shard_map/ppermute | solution.py:203
  12.2 0.2 collective-permute-start.4
  12.4 0.0 collective-permute-done.2.w1
  12.4 6.8 %collective-permute-done.3.w2 = bf16[24,2048]{1,0:T(8,128)(2,1)S(1)} collective-permute-done((bf16[24,2048]{1,0:T(8,128)(2,1)S(1)}, bf16[24,2048]{1,0:T(8,128)(2,1)S(1)}, u32[]{:S(2)}, u32[]{:S(2)}) %collective-permute-start.3) | collective-permute-done | bytes 98336 | tf_op jit(solution)/shard_map/ppermute | solution.py:203
  19.2 0.0 collective-permute-done.4.w3
  19.3 1.2 %collective-permute-start.5 = (bf16[96,2048]{1,0:T(8,128)(2,1)S(1)}, bf16[96,2048]{1,0:T(8,128)(2,1)S(1)}, u32[]{:S(2)}, u32[]{:S(2)}) collective-permute-start(bf16[96,2048]{1,0:T(8,128)(2,1)S(1)} %shard_map.69.w0), channel_id=1, source_target_pairs={{0,2},{1,5},{2,0},{3,7},{4,6},{5,1},{6,4},{7,3},{8,10},{9,13},{10,... | collective-permute-start | bytes 1179656 | tf_op jit(solution)/shard_map/ppermute | solution.py:203
  20.5 0.9 %collective-permute-start.8 = (bf16[96,2048]{1,0:T(8,128)(2,1)S(1)}, bf16[96,2048]{1,0:T(8,128)(2,1)S(1)}, u32[]{:S(2)}, u32[]{:S(2)}) collective-permute-start(bf16[96,2048]{1,0:T(8,128)(2,1)S(1)} %shard_map.69.w0), channel_id=1, source_target_pairs={{0,4},{1,3},{2,6},{3,1},{4,0},{5,7},{6,2},{7,5},{8,12},{9,11},{10,... | collective-permute-start | bytes 1179656 | tf_op jit(solution)/shard_map/ppermute | solution.py:203
  21.4 8.5 %collective-permute-done.5.w1 = bf16[96,2048]{1,0:T(8,128)(2,1)S(1)} collective-permute-done((bf16[96,2048]{1,0:T(8,128)(2,1)S(1)}, bf16[96,2048]{1,0:T(8,128)(2,1)S(1)}, u32[]{:S(2)}, u32[]{:S(2)}) %collective-permute-start.5) | collective-permute-done | bytes 393248 | tf_op jit(solution)/shard_map/ppermute | solution.py:203
  29.9 2.6 %collective-permute-start.6 = (bf16[96,2048]{1,0:T(8,128)(2,1)S(1)}, bf16[96,2048]{1,0:T(8,128)(2,1)S(1)}, u32[]{:S(2)}, u32[]{:S(2)}) collective-permute-start(bf16[96,2048]{1,0:T(8,128)(2,1)S(1)} %collective-permute-done.5.w1), channel_id=1, source_target_pairs={{0,4},{1,3},{2,6},{3,1},{4,0},{5,7},{6,2},{7,5},{8,12},{9,11},{10,... | collective-permute-start | bytes 1179656 | tf_op jit(solution)/shard_map/ppermute | solution.py:203
  32.5 0.4 shard_map.72
  32.9 0.0 collective-permute-done.12.got
  32.9 0.1 shard_map.73
  32.9 0.1 collective-permute-start.13
  33.0 0.1 collective-permute-start.9
  33.1 0.5 collective-permute-start.10
  33.6 0.0 collective-permute-done.8.w2
  33.6 0.1 collective-permute-start.11
  33.7 4.5 %collective-permute-done.6.refs_2_ = bf16[96,2048]{1,0:T(8,128)(2,1)S(1)} collective-permute-done((bf16[96,2048]{1,0:T(8,128)(2,1)S(1)}, bf16[96,2048]{1,0:T(8,128)(2,1)S(1)}, u32[]{:S(2)}, u32[]{:S(2)}) %collective-permute-start.6) | collective-permute-done | bytes 393248 | tf_op jit(solution)/shard_map/ppermute | solution.py:203
  38.2 0.0 collective-permute-start.7
  38.2 4.2 %collective-permute-done.13.got2 = bf16[96,2048]{1,0:T(8,128)(2,1)S(1)} collective-permute-done((bf16[96,2048]{1,0:T(8,128)(2,1)S(1)}, bf16[96,2048]{1,0:T(8,128)(2,1)S(1)}, u32[]{:S(2)}, u32[]{:S(2)}) %collective-permute-start.13) | collective-permute-done | bytes 393248 | tf_op jit(solution)/shard_map/ppermute | solution.py:203
  42.4 0.1 shard_map.74
  42.6 2.2 %collective-permute-start.14 = (bf16[24,2048]{1,0:T(8,128)(2,1)S(1)}, bf16[24,2048]{1,0:T(8,128)(2,1)S(1)}, u32[]{:S(2)}, u32[]{:S(2)}) collective-permute-start(bf16[24,2048]{1,0:T(8,128)(2,1)S(1)} %get-tuple-element.30), channel_id=1, source_target_pairs={{0,8},{1,9},{2,10},{3,11},{4,12},{5,13},{6,14},{7,15},{8,0},{9,1},... | collective-permute-start | bytes 294920 | tf_op jit(solution)/shard_map/ppermute | solution.py:203
  44.7 0.0 collective-permute-done.9.w3
  44.7 1.1 %collective-permute-start.15 = (bf16[24,2048]{1,0:T(8,128)(2,1)S(1)}, bf16[24,2048]{1,0:T(8,128)(2,1)S(1)}, u32[]{:S(2)}, u32[]{:S(2)}) collective-permute-start(bf16[24,2048]{1,0:T(8,128)(2,1)S(1)} %get-tuple-element.31), channel_id=1, source_target_pairs={{0,16},{1,17},{2,18},{3,19},{4,20},{5,21},{6,22},{7,23},{8,24},{9,... | collective-permute-start | bytes 294920 | tf_op jit(solution)/shard_map/ppermute | solution.py:203
  45.8 0.0 collective-permute-done.10.w4
  45.8 1.4 %collective-permute-start.16 = (bf16[24,2048]{1,0:T(8,128)(2,1)S(1)}, bf16[24,2048]{1,0:T(8,128)(2,1)S(1)}, u32[]{:S(2)}, u32[]{:S(2)}) collective-permute-start(bf16[24,2048]{1,0:T(8,128)(2,1)S(1)} %get-tuple-element.32), channel_id=1, source_target_pairs={{0,24},{1,25},{2,26},{3,27},{4,28},{5,29},{6,30},{7,31},{8,16},{9,... | collective-permute-start | bytes 294920 | tf_op jit(solution)/shard_map/ppermute | solution.py:203
  47.2 0.0 collective-permute-done.11.w5
  47.2 1.2 %shard_map.70 = (f32[576,128]{1,0:T(8,128)S(1)}, f32[128,2048]{1,0:T(8,128)S(1)}) custom-call(bf16[256,2048]{1,0:T(8,128)(2,1)S(1)} %get-tuple-element.18.normed.refs_0_.refs_1_, bf16[576,128]{1,0:T(8,128)(2,1)S(1)} %get-tuple-element.20.cot, bf16[96,2048]{1,0:T(8,128)(2,1)S(1)} %shard_map.69.w0, bf16[96,2048]{1,0:T(8,128)(2,1)S(1)} %collective-permute-done.5.w1, ...), custom_call_target="tpu_custom_call" | custom-call | tf_op jit(solution)/shard_map/pallas_call | solution.py:211
  48.4 0.0 collective-permute-done.7.refs_3_
  48.4 1.4 %shard_map.71 = (bf16[128,768]{1,0:T(8,128)(2,1)}, bf16[128,2048]{1,0:T(8,128)(2,1)}) custom-call(bf16[256,2048]{1,0:T(8,128)(2,1)S(1)} %get-tuple-element.18.normed.refs_0_.refs_1_, bf16[192,128]{1,0:T(8,128)(2,1)S(1)} %get-tuple-element.19.refs_1_, bf16[96,2048]{1,0:T(8,128)(2,1)S(1)} %collective-permute-done.6.refs_2_, ...), custom_call_target="tpu_custom_call" | custom-call | tf_op jit(solution)/shard_map/pallas_call | solution.py:211
  49.8 0.0 collective-permute-done.14.g1
  49.8 3.4 %collective-permute-done.15.g2 = bf16[24,2048]{1,0:T(8,128)(2,1)S(1)} collective-permute-done((bf16[24,2048]{1,0:T(8,128)(2,1)S(1)}, bf16[24,2048]{1,0:T(8,128)(2,1)S(1)}, u32[]{:S(2)}, u32[]{:S(2)}) %collective-permute-start.15) | collective-permute-done | bytes 98336 | tf_op jit(solution)/shard_map/ppermute | solution.py:203
  53.1 0.0 collective-permute-done.16.g3
  53.1 0.7 %shard_map.75 = f32[24,2048]{1,0:T(8,128)} custom-call(f32[24,2048]{1,0:T(8,128)S(1)} %get-tuple-element.29.own, bf16[24,2048]{1,0:T(8,128)(2,1)S(1)} %collective-permute-done.14.g1, bf16[24,2048]{1,0:T(8,128)(2,1)S(1)} %collective-permute-done.15.g2, bf16[24,2048]{1,0:T(8,128)(2,1)S(1)} %collective-permute-done.16.g3), custom_call_target="tpu_custom_call" | custom-call | tf_op jit(solution)/shard_map/pallas_call | solution.py:211
  (1 shorter events, 0.0 us)
Async XLA Ops:
  0.6 5.5 %copy-start.1 = (bf16[128,768]{1,0:T(8,128)(2,1)S(1)}, bf16[128,768]{1,0:T(8,128)(2,1)}, u32[]{:S(2)}) copy-start(bf16[128,768]{1,0:T(8,128)(2,1)} %refs_2_.1) | copy-start | bytes 589828
  0.6 5.5 %collective-permute-start = (bf16[128,2048]{1,0:T(8,128)(2,1)}, bf16[128,2048]{1,0:T(8,128)(2,1)S(1)}, u32[]{:S(2)}, u32[]{:S(2)}) collective-permute-start(bf16[128,2048]{1,0:T(8,128)(2,1)} %refs_0_.1), channel_id=1, source_target_pairs={{0,1},{1,0},{2,3},{3,2},{4,5},{5,4},{6,7},{7,6},{8,9},{9,8},{10,11... | collective-permute-start | bytes 1572872 | tf_op jit(solution)/shard_map/ppermute | solution.py:203
  1.2 5.0 %collective-permute-start.1 = (bf16[128,768]{1,0:T(8,128)(2,1)}, bf16[128,768]{1,0:T(8,128)(2,1)S(1)}, u32[]{:S(2)}, u32[]{:S(2)}) collective-permute-start(bf16[128,768]{1,0:T(8,128)(2,1)} %refs_2_.1), channel_id=1, source_target_pairs={{0,1},{1,0},{2,3},{3,2},{4,5},{5,4},{6,7},{7,6},{8,9},{9,8},{10,11... | collective-permute-start | bytes 589832 | tf_op jit(solution)/shard_map/ppermute | solution.py:203
  1.3 0.9 %copy-start.2 = (bf16[24,2048]{1,0:T(8,128)(2,1)S(1)}, bf16[24,2048]{1,0:T(8,128)(2,1)}, u32[]{:S(2)}) copy-start(bf16[24,2048]{1,0:T(8,128)(2,1)} %codes.1) | copy-start | bytes 294916
  2.2 0.7 %copy-start.3 = (f32[24,16]{0,1:T(8,128)S(1)}, f32[24,16]{0,1:T(8,128)}, u32[]{:S(2)}) copy-start(f32[24,16]{0,1:T(8,128)} %param.6) | copy-start | bytes 4612
  3.1 9.3 %collective-permute-start.2 = (bf16[24,2048]{1,0:T(8,128)(2,1)S(1)}, bf16[24,2048]{1,0:T(8,128)(2,1)S(1)}, u32[]{:S(2)}, u32[]{:S(2)}) collective-permute-start(bf16[24,2048]{1,0:T(8,128)(2,1)S(1)} %shard_map.68.w0), channel_id=1, source_target_pairs={{0,8},{1,9},{2,10},{3,11},{4,12},{5,13},{6,14},{7,15},{8,0},{9,1},... | collective-permute-start | bytes 294920 | tf_op jit(solution)/shard_map/ppermute | solution.py:203
  6.2 1.0 %copy-start = (bf16[128,2048]{1,0:T(8,128)(2,1)S(1)}, bf16[128,2048]{1,0:T(8,128)(2,1)}, u32[]{:S(2)}) copy-start(bf16[128,2048]{1,0:T(8,128)(2,1)} %refs_0_.1) | copy-start | bytes 1572868
  8.1 24.8 %collective-permute-start.12 = (bf16[192,2048]{1,0:T(8,128)(2,1)S(1)}, bf16[192,2048]{1,0:T(8,128)(2,1)S(1)}, u32[]{:S(2)}, u32[]{:S(2)}) collective-permute-start(bf16[192,2048]{1,0:T(8,128)(2,1)S(1)} %get-tuple-element.27), channel_id=1, source_target_pairs={{0,2},{1,5},{2,0},{3,7},{4,6},{5,1},{6,4},{7,3},{8,10},{9,13},{10,... | collective-permute-start | bytes 2359304 | tf_op jit(solution)/shard_map/ppermute | solution.py:203
  9.6 9.6 %collective-permute-start.3 = (bf16[24,2048]{1,0:T(8,128)(2,1)S(1)}, bf16[24,2048]{1,0:T(8,128)(2,1)S(1)}, u32[]{:S(2)}, u32[]{:S(2)}) collective-permute-start(bf16[24,2048]{1,0:T(8,128)(2,1)S(1)} %shard_map.68.w0), channel_id=1, source_target_pairs={{0,16},{1,17},{2,18},{3,19},{4,20},{5,21},{6,22},{7,23},{8,24},{9,... | collective-permute-start | bytes 294920 | tf_op jit(solution)/shard_map/ppermute | solution.py:203
  12.2 7.0 %collective-permute-start.4 = (bf16[24,2048]{1,0:T(8,128)(2,1)S(1)}, bf16[24,2048]{1,0:T(8,128)(2,1)S(1)}, u32[]{:S(2)}, u32[]{:S(2)}) collective-permute-start(bf16[24,2048]{1,0:T(8,128)(2,1)S(1)} %shard_map.68.w0), channel_id=1, source_target_pairs={{0,24},{1,25},{2,26},{3,27},{4,28},{5,29},{6,30},{7,31},{8,16},{9,... | collective-permute-start | bytes 294920 | tf_op jit(solution)/shard_map/ppermute | solution.py:203
  19.3 10.6 %collective-permute-start.5 = (bf16[96,2048]{1,0:T(8,128)(2,1)S(1)}, bf16[96,2048]{1,0:T(8,128)(2,1)S(1)}, u32[]{:S(2)}, u32[]{:S(2)}) collective-permute-start(bf16[96,2048]{1,0:T(8,128)(2,1)S(1)} %shard_map.69.w0), channel_id=1, source_target_pairs={{0,2},{1,5},{2,0},{3,7},{4,6},{5,1},{6,4},{7,3},{8,10},{9,13},{10,... | collective-permute-start | bytes 1179656 | tf_op jit(solution)/shard_map/ppermute | solution.py:203
  20.5 13.1 %collective-permute-start.8 = (bf16[96,2048]{1,0:T(8,128)(2,1)S(1)}, bf16[96,2048]{1,0:T(8,128)(2,1)S(1)}, u32[]{:S(2)}, u32[]{:S(2)}) collective-permute-start(bf16[96,2048]{1,0:T(8,128)(2,1)S(1)} %shard_map.69.w0), channel_id=1, source_target_pairs={{0,4},{1,3},{2,6},{3,1},{4,0},{5,7},{6,2},{7,5},{8,12},{9,11},{10,... | collective-permute-start | bytes 1179656 | tf_op jit(solution)/shard_map/ppermute | solution.py:203
  29.9 8.3 %collective-permute-start.6 = (bf16[96,2048]{1,0:T(8,128)(2,1)S(1)}, bf16[96,2048]{1,0:T(8,128)(2,1)S(1)}, u32[]{:S(2)}, u32[]{:S(2)}) collective-permute-start(bf16[96,2048]{1,0:T(8,128)(2,1)S(1)} %collective-permute-done.5.w1), channel_id=1, source_target_pairs={{0,4},{1,3},{2,6},{3,1},{4,0},{5,7},{6,2},{7,5},{8,12},{9,11},{10,... | collective-permute-start | bytes 1179656 | tf_op jit(solution)/shard_map/ppermute | solution.py:203
  32.9 9.5 %collective-permute-start.13 = (bf16[96,2048]{1,0:T(8,128)(2,1)S(1)}, bf16[96,2048]{1,0:T(8,128)(2,1)S(1)}, u32[]{:S(2)}, u32[]{:S(2)}) collective-permute-start(bf16[96,2048]{1,0:T(8,128)(2,1)S(1)} %shard_map.73), channel_id=1, source_target_pairs={{0,4},{1,3},{2,6},{3,1},{4,0},{5,7},{6,2},{7,5},{8,12},{9,11},{10,... | collective-permute-start | bytes 1179656 | tf_op jit(solution)/shard_map/ppermute | solution.py:203
  33.0 11.7 %collective-permute-start.9 = (bf16[96,2048]{1,0:T(8,128)(2,1)S(1)}, bf16[96,2048]{1,0:T(8,128)(2,1)S(1)}, u32[]{:S(2)}, u32[]{:S(2)}) collective-permute-start(bf16[96,2048]{1,0:T(8,128)(2,1)S(1)} %shard_map.69.w0), channel_id=1, source_target_pairs={{0,1},{1,0},{2,3},{3,2},{4,5},{5,4},{6,7},{7,6},{8,9},{9,8},{10,11... | collective-permute-start | bytes 1179656 | tf_op jit(solution)/shard_map/ppermute | solution.py:203
  33.1 12.7 %collective-permute-start.10 = (bf16[96,2048]{1,0:T(8,128)(2,1)S(1)}, bf16[96,2048]{1,0:T(8,128)(2,1)S(1)}, u32[]{:S(2)}, u32[]{:S(2)}) collective-permute-start(bf16[96,2048]{1,0:T(8,128)(2,1)S(1)} %collective-permute-done.5.w1), channel_id=1, source_target_pairs={{0,1},{1,0},{2,3},{3,2},{4,5},{5,4},{6,7},{7,6},{8,9},{9,8},{10,11... | collective-permute-start | bytes 1179656 | tf_op jit(solution)/shard_map/ppermute | solution.py:203
  33.6 13.6 %collective-permute-start.11 = (bf16[96,2048]{1,0:T(8,128)(2,1)S(1)}, bf16[96,2048]{1,0:T(8,128)(2,1)S(1)}, u32[]{:S(2)}, u32[]{:S(2)}) collective-permute-start(bf16[96,2048]{1,0:T(8,128)(2,1)S(1)} %collective-permute-done.8.w2), channel_id=1, source_target_pairs={{0,1},{1,0},{2,3},{3,2},{4,5},{5,4},{6,7},{7,6},{8,9},{9,8},{10,11... | collective-permute-start | bytes 1179656 | tf_op jit(solution)/shard_map/ppermute | solution.py:203
  38.2 10.2 %collective-permute-start.7 = (bf16[96,2048]{1,0:T(8,128)(2,1)S(1)}, bf16[96,2048]{1,0:T(8,128)(2,1)S(1)}, u32[]{:S(2)}, u32[]{:S(2)}) collective-permute-start(bf16[96,2048]{1,0:T(8,128)(2,1)S(1)} %collective-permute-done.6.refs_2_), channel_id=1, source_target_pairs={{0,1},{1,0},{2,3},{3,2},{4,5},{5,4},{6,7},{7,6},{8,9},{9,8},{10,11... | collective-permute-start | bytes 1179656 | tf_op jit(solution)/shard_map/ppermute | solution.py:203
  42.6 7.2 %collective-permute-start.14 = (bf16[24,2048]{1,0:T(8,128)(2,1)S(1)}, bf16[24,2048]{1,0:T(8,128)(2,1)S(1)}, u32[]{:S(2)}, u32[]{:S(2)}) collective-permute-start(bf16[24,2048]{1,0:T(8,128)(2,1)S(1)} %get-tuple-element.30), channel_id=1, source_target_pairs={{0,8},{1,9},{2,10},{3,11},{4,12},{5,13},{6,14},{7,15},{8,0},{9,1},... | collective-permute-start | bytes 294920 | tf_op jit(solution)/shard_map/ppermute | solution.py:203
  44.7 8.4 %collective-permute-start.15 = (bf16[24,2048]{1,0:T(8,128)(2,1)S(1)}, bf16[24,2048]{1,0:T(8,128)(2,1)S(1)}, u32[]{:S(2)}, u32[]{:S(2)}) collective-permute-start(bf16[24,2048]{1,0:T(8,128)(2,1)S(1)} %get-tuple-element.31), channel_id=1, source_target_pairs={{0,16},{1,17},{2,18},{3,19},{4,20},{5,21},{6,22},{7,23},{8,24},{9,... | collective-permute-start | bytes 294920 | tf_op jit(solution)/shard_map/ppermute | solution.py:203
  45.8 7.3 %collective-permute-start.16 = (bf16[24,2048]{1,0:T(8,128)(2,1)S(1)}, bf16[24,2048]{1,0:T(8,128)(2,1)S(1)}, u32[]{:S(2)}, u32[]{:S(2)}) collective-permute-start(bf16[24,2048]{1,0:T(8,128)(2,1)S(1)} %get-tuple-element.32), channel_id=1, source_target_pairs={{0,24},{1,25},{2,26},{3,27},{4,28},{5,29},{6,30},{7,31},{8,16},{9,... | collective-permute-start | bytes 294920 | tf_op jit(solution)/shard_map/ppermute | solution.py:203
where the time goes:
time: 54.1 us; the launch traced here: 53.8 us
  waiting for transfers between devices  27.4 us (51%)
  starting transfers between devices  18.1 us (33%)
  Pallas kernels  4.94 us (9%)
  local copies, waits for them, and re-layouts  2.63 us (5%)
  between operations  0.74 us (1%)
    ppermute x17, waiting for transfers between devices, move(): return lax.ppermute(array, AXES, pairs)  27.4 us
    ppermute x17, starting transfers between devices, move(): return lax.ppermute(array, AXES, pairs)  18.1 us
    pallas_call x9, Pallas kernels, call(): pl.pallas_call(kernel, out_shape=outs, in_specs=[VMEM] * len(args), out_s...  4.94 us
    unnamed x8, local copies, waits for them, and re-layouts  2.63 us
  transfers between devices with their start and end apart: 17, of which 5 were waited for; matrix products, arithmetic and copies ran while one was open for 0% of the time, Pallas kernels for 8%

commit v1 on v0

--- a/solution.py
+++ b/solution.py
@@ -10,6 +10,7 @@
 F32 = jnp.float32
 BF16 = jnp.bfloat16
 VMEM = pl.BlockSpec(memory_space=pltpu.VMEM)
+FAR = pl.BlockSpec(memory_space=pltpu.HBM)
 GRANT = 12 * 1024 * 1024
 
 
@@ -66,58 +67,99 @@
     return [(g * 2 + c, g * 2 + 1 - c) for g in range(16) for c in range(2)]
 
 
-def dequantize_kernel(codes, scales, out):
-    width = codes.shape[1]
+def place_of(g, core, first, second, k):
+    return (g ^ (first * (1 + core) + second * (2 - core) + 4 * k)) * 2 + core
+
+
+PAIRS = ((0, 0), (1, 0), (0, 1), (1, 1))
+
+
+def normalized(tok):
+    floats = tok[...].astype(F32)
+    power = jnp.mean(floats * floats, axis=-1, keepdims=True)
+    return (floats * lax.rsqrt(power + 1e-05)).astype(BF16)
+
+
+def own_kernel(
+    per,
+    tok_far,
+    cot_far,
+    codes_far,
+    scales_far,
+    weight,
+    normed,
+    early,
+    late,
+    cot_t,
+    tok,
+    cot,
+    codes,
+    scales,
+    sem,
+):
+    pairs = ((codes_far, codes), (scales_far, scales), (cot_far, cot), (tok_far, tok))
+    loads = [pltpu.make_async_copy(x, y, sem.at[i]) for i, (x, y) in enumerate(pairs)]
+    for load in loads:
+        load.start()
+    g = lax.axis_index("grp")
+    c = lax.axis_index("node")
+    width = tok.shape[1]
     blocks = scales.shape[0]
     block = width // blocks
     inv_root = width ** (-0.5)
+    loads[0].wait()
+    loads[1].wait()
     by_row = scales[...].T
     for j in range(blocks):
         part = slice(j * block, (j + 1) * block)
-        out[:, part] = (codes[:, part].astype(F32) * by_row[:, j : j + 1] * inv_root).astype(BF16)
-
-
-def place_of(g, core, first, second, k):
-    return (g ^ (first * (1 + core) + second * (2 - core) + 4 * k)) * 2 + core
-
-
-PAIRS = ((0, 0), (1, 0), (0, 1), (1, 1))
-
-
-def term_kernel(per, factor, tok, tok2, cot, cot2, sent, kept_cot, normed, early, late, cot_t):
-    rows = tok.shape[0]
-    half = 8 * per
+        weight[:, part] = (codes[:, part].astype(F32) * by_row[:, j : j + 1] * inv_root).astype(
+            BF16
+        )
+    loads[2].wait()
+    cot_t[...] = cot[...].astype(F32).T
+    loads[3].wait()
+    normed[...] = normalized(tok)
+    for i in range(4):
+        for j in range(2):
+            core = c if j == 0 else 1 - c
+            for k in range(4):
+                start = pl.multiple_of(place_of(g, core, *PAIRS[i], k) * per, 8)
+                piece = cot_t[pl.ds(start, per), :]
+                if i < 3:
+                    at = ((i + 3 * j) * 4 + k) * per
+                    early[at : at + per, :] = piece
+                else:
+                    at = (j * 4 + k) * per
+                    late[at : at + per, :] = piece
+
+
+def term_kernel(
+    per, factor, tok2, cot2, normed1, early1, late1, sent, kept_cot, normed, early, late, cot_t
+):
+    rows = tok2.shape[0]
+    quarter = 4 * per
     g = lax.axis_index("grp")
     c = lax.axis_index("node")
-    cot_t[:, :rows] = cot[...].astype(F32).T
-    cot_t[:, rows:] = cot2[...].astype(F32).T
-
-    def block(core, first, second, k):
-        start = pl.multiple_of(place_of(g, core, first, second, k) * per, 8)
-        return cot_t[pl.ds(start, per), :]
-
-    def picked(core, first, second):
-        return jnp.concatenate([block(core, first, second, k) for k in range(4)], axis=0)
-
-    for i, source in enumerate((tok, tok2)):
-        floats = source[...].astype(F32)
-        power = jnp.mean(floats * floats, axis=-1, keepdims=True)
-        normed[i * rows : (i + 1) * rows, :] = (floats * lax.rsqrt(power + 1e-05)).astype(BF16)
-    mine = [picked(c, first, second).astype(BF16) for first, second in PAIRS]
-    other = [picked(1 - c, first, second)[:, :rows].astype(BF16) for first, second in PAIRS]
-    kept_cot[: half // 2, :] = mine[0]
-    kept_cot[half // 2 :, :] = mine[2]
-    sent[...] = (
-        jnp.dot(
-            jnp.concatenate([mine[1], mine[3]], axis=0), normed[...], preferred_element_type=F32
-        )
-        * factor
-    ).astype(BF16)
-    for i in range(3):
-        early[i * 4 * per : (i + 1) * 4 * per, :] = mine[i][:, :rows]
-        early[(i + 3) * 4 * per : (i + 4) * 4 * per, :] = other[i]
-    late[: 4 * per, :] = mine[3][:, :rows]
-    late[4 * per :, :] = other[3]
+    normed[:rows, :] = normed1[...]
+    normed[rows:, :] = normalized(tok2)
+    cot_t[...] = cot2[...].astype(F32).T
+    early[...] = early1[...].astype(BF16)
+    late[...] = late1[...].astype(BF16)
+
+    def both(i, own):
+        first, second = PAIRS[i]
+        swapped = [
+            cot_t[pl.ds(pl.multiple_of(place_of(g, c, first, second, k) * per, 8), per), :]
+            for k in range(4)
+        ]
+        return jnp.concatenate([own, jnp.concatenate(swapped, axis=0)], axis=1).astype(BF16)
+
+    kept_cot[:quarter, :] = both(0, early1[:quarter, :])
+    kept_cot[quarter:, :] = both(2, early1[2 * quarter : 3 * quarter, :])
+    going = jnp.concatenate(
+        [both(1, early1[quarter : 2 * quarter, :]), both(3, late1[:quarter, :])], axis=0
+    )
+    sent[...] = (jnp.dot(going, normed[...], preferred_element_type=F32) * factor).astype(BF16)
 
 
 def kept_kernel(factor, kept_cot, normed, near, far):
@@ -203,15 +245,15 @@
     return lax.ppermute(array, AXES, pairs)
 
 
-def call(kernel, outs, *args, scratch=(), hbm=()):
+def call(kernel, outs, *args, scratch=(), far=()):
     args = [
-        a if i in hbm else pltpu.with_memory_space_constraint(a, pltpu.VMEM)
+        pltpu.with_memory_space_constraint(a, pltpu.HBM if i in far else pltpu.VMEM)
         for i, a in enumerate(args)
     ]
     return pl.pallas_call(
         kernel,
         out_shape=outs,
-        in_specs=[VMEM] * len(args),
+        in_specs=[FAR if i in far else VMEM for i in range(len(args))],
         out_specs=jax.tree.map(lambda _: VMEM, outs),
         scratch_shapes=scratch,
         compiler_params=pltpu.CompilerParams(vmem_limit_bytes=GRANT),
@@ -231,8 +273,28 @@
 
     tokens2 = move(tokens, swap_core())
     cotangent2 = move(cotangent, swap_core())
-    own = call(dequantize_kernel, held(per, width, BF16), codes, scales.T, hbm=(0, 1))
-
+    own, normed1, early1, late1 = call(
+        lambda *refs: own_kernel(per, *refs),
+        [
+            held(per, width, BF16),
+            held(rows, width, BF16),
+            held(6 * quarter, rows, F32),
+            held(2 * quarter, rows, F32),
+        ],
+        tokens,
+        cotangent,
+        codes,
+        scales.T,
+        scratch=[
+            pltpu.VMEM((height, rows), F32),
+            pltpu.VMEM((rows, width), BF16),
+            pltpu.VMEM((rows, height), BF16),
+            pltpu.VMEM((per, width), BF16),
+            pltpu.VMEM((scales.shape[1], per), F32),
+            pltpu.SemaphoreType.DMA((4,)),
+        ],
+        far=(0, 1, 2, 3),
+    )
     sent, kept_cot, normed, early, late = call(
         lambda *refs: term_kernel(per, factor, *refs),
         [
@@ -242,12 +304,12 @@
             held(6 * quarter, rows, BF16),
             held(2 * quarter, rows, BF16),
         ],
-        tokens,
         tokens2,
-        cotangent,
         cotangent2,
-        scratch=[pltpu.VMEM((height, 2 * rows), F32)],
-        hbm=(0, 2),
+        normed1,
+        early1,
+        late1,
+        scratch=[pltpu.VMEM((height, rows), F32)],
     )
     got = move(sent, swap_first())
     by_z = [own] + [move(own, swap_z(k)) for k in (1, 2, 3)]
@@ -260,7 +322,7 @@
     w10 = move(w00, swap_first())
     w01 = move(w00, swap_second())
     v00 = move(w00, swap_core())
-    w11 = move(w10, swap_second())
+    w11 = move(w01, swap_first())
     v10 = move(w10, swap_core())
     v01 = move(w01, swap_core())
 

time: 54.1 us -> 53 us (0.980)
  local copies, waits for them, and re-layouts: 2.63 us -> 0 us
  Pallas kernels: 4.94 us -> 6.01 us
  waiting for transfers between devices: 27.4 us -> 28.1 us
    unnamed x8 -> x0, local copies, waits for them, and re-layouts: 2.63 us -> none
    pallas_call x9, Pallas kernels: 4.94 us -> 6.01 us  [call(): pl.pallas_call(kernel, out_shape=outs, in_specs=[FAR if i in far else VME...]
    ppermute x17, waiting for transfers between devices: 27.4 us -> 28.1 us  [move(): return lax.ppermute(array, AXES, pairs)]
  transfers between devices with their start and end apart: 17 -> 17, of which waited for: 5 -> 5; matrix products, arithmetic and copies ran while one was open for 0% -> 0% of each run, Pallas kernels for 8% -> 10%
where the time goes in v1:
time: 53 us; the launch traced here: 52.8 us
  waiting for transfers between devices  28.1 us (53%)
  starting transfers between devices  18 us (34%)
  Pallas kernels  6.01 us (11%)
  between operations  0.7 us (1%)
    ppermute x17, waiting for transfers between devices, move(): return lax.ppermute(array, AXES, pairs)  28.1 us
    ppermute x17, starting transfers between devices, move(): return lax.ppermute(array, AXES, pairs)  18 us
    pallas_call x9, Pallas kernels, call(): pl.pallas_call(kernel, out_shape=outs, in_specs=[FAR if i in far else VME...  6.01 us
  transfers between devices with their start and end apart: 17, of which 5 were waited for; matrix products, arithmetic and copies ran while one was open for 0% of the time, Pallas kernels for 10%

profile of v1, /device:TPU:0, one launch (start us, length us, event | category | flops | bytes accessed | tf_op | source)
XLA Modules:
  0.0 52.8 jit_solution(6104592342095366542)
XLA Ops:
  0.6 0.6 %collective-permute-start = (bf16[128,2048]{1,0:T(8,128)(2,1)}, bf16[128,2048]{1,0:T(8,128)(2,1)S(1)}, u32[]{:S(2)}, u32[]{:S(2)}) collective-permute-start(bf16[128,2048]{1,0:T(8,128)(2,1)} %refs_0_.1), channel_id=1, source_target_pairs={{0,1},{1,0},{2,3},{3,2},{4,5},{5,4},{6,7},{7,6},{8,9},{9,8},{10,11... | collective-permute-start | bytes 1572872 | tf_op jit(solution)/shard_map/ppermute | solution.py:245
  1.2 0.1 collective-permute-start.1
  1.3 1.5 %shard_map.67 = (bf16[24,2048]{1,0:T(8,128)(2,1)S(1)}, bf16[128,2048]{1,0:T(8,128)(2,1)S(1)}, f32[576,128]{1,0:T(8,128)S(1)}, f32[192,128]{1,0:T(8,128)S(1)}) custom-call(bf16[128,2048]{1,0:T(8,128)(2,1)} %refs_0_.1, bf16[128,768]{1,0:T(8,128)(2,1)} %refs_1_.1, bf16[24,2048]{1,0:T(8,128)(2,1)} %refs_2_.1, f32[16,24]{1,0:T(8,128)} %bitcast.1), custom_call_target="tpu_custom_call" | custom-call | tf_op jit(solution)/shard_map/pallas_call | solution.py:253
  2.8 3.1 %collective-permute-start.2 = (bf16[24,2048]{1,0:T(8,128)(2,1)S(1)}, bf16[24,2048]{1,0:T(8,128)(2,1)S(1)}, u32[]{:S(2)}, u32[]{:S(2)}) collective-permute-start(bf16[24,2048]{1,0:T(8,128)(2,1)S(1)} %get-tuple-element.27.w0), channel_id=1, source_target_pairs={{0,8},{1,9},{2,10},{3,11},{4,12},{5,13},{6,14},{7,15},{8,0},{9,1},... | collective-permute-start | bytes 294920 | tf_op jit(solution)/shard_map/ppermute | solution.py:245
  5.8 0.0 collective-permute-done.1.refs_1_
  5.8 0.0 collective-permute-done.refs_0_
  5.8 0.6 %shard_map.68 = (bf16[192,2048]{1,0:T(8,128)(2,1)S(1)}, bf16[192,256]{1,0:T(8,128)(2,1)S(1)}, bf16[256,2048]{1,0:T(8,128)(2,1)S(1)}, bf16[576,128]{1,0:T(8,128)(2,1)S(1)}, bf16[192,128]{1,0:T(8,128)(2,1)S(1)}) custom-call(bf16[128,2048]{1,0:T(8,128)(2,1)S(1)} %collective-permute-done.refs_0_, bf16[128,768]{1,0:T(8,128)(2,1)S(1)} %collective-permute-done.1.refs_1_, ...), custom_call_target="tpu_custom_call" | custom-call | tf_op jit(solution)/shard_map/pallas_call | solution.py:253
  6.5 1.6 %collective-permute-start.12 = (bf16[192,2048]{1,0:T(8,128)(2,1)S(1)}, bf16[192,2048]{1,0:T(8,128)(2,1)S(1)}, u32[]{:S(2)}, u32[]{:S(2)}) collective-permute-start(bf16[192,2048]{1,0:T(8,128)(2,1)S(1)} %get-tuple-element.35), channel_id=1, source_target_pairs={{0,2},{1,5},{2,0},{3,7},{4,6},{5,1},{6,4},{7,3},{8,10},{9,13},{10,... | collective-permute-start | bytes 2359304 | tf_op jit(solution)/shard_map/ppermute | solution.py:245
  8.1 2.6 %collective-permute-start.3 = (bf16[24,2048]{1,0:T(8,128)(2,1)S(1)}, bf16[24,2048]{1,0:T(8,128)(2,1)S(1)}, u32[]{:S(2)}, u32[]{:S(2)}) collective-permute-start(bf16[24,2048]{1,0:T(8,128)(2,1)S(1)} %get-tuple-element.27.w0), channel_id=1, source_target_pairs={{0,16},{1,17},{2,18},{3,19},{4,20},{5,21},{6,22},{7,23},{8,24},{9,... | collective-permute-start | bytes 294920 | tf_op jit(solution)/shard_map/ppermute | solution.py:245
  10.7 0.2 collective-permute-start.4
  10.9 0.0 collective-permute-done.2.w1
  10.9 6.8 %collective-permute-done.3.w2 = bf16[24,2048]{1,0:T(8,128)(2,1)S(1)} collective-permute-done((bf16[24,2048]{1,0:T(8,128)(2,1)S(1)}, bf16[24,2048]{1,0:T(8,128)(2,1)S(1)}, u32[]{:S(2)}, u32[]{:S(2)}) %collective-permute-start.3) | collective-permute-done | bytes 98336 | tf_op jit(solution)/shard_map/ppermute | solution.py:245
  17.7 0.0 collective-permute-done.4.w3
  17.7 1.4 %collective-permute-start.5 = (bf16[96,2048]{1,0:T(8,128)(2,1)S(1)}, bf16[96,2048]{1,0:T(8,128)(2,1)S(1)}, u32[]{:S(2)}, u32[]{:S(2)}) collective-permute-start(bf16[96,2048]{1,0:T(8,128)(2,1)S(1)} %shard_map.69.w0), channel_id=1, source_target_pairs={{0,4},{1,3},{2,6},{3,1},{4,0},{5,7},{6,2},{7,5},{8,12},{9,11},{10,... | collective-permute-start | bytes 1179656 | tf_op jit(solution)/shard_map/ppermute | solution.py:245
  19.1 1.2 %collective-permute-start.8 = (bf16[96,2048]{1,0:T(8,128)(2,1)S(1)}, bf16[96,2048]{1,0:T(8,128)(2,1)S(1)}, u32[]{:S(2)}, u32[]{:S(2)}) collective-permute-start(bf16[96,2048]{1,0:T(8,128)(2,1)S(1)} %shard_map.69.w0), channel_id=1, source_target_pairs={{0,2},{1,5},{2,0},{3,7},{4,6},{5,1},{6,4},{7,3},{8,10},{9,13},{10,... | collective-permute-start | bytes 1179656 | tf_op jit(solution)/shard_map/ppermute | solution.py:245
  20.3 9.5 %collective-permute-done.5.w2 = bf16[96,2048]{1,0:T(8,128)(2,1)S(1)} collective-permute-done((bf16[96,2048]{1,0:T(8,128)(2,1)S(1)}, bf16[96,2048]{1,0:T(8,128)(2,1)S(1)}, u32[]{:S(2)}, u32[]{:S(2)}) %collective-permute-start.5) | collective-permute-done | bytes 393248 | tf_op jit(solution)/shard_map/ppermute | solution.py:245
  29.8 0.3 collective-permute-start.6
  30.1 0.4 shard_map.72
  30.4 0.0 collective-permute-done.12.got
  30.5 0.1 shard_map.73
  30.5 1.1 %collective-permute-start.13 = (bf16[96,2048]{1,0:T(8,128)(2,1)S(1)}, bf16[96,2048]{1,0:T(8,128)(2,1)S(1)}, u32[]{:S(2)}, u32[]{:S(2)}) collective-permute-start(bf16[96,2048]{1,0:T(8,128)(2,1)S(1)} %shard_map.73), channel_id=1, source_target_pairs={{0,4},{1,3},{2,6},{3,1},{4,0},{5,7},{6,2},{7,5},{8,12},{9,11},{10,... | collective-permute-start | bytes 1179656 | tf_op jit(solution)/shard_map/ppermute | solution.py:245
  31.6 0.0 collective-permute-start.9
  31.6 0.5 collective-permute-start.11
  32.1 0.0 collective-permute-done.8.w1
  32.1 0.0 collective-permute-start.10
  32.1 5.5 %collective-permute-done.6.refs_2_ = bf16[96,2048]{1,0:T(8,128)(2,1)S(1)} collective-permute-done((bf16[96,2048]{1,0:T(8,128)(2,1)S(1)}, bf16[96,2048]{1,0:T(8,128)(2,1)S(1)}, u32[]{:S(2)}, u32[]{:S(2)}) %collective-permute-start.6) | collective-permute-done | bytes 393248 | tf_op jit(solution)/shard_map/ppermute | solution.py:245
  37.6 0.0 collective-permute-start.7
  37.6 0.8 %collective-permute-done.13.got2 = bf16[96,2048]{1,0:T(8,128)(2,1)S(1)} collective-permute-done((bf16[96,2048]{1,0:T(8,128)(2,1)S(1)}, bf16[96,2048]{1,0:T(8,128)(2,1)S(1)}, u32[]{:S(2)}, u32[]{:S(2)}) %collective-permute-start.13) | collective-permute-done | bytes 393248 | tf_op jit(solution)/shard_map/ppermute | solution.py:245
  38.4 0.1 shard_map.74
  38.5 2.8 %collective-permute-start.14 = (bf16[24,2048]{1,0:T(8,128)(2,1)S(1)}, bf16[24,2048]{1,0:T(8,128)(2,1)S(1)}, u32[]{:S(2)}, u32[]{:S(2)}) collective-permute-start(bf16[24,2048]{1,0:T(8,128)(2,1)S(1)} %get-tuple-element.38), channel_id=1, source_target_pairs={{0,8},{1,9},{2,10},{3,11},{4,12},{5,13},{6,14},{7,15},{8,0},{9,1},... | collective-permute-start | bytes 294920 | tf_op jit(solution)/shard_map/ppermute | solution.py:245
  41.3 0.0 collective-permute-done.9.w3
  41.3 1.1 %collective-permute-start.15 = (bf16[24,2048]{1,0:T(8,128)(2,1)S(1)}, bf16[24,2048]{1,0:T(8,128)(2,1)S(1)}, u32[]{:S(2)}, u32[]{:S(2)}) collective-permute-start(bf16[24,2048]{1,0:T(8,128)(2,1)S(1)} %get-tuple-element.39), channel_id=1, source_target_pairs={{0,16},{1,17},{2,18},{3,19},{4,20},{5,21},{6,22},{7,23},{8,24},{9,... | collective-permute-start | bytes 294920 | tf_op jit(solution)/shard_map/ppermute | solution.py:245
  42.4 0.0 collective-permute-done.11.w5
  42.5 1.4 %collective-permute-start.16 = (bf16[24,2048]{1,0:T(8,128)(2,1)S(1)}, bf16[24,2048]{1,0:T(8,128)(2,1)S(1)}, u32[]{:S(2)}, u32[]{:S(2)}) collective-permute-start(bf16[24,2048]{1,0:T(8,128)(2,1)S(1)} %get-tuple-element.40), channel_id=1, source_target_pairs={{0,24},{1,25},{2,26},{3,27},{4,28},{5,29},{6,30},{7,31},{8,16},{9,... | collective-permute-start | bytes 294920 | tf_op jit(solution)/shard_map/ppermute | solution.py:245
  43.9 0.0 collective-permute-done.10.w4
  43.9 1.2 %shard_map.70 = (f32[576,128]{1,0:T(8,128)S(1)}, f32[128,2048]{1,0:T(8,128)S(1)}) custom-call(bf16[256,2048]{1,0:T(8,128)(2,1)S(1)} %get-tuple-element.25.normed.refs_0_.refs_1_, bf16[576,128]{1,0:T(8,128)(2,1)S(1)} %get-tuple-element.28.cot, bf16[96,2048]{1,0:T(8,128)(2,1)S(1)} %shard_map.69.w0, bf16[96,2048]{1,0:T(8,128)(2,1)S(1)} %collective-permute-done.8.w1, ...), custom_call_target="tpu_custom_call" | custom-call | tf_op jit(solution)/shard_map/pallas_call | solution.py:253
  45.1 0.0 collective-permute-done.7.refs_3_
  45.1 1.4 %shard_map.71 = (bf16[128,768]{1,0:T(8,128)(2,1)}, bf16[128,2048]{1,0:T(8,128)(2,1)}) custom-call(bf16[256,2048]{1,0:T(8,128)(2,1)S(1)} %get-tuple-element.25.normed.refs_0_.refs_1_, bf16[192,128]{1,0:T(8,128)(2,1)S(1)} %get-tuple-element.26.refs_1_, bf16[96,2048]{1,0:T(8,128)(2,1)S(1)} %collective-permute-done.6.refs_2_, ...), custom_call_target="tpu_custom_call" | custom-call | tf_op jit(solution)/shard_map/pallas_call | solution.py:253
  46.5 0.0 collective-permute-done.14.g1
  46.5 5.6 %collective-permute-done.15.g2 = bf16[24,2048]{1,0:T(8,128)(2,1)S(1)} collective-permute-done((bf16[24,2048]{1,0:T(8,128)(2,1)S(1)}, bf16[24,2048]{1,0:T(8,128)(2,1)S(1)}, u32[]{:S(2)}, u32[]{:S(2)}) %collective-permute-start.15) | collective-permute-done | bytes 98336 | tf_op jit(solution)/shard_map/ppermute | solution.py:245
  52.1 0.0 collective-permute-done.16.g3
  52.1 0.7 %shard_map.75 = f32[24,2048]{1,0:T(8,128)} custom-call(f32[24,2048]{1,0:T(8,128)S(1)} %get-tuple-element.37.own, bf16[24,2048]{1,0:T(8,128)(2,1)S(1)} %collective-permute-done.14.g1, bf16[24,2048]{1,0:T(8,128)(2,1)S(1)} %collective-permute-done.15.g2, bf16[24,2048]{1,0:T(8,128)(2,1)S(1)} %collective-permute-done.16.g3), custom_call_target="tpu_custom_call" | custom-call | tf_op jit(solution)/shard_map/pallas_call | solution.py:253
  (1 shorter events, 0.0 us)
Async XLA Ops:
  0.6 5.2 %collective-permute-start = (bf16[128,2048]{1,0:T(8,128)(2,1)}, bf16[128,2048]{1,0:T(8,128)(2,1)S(1)}, u32[]{:S(2)}, u32[]{:S(2)}) collective-permute-start(bf16[128,2048]{1,0:T(8,128)(2,1)} %refs_0_.1), channel_id=1, source_target_pairs={{0,1},{1,0},{2,3},{3,2},{4,5},{5,4},{6,7},{7,6},{8,9},{9,8},{10,11... | collective-permute-start | bytes 1572872 | tf_op jit(solution)/shard_map/ppermute | solution.py:245
  1.2 4.7 %collective-permute-start.1 = (bf16[128,768]{1,0:T(8,128)(2,1)}, bf16[128,768]{1,0:T(8,128)(2,1)S(1)}, u32[]{:S(2)}, u32[]{:S(2)}) collective-permute-start(bf16[128,768]{1,0:T(8,128)(2,1)} %refs_1_.1), channel_id=1, source_target_pairs={{0,1},{1,0},{2,3},{3,2},{4,5},{5,4},{6,7},{7,6},{8,9},{9,8},{10,11... | collective-permute-start | bytes 589832 | tf_op jit(solution)/shard_map/ppermute | solution.py:245
  2.8 8.1 %collective-permute-start.2 = (bf16[24,2048]{1,0:T(8,128)(2,1)S(1)}, bf16[24,2048]{1,0:T(8,128)(2,1)S(1)}, u32[]{:S(2)}, u32[]{:S(2)}) collective-permute-start(bf16[24,2048]{1,0:T(8,128)(2,1)S(1)} %get-tuple-element.27.w0), channel_id=1, source_target_pairs={{0,8},{1,9},{2,10},{3,11},{4,12},{5,13},{6,14},{7,15},{8,0},{9,1},... | collective-permute-start | bytes 294920 | tf_op jit(solution)/shard_map/ppermute | solution.py:245
  6.5 24.0 %collective-permute-start.12 = (bf16[192,2048]{1,0:T(8,128)(2,1)S(1)}, bf16[192,2048]{1,0:T(8,128)(2,1)S(1)}, u32[]{:S(2)}, u32[]{:S(2)}) collective-permute-start(bf16[192,2048]{1,0:T(8,128)(2,1)S(1)} %get-tuple-element.35), channel_id=1, source_target_pairs={{0,2},{1,5},{2,0},{3,7},{4,6},{5,1},{6,4},{7,3},{8,10},{9,13},{10,... | collective-permute-start | bytes 2359304 | tf_op jit(solution)/shard_map/ppermute | solution.py:245
  8.1 9.6 %collective-permute-start.3 = (bf16[24,2048]{1,0:T(8,128)(2,1)S(1)}, bf16[24,2048]{1,0:T(8,128)(2,1)S(1)}, u32[]{:S(2)}, u32[]{:S(2)}) collective-permute-start(bf16[24,2048]{1,0:T(8,128)(2,1)S(1)} %get-tuple-element.27.w0), channel_id=1, source_target_pairs={{0,16},{1,17},{2,18},{3,19},{4,20},{5,21},{6,22},{7,23},{8,24},{9,... | collective-permute-start | bytes 294920 | tf_op jit(solution)/shard_map/ppermute | solution.py:245
  10.7 7.0 %collective-permute-start.4 = (bf16[24,2048]{1,0:T(8,128)(2,1)S(1)}, bf16[24,2048]{1,0:T(8,128)(2,1)S(1)}, u32[]{:S(2)}, u32[]{:S(2)}) collective-permute-start(bf16[24,2048]{1,0:T(8,128)(2,1)S(1)} %get-tuple-element.27.w0), channel_id=1, source_target_pairs={{0,24},{1,25},{2,26},{3,27},{4,28},{5,29},{6,30},{7,31},{8,16},{9,... | collective-permute-start | bytes 294920 | tf_op jit(solution)/shard_map/ppermute | solution.py:245
  17.7 12.1 %collective-permute-start.5 = (bf16[96,2048]{1,0:T(8,128)(2,1)S(1)}, bf16[96,2048]{1,0:T(8,128)(2,1)S(1)}, u32[]{:S(2)}, u32[]{:S(2)}) collective-permute-start(bf16[96,2048]{1,0:T(8,128)(2,1)S(1)} %shard_map.69.w0), channel_id=1, source_target_pairs={{0,4},{1,3},{2,6},{3,1},{4,0},{5,7},{6,2},{7,5},{8,12},{9,11},{10,... | collective-permute-start | bytes 1179656 | tf_op jit(solution)/shard_map/ppermute | solution.py:245
  19.1 13.0 %collective-permute-start.8 = (bf16[96,2048]{1,0:T(8,128)(2,1)S(1)}, bf16[96,2048]{1,0:T(8,128)(2,1)S(1)}, u32[]{:S(2)}, u32[]{:S(2)}) collective-permute-start(bf16[96,2048]{1,0:T(8,128)(2,1)S(1)} %shard_map.69.w0), channel_id=1, source_target_pairs={{0,2},{1,5},{2,0},{3,7},{4,6},{5,1},{6,4},{7,3},{8,10},{9,13},{10,... | collective-permute-start | bytes 1179656 | tf_op jit(solution)/shard_map/ppermute | solution.py:245
  29.8 7.8 %collective-permute-start.6 = (bf16[96,2048]{1,0:T(8,128)(2,1)S(1)}, bf16[96,2048]{1,0:T(8,128)(2,1)S(1)}, u32[]{:S(2)}, u32[]{:S(2)}) collective-permute-start(bf16[96,2048]{1,0:T(8,128)(2,1)S(1)} %collective-permute-done.5.w2), channel_id=1, source_target_pairs={{0,2},{1,5},{2,0},{3,7},{4,6},{5,1},{6,4},{7,3},{8,10},{9,13},{10,... | collective-permute-start | bytes 1179656 | tf_op jit(solution)/shard_map/ppermute | solution.py:245
  30.5 7.8 %collective-permute-start.13 = (bf16[96,2048]{1,0:T(8,128)(2,1)S(1)}, bf16[96,2048]{1,0:T(8,128)(2,1)S(1)}, u32[]{:S(2)}, u32[]{:S(2)}) collective-permute-start(bf16[96,2048]{1,0:T(8,128)(2,1)S(1)} %shard_map.73), channel_id=1, source_target_pairs={{0,4},{1,3},{2,6},{3,1},{4,0},{5,7},{6,2},{7,5},{8,12},{9,11},{10,... | collective-permute-start | bytes 1179656 | tf_op jit(solution)/shard_map/ppermute | solution.py:245
  31.6 9.7 %collective-permute-start.9 = (bf16[96,2048]{1,0:T(8,128)(2,1)S(1)}, bf16[96,2048]{1,0:T(8,128)(2,1)S(1)}, u32[]{:S(2)}, u32[]{:S(2)}) collective-permute-start(bf16[96,2048]{1,0:T(8,128)(2,1)S(1)} %shard_map.69.w0), channel_id=1, source_target_pairs={{0,1},{1,0},{2,3},{3,2},{4,5},{5,4},{6,7},{7,6},{8,9},{9,8},{10,11... | collective-permute-start | bytes 1179656 | tf_op jit(solution)/shard_map/ppermute | solution.py:245
  31.6 10.8 %collective-permute-start.11 = (bf16[96,2048]{1,0:T(8,128)(2,1)S(1)}, bf16[96,2048]{1,0:T(8,128)(2,1)S(1)}, u32[]{:S(2)}, u32[]{:S(2)}) collective-permute-start(bf16[96,2048]{1,0:T(8,128)(2,1)S(1)} %collective-permute-done.5.w2), channel_id=1, source_target_pairs={{0,1},{1,0},{2,3},{3,2},{4,5},{5,4},{6,7},{7,6},{8,9},{9,8},{10,11... | collective-permute-start | bytes 1179656 | tf_op jit(solution)/shard_map/ppermute | solution.py:245
  32.1 11.8 %collective-permute-start.10 = (bf16[96,2048]{1,0:T(8,128)(2,1)S(1)}, bf16[96,2048]{1,0:T(8,128)(2,1)S(1)}, u32[]{:S(2)}, u32[]{:S(2)}) collective-permute-start(bf16[96,2048]{1,0:T(8,128)(2,1)S(1)} %collective-permute-done.8.w1), channel_id=1, source_target_pairs={{0,1},{1,0},{2,3},{3,2},{4,5},{5,4},{6,7},{7,6},{8,9},{9,8},{10,11... | collective-permute-start | bytes 1179656 | tf_op jit(solution)/shard_map/ppermute | solution.py:245
  37.6 7.5 %collective-permute-start.7 = (bf16[96,2048]{1,0:T(8,128)(2,1)S(1)}, bf16[96,2048]{1,0:T(8,128)(2,1)S(1)}, u32[]{:S(2)}, u32[]{:S(2)}) collective-permute-start(bf16[96,2048]{1,0:T(8,128)(2,1)S(1)} %collective-permute-done.6.refs_2_), channel_id=1, source_target_pairs={{0,1},{1,0},{2,3},{3,2},{4,5},{5,4},{6,7},{7,6},{8,9},{9,8},{10,11... | collective-permute-start | bytes 1179656 | tf_op jit(solution)/shard_map/ppermute | solution.py:245
  38.5 8.0 %collective-permute-start.14 = (bf16[24,2048]{1,0:T(8,128)(2,1)S(1)}, bf16[24,2048]{1,0:T(8,128)(2,1)S(1)}, u32[]{:S(2)}, u32[]{:S(2)}) collective-permute-start(bf16[24,2048]{1,0:T(8,128)(2,1)S(1)} %get-tuple-element.38), channel_id=1, source_target_pairs={{0,8},{1,9},{2,10},{3,11},{4,12},{5,13},{6,14},{7,15},{8,0},{9,1},... | collective-permute-start | bytes 294920 | tf_op jit(solution)/shard_map/ppermute | solution.py:245
  41.3 10.8 %collective-permute-start.15 = (bf16[24,2048]{1,0:T(8,128)(2,1)S(1)}, bf16[24,2048]{1,0:T(8,128)(2,1)S(1)}, u32[]{:S(2)}, u32[]{:S(2)}) collective-permute-start(bf16[24,2048]{1,0:T(8,128)(2,1)S(1)} %get-tuple-element.39), channel_id=1, source_target_pairs={{0,16},{1,17},{2,18},{3,19},{4,20},{5,21},{6,22},{7,23},{8,24},{9,... | collective-permute-start | bytes 294920 | tf_op jit(solution)/shard_map/ppermute | solution.py:245
  42.5 9.6 %collective-permute-start.16 = (bf16[24,2048]{1,0:T(8,128)(2,1)S(1)}, bf16[24,2048]{1,0:T(8,128)(2,1)S(1)}, u32[]{:S(2)}, u32[]{:S(2)}) collective-permute-start(bf16[24,2048]{1,0:T(8,128)(2,1)S(1)} %get-tuple-element.40), channel_id=1, source_target_pairs={{0,24},{1,25},{2,26},{3,27},{4,28},{5,29},{6,30},{7,31},{8,16},{9,... | collective-permute-start | bytes 294920 | tf_op jit(solution)/shard_map/ppermute | solution.py:245

commit v2 on v1

v2 whole, which is shorter than its diff:
```python
import jax
import jax.numpy as jnp
from jax import lax
from jax.experimental import pallas as pl
from jax.experimental.pallas import tpu as pltpu
from jax.sharding import PartitionSpec as P


AXES = ("grp", "node")
F32 = jnp.float32
BF16 = jnp.bfloat16
VMEM = pl.BlockSpec(memory_space=pltpu.VMEM)
FAR = pl.BlockSpec(memory_space=pltpu.HBM)
GRANT = 12 * 1024 * 1024


def dequantize(block_codes, block_scales):
    count, width = block_codes.shape
    blocks = block_scales.shape[1]
    floats = (
        block_codes.astype(F32).reshape(count, blocks, -1)
        * block_scales[:, :, None]
        * width ** (-0.5)
    )
    return floats.reshape(count, -1).astype(BF16)


def plain_body(tokens, codes, scales, cotangent):
    rows_here = tokens.shape[0]
    groups = lax.axis_size("grp")
    nodes = lax.axis_size("node")
    per_device = codes.shape[0]
    height = cotangent.shape[1]
    floats = tokens.astype(F32)
    power = jnp.mean(floats * floats, axis=-1, keepdims=True)
    normed = (floats * lax.rsqrt(power + 1e-05)).astype(BF16)
    weight = lax.all_gather(dequantize(codes, scales), AXES, axis=0, tiled=True)
    values = jnp.dot(normed, weight.T, preferred_element_type=F32).astype(BF16)
    input_grad = jnp.dot(cotangent, weight, preferred_element_type=F32).astype(BF16)
    reordered = (
        cotangent.reshape(rows_here, groups, nodes, per_device)
        .transpose(0, 2, 1, 3)
        .reshape(rows_here, height)
    )
    factor = (rows_here * groups * nodes) ** (-0.5)
    term = jnp.einsum("tr,td->rd", reordered, normed, preferred_element_type=F32) * factor
    node_sum = lax.psum_scatter(
        term.astype(BF16), "node", scatter_dimension=0, tiled=True
    ).astype(F32)
    weight_grad = lax.psum_scatter(node_sum, "grp", scatter_dimension=0, tiled=True)
    return (values, input_grad, weight_grad)


def swap_first():
    return [(g * 2 + c, (g ^ (1 + c)) * 2 + c) for g in range(16) for c in range(2)]


def swap_second():
    return [(g * 2 + c, (g ^ (2 - c)) * 2 + c) for g in range(16) for c in range(2)]


def swap_z(k):
    return [(g * 2 + c, (g ^ (4 * k)) * 2 + c) for g in range(16) for c in range(2)]


def swap_core():
    return [(g * 2 + c, g * 2 + 1 - c) for g in range(16) for c in range(2)]


def row_block(g, c, j, block, per):
    core = c if j == 0 else 1 - c
    start = place_of(g, core, *PAIRS[block[0]], block[1]) * per
    return pl.ds(pl.multiple_of(start, 8), per)


def place_of(g, core, first, second, k):
    return (g ^ (first * (1 + core) + second * (2 - core) + 4 * k)) * 2 + core


PAIRS = ((0, 0), (1, 0), (0, 1), (1, 1))
EARLY = tuple((i, k) for i in (0, 2, 1) for k in range(4))
MID = ((3, 0), (3, 1))
LATE = ((3, 2), (3, 3))


def normalized(tok):
    floats = tok[...].astype(F32)
    power = jnp.mean(floats * floats, axis=-1, keepdims=True)
    return (floats * lax.rsqrt(power + 1e-05)).astype(BF16)


def own_kernel(
    per,
    tok_far,
    cot_far,
    codes_far,
    scales_far,
    weight,
    normed,
    early,
    mid,
    late,
    cot_t,
    tok,
    cot,
    codes,
    scales,
    sem,
):
    pairs = ((codes_far, codes), (scales_far, scales), (cot_far, cot), (tok_far, tok))
    loads = [pltpu.make_async_copy(x, y, sem.at[i]) for i, (x, y) in enumerate(pairs)]
    for load in loads:
        load.start()
    g = lax.axis_index("grp")
    c = lax.axis_index("node")
    width = tok.shape[1]
    blocks = scales.shape[0]
    wide = width // blocks
    inv_root = width ** (-0.5)
    loads[0].wait()
    loads[1].wait()
    by_row = scales[...].T
    for j in range(blocks):
        part = slice(j * wide, (j + 1) * wide)
        weight[:, part] = (codes[:, part].astype(F32) * by_row[:, j : j + 1] * inv_root).astype(
            BF16
        )
    loads[2].wait()
    cot_t[...] = cot[...].astype(F32).T
    loads[3].wait()
    normed[...] = normalized(tok)
    for out, blocks in ((early, EARLY), (mid, MID), (late, LATE)):
        for j in range(2):
            for n, block in enumerate(blocks):
                at = (j * len(blocks) + n) * per
                out[at : at + per, :] = cot_t[row_block(g, c, j, block, per), :]


def term_kernel(
    per, factor, tok2, cot2, normed1, early, mid, late, sent, going, kept_cot, normed, cot_t
):
    rows = tok2.shape[0]
    quarter = 4 * per
    g = lax.axis_index("grp")
    c = lax.axis_index("node")
    normed[:rows, :] = normed1[...]
    normed[rows:, :] = normalized(tok2)
    cot_t[...] = cot2[...].astype(F32).T

    def both(i, own):
        swapped = [cot_t[row_block(g, c, 0, (i, k), per), :] for k in range(4)]
        return jnp.concatenate([own, jnp.concatenate(swapped, axis=0)], axis=1).astype(BF16)

    kept_cot[:quarter, :] = both(0, early[:quarter, :])
    kept_cot[quarter:, :] = both(2, early[quarter : 2 * quarter, :])
    going[...] = both(1, early[2 * quarter : 3 * quarter, :])
    last = jnp.concatenate([mid[: 2 * per, :], late[: 2 * per, :]], axis=0)
    sent[...] = (
        jnp.dot(both(3, last), normed[...], preferred_element_type=F32) * factor
    ).astype(BF16)


def kept_kernel(factor, going, kept_cot, normed, *refs):
    (early1, mid1, late1), (sent, near, far, early, mid, late) = refs[:3], refs[3:]
    half = near.shape[0]
    sent[...] = (
        jnp.dot(going[...], normed[...], preferred_element_type=F32) * factor
    ).astype(BF16)
    both = jnp.dot(kept_cot[...], normed[...], preferred_element_type=F32) * factor
    near[...] = both[:half, :]
    far[...] = both[half:, :]
    early[...] = early1[...].astype(BF16)
    mid[...] = mid1[...].astype(BF16)
    late[...] = late1[...].astype(BF16)


def second_kernel(far, got_a, sent):
    sent[...] = (far[...] + got_a[...].astype(F32)).astype(BF16)


def spread_kernel(near, got_b, got2, own, s1, s2, s3):
    per = own.shape[0]
    for k, out in enumerate((own, s1, s2, s3)):
        part = slice(k * per, (k + 1) * per)
        total = near[part, :] + got_b[part, :].astype(F32) + got2[part, :].astype(F32)
        out[...] = total.astype(out.dtype)


def total_kernel(own, g1, g2, g3, out):
    out[...] = own[...] + g1[...].astype(F32) + g2[...].astype(F32) + g3[...].astype(F32)


def join_kernel(w0, w1, w2, w3, out, front, back):
    per = w0.shape[0]
    for k, piece in enumerate((w0, w1, w2, w3)):
        part = slice(k * per, (k + 1) * per)
        half = slice(k % 2 * per, (k % 2 + 1) * per)
        out[part, :] = piece[...]
        (front if k < 2 else back)[half, :] = piece[...]


LAST = (((1,), (1,)), ((), ()))
FIRST = (((0,), (0,)), ((), ()))


def stack(pieces, joined):
    at = 0
    for piece in pieces:
        joined[at : at + piece.shape[0], :] = piece[...]
        at += piece.shape[0]


def early_kernel(per, normed, cot, *refs):
    pieces, (full_t, grad, joined) = refs[:8], refs[8:]
    rows = grad.shape[0]
    g = lax.axis_index("grp")
    c = lax.axis_index("node")
    stack(pieces, joined)
    values_t = lax.dot_general(joined[...], normed[:rows, :], LAST, preferred_element_type=F32)
    for j in range(2):
        for n, block in enumerate(EARLY):
            at = (j * len(EARLY) + n) * per
            full_t[row_block(g, c, j, block, per), :] = values_t[at : at + per, :]
        for block in MID + LATE:
            full_t[row_block(g, c, j, block, per), :] = jnp.zeros((per, rows), F32)
    grad[...] = lax.dot_general(cot[...], joined[...], FIRST, preferred_element_type=F32)


def mid_kernel(per, normed, cot, w0, w1, full_t1, grad1, full_t, grad, joined):
    rows = grad.shape[0]
    g = lax.axis_index("grp")
    c = lax.axis_index("node")
    stack((w0, w1), joined)
    values_t = lax.dot_general(joined[...], normed[:rows, :], LAST, preferred_element_type=F32)
    full_t[...] = full_t1[...]
    for j in range(2):
        for n, block in enumerate(MID):
            at = (j * len(MID) + n) * per
            full_t[row_block(g, c, j, block, per), :] = values_t[at : at + per, :]
    grad[...] = grad1[...] + lax.dot_general(
        cot[...], joined[...], FIRST, preferred_element_type=F32
    )


def late_kernel(per, normed, cot, w0, w1, full_t1, grad, values_far, grad_far, *refs):
    joined, full_t, values, out, sem = refs
    rows = grad.shape[0]
    half = out.shape[1] // 2
    g = lax.axis_index("grp")
    c = lax.axis_index("node")
    stores = [
        pltpu.make_async_copy(
            out.at[:, pl.ds(i * half, half)], grad_far.at[:, pl.ds(i * half, half)], sem.at[i]
        )
        for i in range(2)
    ] + [pltpu.make_async_copy(values, values_far, sem.at[2])]
    stack((w0, w1), joined)
    for i in range(2):
        part = slice(i * half, (i + 1) * half)
        out[:, part] = (
            grad[:, part]
            + lax.dot_general(cot[...], joined[:, part], FIRST, preferred_element_type=F32)
        ).astype(BF16)
        stores[i].start()
    values_t = lax.dot_general(joined[...], normed[:rows, :], LAST, preferred_element_type=F32)
    full_t[...] = full_t1[...]
    for j in range(2):
        for n, block in enumerate(LATE):
            at = (j * len(LATE) + n) * per
            full_t[row_block(g, c, j, block, per), :] = values_t[at : at + per, :]
    values[...] = full_t[...].T.astype(BF16)
    stores[2].start()
    for store in stores:
        store.wait()


def plain(rows, columns, dtype):
    return jax.ShapeDtypeStruct((rows, columns), dtype)


def held(rows, columns, dtype):
    return pltpu.VMEM((rows, columns), dtype)


def move(array, pairs):
    return lax.ppermute(array, AXES, pairs)


def call(kernel, outs, *args, scratch=(), far=(), far_outs=False):
    args = [
        pltpu.with_memory_space_constraint(a, pltpu.HBM if i in far else pltpu.VMEM)
        for i, a in enumerate(args)
    ]
    return pl.pallas_call(
        kernel,
        out_shape=outs,
        in_specs=[FAR if i in far else VMEM for i in range(len(args))],
        out_specs=jax.tree.map(lambda _: FAR if far_outs else VMEM, outs),
        scratch_shapes=scratch,
        compiler_params=pltpu.CompilerParams(vmem_limit_bytes=GRANT),
    )(*args)


def block_body(tokens, codes, scales, cotangent):
    return block_steps(tokens, codes, scales, cotangent)


def block_steps(tokens, codes, scales, cotangent):
    rows, width = tokens.shape
    height = cotangent.shape[1]
    per = codes.shape[0]
    quarter = 4 * per
    factor = (rows * 32) ** (-0.5)

    tokens2 = move(tokens, swap_core())
    cotangent2 = move(cotangent, swap_core())
    own, normed1, *cots = call(
        lambda *refs: own_kernel(per, *refs),
        [
            held(per, width, BF16),
            held(rows, width, BF16),
            held(24 * per, rows, F32),
            held(4 * per, rows, F32),
            held(4 * per, rows, F32),
        ],
        tokens,
        cotangent,
        codes,
        scales.T,
        scratch=[
            pltpu.VMEM((height, rows), F32),
            pltpu.VMEM((rows, width), BF16),
            pltpu.VMEM((rows, height), BF16),
            pltpu.VMEM((per, width), BF16),
            pltpu.VMEM((scales.shape[1], per), F32),
            pltpu.SemaphoreType.DMA((4,)),
        ],
        far=(0, 1, 2, 3),
    )
    sent_a, going, kept_cot, normed = call(
        lambda *refs: term_kernel(per, factor, *refs),
        [
            held(quarter, width, BF16),
            held(quarter, 2 * rows, BF16),
            held(2 * quarter, 2 * rows, BF16),
            held(2 * rows, width, BF16),
        ],
        tokens2,
        cotangent2,
        normed1,
        *cots,
        scratch=[pltpu.VMEM((height, rows), F32)],
    )
    got_a = move(sent_a, swap_first())
    by_z = [own] + [move(own, swap_z(k)) for k in (1, 2, 3)]
    sent_b, near, far, early, mid, late = call(
        lambda *refs: kept_kernel(factor, *refs),
        [
            held(quarter, width, BF16),
            held(quarter, width, F32),
            held(quarter, width, F32),
            held(24 * per, rows, BF16),
            held(4 * per, rows, BF16),
            held(4 * per, rows, BF16),
        ],
        going,
        kept_cot,
        normed,
        *cots,
    )
    got_b = move(sent_b, swap_first())
    w00, front, back = call(
        join_kernel, [held(quarter, width, BF16)] + [held(2 * per, width, BF16)] * 2, *by_z
    )
    sent2 = call(second_kernel, held(quarter, width, BF16), far, got_a)
    got2 = move(sent2, swap_second())
    w01a = move(front, swap_second())
    w01b = move(back, swap_second())
    w10 = move(w00, swap_first())
    w11a = move(w01a, swap_first())
    w11b = move(w01b, swap_first())
    v00 = move(w00, swap_core())
    v01a = move(w01a, swap_core())
    v01b = move(w01b, swap_core())
    v10 = move(w10, swap_core())

    mine, s1, s2, s3 = call(
        spread_kernel, [held(per, width, F32)] + [held(per, width, BF16)] * 3, near, got_b, got2
    )
    others = [move(s, swap_z(k)) for k, s in ((1, s1), (2, s2), (3, s3))]
    full_t, grad = call(
        lambda *refs: early_kernel(per, *refs),
        [held(height, rows, F32), held(rows, width, F32)],
        normed,
        early,
        w00,
        w01a,
        w01b,
        w10,
        v00,
        v01a,
        v01b,
        v10,
        scratch=[pltpu.VMEM((24 * per, width), BF16)],
    )
    v11a = move(w11a, swap_core())
    full_t, grad = call(
        lambda *refs: mid_kernel(per, *refs),
        [held(height, rows, F32), held(rows, width, F32)],
        normed,
        mid,
        w11a,
        v11a,
        full_t,
        grad,
        scratch=[pltpu.VMEM((4 * per, width), BF16)],
    )
    v11b = move(w11b, swap_core())
    values, input_grad = call(
        lambda *refs: late_kernel(per, *refs),
        [plain(rows, height, BF16), plain(rows, width, BF16)],
        normed,
        late,
        w11b,
        v11b,
        full_t,
        grad,
        scratch=[
            pltpu.VMEM((4 * per, width), BF16),
            pltpu.VMEM((height, rows), F32),
            pltpu.VMEM((rows, height), BF16),
            pltpu.VMEM((rows, width), BF16),
            pltpu.SemaphoreType.DMA((3,)),
        ],
        far_outs=True,
    )
    weight_grad = call(total_kernel, plain(per, width, F32), mine, *others)
    return (values, input_grad, weight_grad)


def solution(mesh):
    sizes = dict(mesh.shape)
    blocked = (sizes["grp"], sizes["node"]) == (16, 2)
    split = P(AXES, None)
    return jax.shard_map(
        block_body if blocked else plain_body,
        mesh=mesh,
        in_specs=(split,) * 4,
        out_specs=(split,) * 3,
        check_vma=False,
    )
```

time: 53 us -> 58 us (1.094)
  starting transfers between devices: 18 us -> 23.1 us
  waiting for transfers between devices: 28.1 us -> 27.4 us
    ppermute x17 -> x22, starting transfers between devices: 18 us -> 23.1 us  [move(): return lax.ppermute(array, AXES, pairs)]
    ppermute x17 -> x22, waiting for transfers between devices: 28.1 us -> 27.4 us  [move(): return lax.ppermute(array, AXES, pairs)]
    pallas_call x9 -> x10, Pallas kernels: 6.01 us -> 6.56 us  [call(): pl.pallas_call(kernel, out_shape=outs, in_specs=[FAR if i in far else VME...]
  transfers between devices with their start and end apart: 17 -> 22, of which waited for: 5 -> 6; matrix products, arithmetic and copies ran while one was open for 0% -> 0% of each run, Pallas kernels for 10% -> 10%
where the time goes in v2:
time: 58 us; the launch traced here: 57.8 us
  waiting for transfers between devices  27.4 us (47%)
  starting transfers between devices  23.1 us (40%)
  Pallas kernels  6.56 us (11%)
  between operations  0.75 us (1%)
    ppermute x22, waiting for transfers between devices, move(): return lax.ppermute(array, AXES, pairs)  27.4 us
    ppermute x22, starting transfers between devices, move(): return lax.ppermute(array, AXES, pairs)  23.1 us
    pallas_call x10, Pallas kernels, call(): pl.pallas_call(kernel, out_shape=outs, in_specs=[FAR if i in far else VME...  6.56 us
  transfers between devices with their start and end apart: 22, of which 6 were waited for; matrix products, arithmetic and copies ran while one was open for 0% of the time, Pallas kernels for 10%

profile of v2, /device:TPU:0, one launch (start us, length us, event | category | flops | bytes accessed | tf_op | source)
XLA Modules:
  0.0 57.8 jit_solution(12281726623336150823)
XLA Ops:
  0.6 0.6 collective-permute-start
  1.2 0.1 collective-permute-start.1
  1.3 1.5 %shard_map.67 = (bf16[24,2048]{1,0:T(8,128)(2,1)S(1)}, bf16[128,2048]{1,0:T(8,128)(2,1)S(1)}, f32[576,128]{1,0:T(8,128)S(1)}, f32[96,128]{1,0:T(8,128)S(1)}, f32[96,128]{1,0:T(8,128)S(1)}) custom-call(bf16[128,2048]{1,0:T(8,128)(2,1)} %refs_0_.1, bf16[128,768]{1,0:T(8,128)(2,1)} %refs_1_.1, bf16[24,2048]{1,0:T(8,128)(2,1)} %refs_2_.1, f32[16,24]{1,0:T(8,128)} %bitcast.1), custom_call_target="tpu_custom_call" | custom-call | tf_op jit(solution)/shard_map/pallas_call | solution.py:294
  2.8 3.1 %collective-permute-start.2 = (bf16[24,2048]{1,0:T(8,128)(2,1)S(1)}, bf16[24,2048]{1,0:T(8,128)(2,1)S(1)}, u32[]{:S(2)}, u32[]{:S(2)}) collective-permute-start(bf16[24,2048]{1,0:T(8,128)(2,1)S(1)} %get-tuple-element.39.w0), channel_id=1, source_target_pairs={{0,8},{1,9},{2,10},{3,11},{4,12},{5,13},{6,14},{7,15},{8,0},{9,1},... | collective-permute-start | bytes 294920 | tf_op jit(solution)/shard_map/ppermute | solution.py:286
  5.8 0.0 collective-permute-done.1.refs_1_
  5.8 0.0 collective-permute-done.refs_0_
  5.8 0.6 %shard_map.68 = (bf16[96,2048]{1,0:T(8,128)(2,1)S(1)}, bf16[96,256]{1,0:T(8,128)(2,1)S(1)}, bf16[192,256]{1,0:T(8,128)(2,1)S(1)}, bf16[256,2048]{1,0:T(8,128)(2,1)S(1)}) custom-call(bf16[128,2048]{1,0:T(8,128)(2,1)S(1)} %collective-permute-done.refs_0_, bf16[128,768]{1,0:T(8,128)(2,1)S(1)} %collective-permute-done.1.refs_1_, ...), custom_call_target="tpu_custom_call" | custom-call | tf_op jit(solution)/shard_map/pallas_call | solution.py:294
  6.4 1.6 %collective-permute-start.17 = (bf16[96,2048]{1,0:T(8,128)(2,1)S(1)}, bf16[96,2048]{1,0:T(8,128)(2,1)S(1)}, u32[]{:S(2)}, u32[]{:S(2)}) collective-permute-start(bf16[96,2048]{1,0:T(8,128)(2,1)S(1)} %get-tuple-element.54), channel_id=1, source_target_pairs={{0,2},{1,5},{2,0},{3,7},{4,6},{5,1},{6,4},{7,3},{8,10},{9,13},{10,... | collective-permute-start | bytes 1179656 | tf_op jit(solution)/shard_map/ppermute | solution.py:286
  8.0 2.6 %collective-permute-start.3 = (bf16[24,2048]{1,0:T(8,128)(2,1)S(1)}, bf16[24,2048]{1,0:T(8,128)(2,1)S(1)}, u32[]{:S(2)}, u32[]{:S(2)}) collective-permute-start(bf16[24,2048]{1,0:T(8,128)(2,1)S(1)} %get-tuple-element.39.w0), channel_id=1, source_target_pairs={{0,16},{1,17},{2,18},{3,19},{4,20},{5,21},{6,22},{7,23},{8,24},{9,... | collective-permute-start | bytes 294920 | tf_op jit(solution)/shard_map/ppermute | solution.py:286
  10.6 0.2 collective-permute-start.4
  10.8 0.0 collective-permute-done.2.w1
  10.8 6.8 %collective-permute-done.3.w2 = bf16[24,2048]{1,0:T(8,128)(2,1)S(1)} collective-permute-done((bf16[24,2048]{1,0:T(8,128)(2,1)S(1)}, bf16[24,2048]{1,0:T(8,128)(2,1)S(1)}, u32[]{:S(2)}, u32[]{:S(2)}) %collective-permute-start.3) | collective-permute-done | bytes 98336 | tf_op jit(solution)/shard_map/ppermute | solution.py:286
  17.6 0.0 collective-permute-done.4.w3
  17.6 0.1 shard_map.70
  17.7 1.5 %collective-permute-start.11 = (bf16[96,2048]{1,0:T(8,128)(2,1)S(1)}, bf16[96,2048]{1,0:T(8,128)(2,1)S(1)}, u32[]{:S(2)}, u32[]{:S(2)}) collective-permute-start(bf16[96,2048]{1,0:T(8,128)(2,1)S(1)} %get-tuple-element.44.refs_2_), channel_id=1, source_target_pairs={{0,2},{1,5},{2,0},{3,7},{4,6},{5,1},{6,4},{7,3},{8,10},{9,13},{10,... | collective-permute-start | bytes 1179656 | tf_op jit(solution)/shard_map/ppermute | solution.py:286
  19.1 1.1 %collective-permute-start.8 = (bf16[48,2048]{1,0:T(8,128)(2,1)S(1)}, bf16[48,2048]{1,0:T(8,128)(2,1)S(1)}, u32[]{:S(2)}, u32[]{:S(2)}) collective-permute-start(bf16[48,2048]{1,0:T(8,128)(2,1)S(1)} %get-tuple-element.42), channel_id=1, source_target_pairs={{0,4},{1,3},{2,6},{3,1},{4,0},{5,7},{6,2},{7,5},{8,12},{9,11},{10,... | collective-permute-start | bytes 589832 | tf_op jit(solution)/shard_map/ppermute | solution.py:286
  20.3 0.9 %collective-permute-start.5 = (bf16[48,2048]{1,0:T(8,128)(2,1)S(1)}, bf16[48,2048]{1,0:T(8,128)(2,1)S(1)}, u32[]{:S(2)}, u32[]{:S(2)}) collective-permute-start(bf16[48,2048]{1,0:T(8,128)(2,1)S(1)} %get-tuple-element.40), channel_id=1, source_target_pairs={{0,4},{1,3},{2,6},{3,1},{4,0},{5,7},{6,2},{7,5},{8,12},{9,11},{10,... | collective-permute-start | bytes 589832 | tf_op jit(solution)/shard_map/ppermute | solution.py:286
  21.2 4.0 %collective-permute-done.8.refs_3_ = bf16[48,2048]{1,0:T(8,128)(2,1)S(1)} collective-permute-done((bf16[48,2048]{1,0:T(8,128)(2,1)S(1)}, bf16[48,2048]{1,0:T(8,128)(2,1)S(1)}, u32[]{:S(2)}, u32[]{:S(2)}) %collective-permute-start.8) | collective-permute-done | bytes 196640 | tf_op jit(solution)/shard_map/ppermute | solution.py:286
  25.2 0.0 collective-permute-start.13
  25.2 2.3 %collective-permute-start.9 = (bf16[48,2048]{1,0:T(8,128)(2,1)S(1)}, bf16[48,2048]{1,0:T(8,128)(2,1)S(1)}, u32[]{:S(2)}, u32[]{:S(2)}) collective-permute-start(bf16[48,2048]{1,0:T(8,128)(2,1)S(1)} %collective-permute-done.8.refs_3_), channel_id=1, source_target_pairs={{0,2},{1,5},{2,0},{3,7},{4,6},{5,1},{6,4},{7,3},{8,10},{9,13},{10,... | collective-permute-start | bytes 589832 | tf_op jit(solution)/shard_map/ppermute | solution.py:286
  27.5 0.5 shard_map.69
  28.1 0.0 collective-permute-done.17.got_a
  28.1 0.1 collective-permute-start.16
  28.2 0.1 shard_map.74
  28.2 0.0 collective-permute-done.5.refs_4_
  28.2 0.6 %collective-permute-start.18 = (bf16[96,2048]{1,0:T(8,128)(2,1)S(1)}, bf16[96,2048]{1,0:T(8,128)(2,1)S(1)}, u32[]{:S(2)}, u32[]{:S(2)}) collective-permute-start(bf16[96,2048]{1,0:T(8,128)(2,1)S(1)} %shard_map.74), channel_id=1, source_target_pairs={{0,4},{1,3},{2,6},{3,1},{4,0},{5,7},{6,2},{7,5},{8,12},{9,11},{10,... | collective-permute-start | bytes 1179656 | tf_op jit(solution)/shard_map/ppermute | solution.py:286
  28.9 0.0 collective-permute-done.11.refs_5_
  28.9 2.0 %collective-permute-start.6 = (bf16[48,2048]{1,0:T(8,128)(2,1)S(1)}, bf16[48,2048]{1,0:T(8,128)(2,1)S(1)}, u32[]{:S(2)}, u32[]{:S(2)}) collective-permute-start(bf16[48,2048]{1,0:T(8,128)(2,1)S(1)} %collective-permute-done.5.refs_4_), channel_id=1, source_target_pairs={{0,2},{1,5},{2,0},{3,7},{4,6},{5,1},{6,4},{7,3},{8,10},{9,13},{10,... | collective-permute-start | bytes 589832 | tf_op jit(solution)/shard_map/ppermute | solution.py:286
  30.9 0.0 collective-permute-done.13.refs_7_
  30.9 0.0 collective-permute-start.12
  30.9 0.3 collective-permute-done.9.refs_2_
  31.2 0.2 collective-permute-start.15
  31.4 10.3 %collective-permute-done.6.refs_2_ = bf16[48,2048]{1,0:T(8,128)(2,1)S(1)} collective-permute-done((bf16[48,2048]{1,0:T(8,128)(2,1)S(1)}, bf16[48,2048]{1,0:T(8,128)(2,1)S(1)}, u32[]{:S(2)}, u32[]{:S(2)}) %collective-permute-start.6) | collective-permute-done | bytes 196640 | tf_op jit(solution)/shard_map/ppermute | solution.py:286
  41.7 0.0 collective-permute-start.14
  41.7 0.0 collective-permute-done.16.got_b
  41.7 0.5 collective-permute-start.10
  42.2 0.0 collective-permute-done.18.got2
  42.2 0.1 collective-permute-start.7
  42.3 0.1 shard_map.75
  42.4 0.7 %collective-permute-done.14.refs_8_ = bf16[48,2048]{1,0:T(8,128)(2,1)S(1)} collective-permute-done((bf16[48,2048]{1,0:T(8,128)(2,1)S(1)}, bf16[48,2048]{1,0:T(8,128)(2,1)S(1)}, u32[]{:S(2)}, u32[]{:S(2)}) %collective-permute-start.14) | collective-permute-done | bytes 196640 | tf_op jit(solution)/shard_map/ppermute | solution.py:286
  43.2 3.4 %collective-permute-start.19 = (bf16[24,2048]{1,0:T(8,128)(2,1)S(1)}, bf16[24,2048]{1,0:T(8,128)(2,1)S(1)}, u32[]{:S(2)}, u32[]{:S(2)}) collective-permute-start(bf16[24,2048]{1,0:T(8,128)(2,1)S(1)} %get-tuple-element.56), channel_id=1, source_target_pairs={{0,8},{1,9},{2,10},{3,11},{4,12},{5,13},{6,14},{7,15},{8,0},{9,1},... | collective-permute-start | bytes 294920 | tf_op jit(solution)/shard_map/ppermute | solution.py:286
  46.6 0.0 collective-permute-done.12.refs_6_
  46.6 0.5 collective-permute-start.20
  47.1 0.0 collective-permute-done.15.refs_9_
  47.1 1.8 %collective-permute-start.21 = (bf16[24,2048]{1,0:T(8,128)(2,1)S(1)}, bf16[24,2048]{1,0:T(8,128)(2,1)S(1)}, u32[]{:S(2)}, u32[]{:S(2)}) collective-permute-start(bf16[24,2048]{1,0:T(8,128)(2,1)S(1)} %get-tuple-element.58), channel_id=1, source_target_pairs={{0,24},{1,25},{2,26},{3,27},{4,28},{5,29},{6,30},{7,31},{8,16},{9,... | collective-permute-start | bytes 294920 | tf_op jit(solution)/shard_map/ppermute | solution.py:286
  48.9 1.2 %shard_map.71 = (f32[768,128]{1,0:T(8,128)S(1)}, f32[128,2048]{1,0:T(8,128)S(1)}) custom-call(bf16[256,2048]{1,0:T(8,128)(2,1)S(1)} %get-tuple-element.35.refs_2_.refs_0_, bf16[576,128]{1,0:T(8,128)(2,1)S(1)} %get-tuple-element.43.refs_1_, bf16[96,2048]{1,0:T(8,128)(2,1)S(1)} %get-tuple-element.44.refs_2_, ...), custom_call_target="tpu_custom_call" | custom-call | tf_op jit(solution)/shard_map/pallas_call | solution.py:294
  50.1 0.0 collective-permute-done.10.refs_3_
  50.1 0.5 shard_map.72
  50.6 0.0 collective-permute-done.7.refs_3_
  50.6 1.3 %shard_map.73 = (bf16[128,768]{1,0:T(8,128)(2,1)}, bf16[128,2048]{1,0:T(8,128)(2,1)}) custom-call(bf16[256,2048]{1,0:T(8,128)(2,1)S(1)} %get-tuple-element.35.refs_2_.refs_0_, bf16[96,128]{1,0:T(8,128)(2,1)S(1)} %get-tuple-element.38.refs_1_, bf16[48,2048]{1,0:T(8,128)(2,1)S(1)} %collective-permute-done.6.refs_2_, ...), custom_call_target="tpu_custom_call" | custom-call | tf_op jit(solution)/shard_map/pallas_call | solution.py:294
  52.0 0.0 collective-permute-done.19.g1
  52.0 5.1 %collective-permute-done.20.g2 = bf16[24,2048]{1,0:T(8,128)(2,1)S(1)} collective-permute-done((bf16[24,2048]{1,0:T(8,128)(2,1)S(1)}, bf16[24,2048]{1,0:T(8,128)(2,1)S(1)}, u32[]{:S(2)}, u32[]{:S(2)}) %collective-permute-start.20) | collective-permute-done | bytes 98336 | tf_op jit(solution)/shard_map/ppermute | solution.py:286
  57.1 0.0 collective-permute-done.21.g3
  57.1 0.7 %shard_map.76 = f32[24,2048]{1,0:T(8,128)} custom-call(f32[24,2048]{1,0:T(8,128)S(1)} %get-tuple-element.55.own, bf16[24,2048]{1,0:T(8,128)(2,1)S(1)} %collective-permute-done.19.g1, bf16[24,2048]{1,0:T(8,128)(2,1)S(1)} %collective-permute-done.20.g2, bf16[24,2048]{1,0:T(8,128)(2,1)S(1)} %collective-permute-done.21.g3), custom_call_target="tpu_custom_call" | custom-call | tf_op jit(solution)/shard_map/pallas_call | solution.py:294
Async XLA Ops:
  0.6 5.2 %collective-permute-start = (bf16[128,2048]{1,0:T(8,128)(2,1)}, bf16[128,2048]{1,0:T(8,128)(2,1)S(1)}, u32[]{:S(2)}, u32[]{:S(2)}) collective-permute-start(bf16[128,2048]{1,0:T(8,128)(2,1)} %refs_0_.1), channel_id=1, source_target_pairs={{0,1},{1,0},{2,3},{3,2},{4,5},{5,4},{6,7},{7,6},{8,9},{9,8},{10,11... | collective-permute-start | bytes 1572872 | tf_op jit(solution)/shard_map/ppermute | solution.py:286
  1.2 4.7 %collective-permute-start.1 = (bf16[128,768]{1,0:T(8,128)(2,1)}, bf16[128,768]{1,0:T(8,128)(2,1)S(1)}, u32[]{:S(2)}, u32[]{:S(2)}) collective-permute-start(bf16[128,768]{1,0:T(8,128)(2,1)} %refs_1_.1), channel_id=1, source_target_pairs={{0,1},{1,0},{2,3},{3,2},{4,5},{5,4},{6,7},{7,6},{8,9},{9,8},{10,11... | collective-permute-start | bytes 589832 | tf_op jit(solution)/shard_map/ppermute | solution.py:286
  2.8 8.0 %collective-permute-start.2 = (bf16[24,2048]{1,0:T(8,128)(2,1)S(1)}, bf16[24,2048]{1,0:T(8,128)(2,1)S(1)}, u32[]{:S(2)}, u32[]{:S(2)}) collective-permute-start(bf16[24,2048]{1,0:T(8,128)(2,1)S(1)} %get-tuple-element.39.w0), channel_id=1, source_target_pairs={{0,8},{1,9},{2,10},{3,11},{4,12},{5,13},{6,14},{7,15},{8,0},{9,1},... | collective-permute-start | bytes 294920 | tf_op jit(solution)/shard_map/ppermute | solution.py:286
  6.4 21.6 %collective-permute-start.17 = (bf16[96,2048]{1,0:T(8,128)(2,1)S(1)}, bf16[96,2048]{1,0:T(8,128)(2,1)S(1)}, u32[]{:S(2)}, u32[]{:S(2)}) collective-permute-start(bf16[96,2048]{1,0:T(8,128)(2,1)S(1)} %get-tuple-element.54), channel_id=1, source_target_pairs={{0,2},{1,5},{2,0},{3,7},{4,6},{5,1},{6,4},{7,3},{8,10},{9,13},{10,... | collective-permute-start | bytes 1179656 | tf_op jit(solution)/shard_map/ppermute | solution.py:286
  8.0 9.6 %collective-permute-start.3 = (bf16[24,2048]{1,0:T(8,128)(2,1)S(1)}, bf16[24,2048]{1,0:T(8,128)(2,1)S(1)}, u32[]{:S(2)}, u32[]{:S(2)}) collective-permute-start(bf16[24,2048]{1,0:T(8,128)(2,1)S(1)} %get-tuple-element.39.w0), channel_id=1, source_target_pairs={{0,16},{1,17},{2,18},{3,19},{4,20},{5,21},{6,22},{7,23},{8,24},{9,... | collective-permute-start | bytes 294920 | tf_op jit(solution)/shard_map/ppermute | solution.py:286
  10.6 7.0 %collective-permute-start.4 = (bf16[24,2048]{1,0:T(8,128)(2,1)S(1)}, bf16[24,2048]{1,0:T(8,128)(2,1)S(1)}, u32[]{:S(2)}, u32[]{:S(2)}) collective-permute-start(bf16[24,2048]{1,0:T(8,128)(2,1)S(1)} %get-tuple-element.39.w0), channel_id=1, source_target_pairs={{0,24},{1,25},{2,26},{3,27},{4,28},{5,29},{6,30},{7,31},{8,16},{9,... | collective-permute-start | bytes 294920 | tf_op jit(solution)/shard_map/ppermute | solution.py:286
  17.7 11.2 %collective-permute-start.11 = (bf16[96,2048]{1,0:T(8,128)(2,1)S(1)}, bf16[96,2048]{1,0:T(8,128)(2,1)S(1)}, u32[]{:S(2)}, u32[]{:S(2)}) collective-permute-start(bf16[96,2048]{1,0:T(8,128)(2,1)S(1)} %get-tuple-element.44.refs_2_), channel_id=1, source_target_pairs={{0,2},{1,5},{2,0},{3,7},{4,6},{5,1},{6,4},{7,3},{8,10},{9,13},{10,... | collective-permute-start | bytes 1179656 | tf_op jit(solution)/shard_map/ppermute | solution.py:286
  19.1 6.1 %collective-permute-start.8 = (bf16[48,2048]{1,0:T(8,128)(2,1)S(1)}, bf16[48,2048]{1,0:T(8,128)(2,1)S(1)}, u32[]{:S(2)}, u32[]{:S(2)}) collective-permute-start(bf16[48,2048]{1,0:T(8,128)(2,1)S(1)} %get-tuple-element.42), channel_id=1, source_target_pairs={{0,4},{1,3},{2,6},{3,1},{4,0},{5,7},{6,2},{7,5},{8,12},{9,11},{10,... | collective-permute-start | bytes 589832 | tf_op jit(solution)/shard_map/ppermute | solution.py:286
  20.3 7.9 %collective-permute-start.5 = (bf16[48,2048]{1,0:T(8,128)(2,1)S(1)}, bf16[48,2048]{1,0:T(8,128)(2,1)S(1)}, u32[]{:S(2)}, u32[]{:S(2)}) collective-permute-start(bf16[48,2048]{1,0:T(8,128)(2,1)S(1)} %get-tuple-element.40), channel_id=1, source_target_pairs={{0,4},{1,3},{2,6},{3,1},{4,0},{5,7},{6,2},{7,5},{8,12},{9,11},{10,... | collective-permute-start | bytes 589832 | tf_op jit(solution)/shard_map/ppermute | solution.py:286
  25.2 5.7 %collective-permute-start.13 = (bf16[48,2048]{1,0:T(8,128)(2,1)S(1)}, bf16[48,2048]{1,0:T(8,128)(2,1)S(1)}, u32[]{:S(2)}, u32[]{:S(2)}) collective-permute-start(bf16[48,2048]{1,0:T(8,128)(2,1)S(1)} %collective-permute-done.8.refs_3_), channel_id=1, source_target_pairs={{0,1},{1,0},{2,3},{3,2},{4,5},{5,4},{6,7},{7,6},{8,9},{9,8},{10,11... | collective-permute-start | bytes 589832 | tf_op jit(solution)/shard_map/ppermute | solution.py:286
  25.2 6.0 %collective-permute-start.9 = (bf16[48,2048]{1,0:T(8,128)(2,1)S(1)}, bf16[48,2048]{1,0:T(8,128)(2,1)S(1)}, u32[]{:S(2)}, u32[]{:S(2)}) collective-permute-start(bf16[48,2048]{1,0:T(8,128)(2,1)S(1)} %collective-permute-done.8.refs_3_), channel_id=1, source_target_pairs={{0,2},{1,5},{2,0},{3,7},{4,6},{5,1},{6,4},{7,3},{8,10},{9,13},{10,... | collective-permute-start | bytes 589832 | tf_op jit(solution)/shard_map/ppermute | solution.py:286
  28.1 13.6 %collective-permute-start.16 = (bf16[96,2048]{1,0:T(8,128)(2,1)S(1)}, bf16[96,2048]{1,0:T(8,128)(2,1)S(1)}, u32[]{:S(2)}, u32[]{:S(2)}) collective-permute-start(bf16[96,2048]{1,0:T(8,128)(2,1)S(1)} %get-tuple-element.52), channel_id=1, source_target_pairs={{0,2},{1,5},{2,0},{3,7},{4,6},{5,1},{6,4},{7,3},{8,10},{9,13},{10,... | collective-permute-start | bytes 1179656 | tf_op jit(solution)/shard_map/ppermute | solution.py:286
  28.2 14.0 %collective-permute-start.18 = (bf16[96,2048]{1,0:T(8,128)(2,1)S(1)}, bf16[96,2048]{1,0:T(8,128)(2,1)S(1)}, u32[]{:S(2)}, u32[]{:S(2)}) collective-permute-start(bf16[96,2048]{1,0:T(8,128)(2,1)S(1)} %shard_map.74), channel_id=1, source_target_pairs={{0,4},{1,3},{2,6},{3,1},{4,0},{5,7},{6,2},{7,5},{8,12},{9,11},{10,... | collective-permute-start | bytes 1179656 | tf_op jit(solution)/shard_map/ppermute | solution.py:286
  28.9 12.8 %collective-permute-start.6 = (bf16[48,2048]{1,0:T(8,128)(2,1)S(1)}, bf16[48,2048]{1,0:T(8,128)(2,1)S(1)}, u32[]{:S(2)}, u32[]{:S(2)}) collective-permute-start(bf16[48,2048]{1,0:T(8,128)(2,1)S(1)} %collective-permute-done.5.refs_4_), channel_id=1, source_target_pairs={{0,2},{1,5},{2,0},{3,7},{4,6},{5,1},{6,4},{7,3},{8,10},{9,13},{10,... | collective-permute-start | bytes 589832 | tf_op jit(solution)/shard_map/ppermute | solution.py:286
  30.9 15.7 %collective-permute-start.12 = (bf16[96,2048]{1,0:T(8,128)(2,1)S(1)}, bf16[96,2048]{1,0:T(8,128)(2,1)S(1)}, u32[]{:S(2)}, u32[]{:S(2)}) collective-permute-start(bf16[96,2048]{1,0:T(8,128)(2,1)S(1)} %get-tuple-element.44.refs_2_), channel_id=1, source_target_pairs={{0,1},{1,0},{2,3},{3,2},{4,5},{5,4},{6,7},{7,6},{8,9},{9,8},{10,11... | collective-permute-start | bytes 1179656 | tf_op jit(solution)/shard_map/ppermute | solution.py:286
  31.2 15.9 %collective-permute-start.15 = (bf16[96,2048]{1,0:T(8,128)(2,1)S(1)}, bf16[96,2048]{1,0:T(8,128)(2,1)S(1)}, u32[]{:S(2)}, u32[]{:S(2)}) collective-permute-start(bf16[96,2048]{1,0:T(8,128)(2,1)S(1)} %collective-permute-done.11.refs_5_), channel_id=1, source_target_pairs={{0,1},{1,0},{2,3},{3,2},{4,5},{5,4},{6,7},{7,6},{8,9},{9,8},{10,11... | collective-permute-start | bytes 1179656 | tf_op jit(solution)/shard_map/ppermute | solution.py:286
  41.7 1.4 %collective-permute-start.14 = (bf16[48,2048]{1,0:T(8,128)(2,1)S(1)}, bf16[48,2048]{1,0:T(8,128)(2,1)S(1)}, u32[]{:S(2)}, u32[]{:S(2)}) collective-permute-start(bf16[48,2048]{1,0:T(8,128)(2,1)S(1)} %collective-permute-done.5.refs_4_), channel_id=1, source_target_pairs={{0,1},{1,0},{2,3},{3,2},{4,5},{5,4},{6,7},{7,6},{8,9},{9,8},{10,11... | collective-permute-start | bytes 589832 | tf_op jit(solution)/shard_map/ppermute | solution.py:286
  41.7 8.4 %collective-permute-start.10 = (bf16[48,2048]{1,0:T(8,128)(2,1)S(1)}, bf16[48,2048]{1,0:T(8,128)(2,1)S(1)}, u32[]{:S(2)}, u32[]{:S(2)}) collective-permute-start(bf16[48,2048]{1,0:T(8,128)(2,1)S(1)} %collective-permute-done.9.refs_2_), channel_id=1, source_target_pairs={{0,1},{1,0},{2,3},{3,2},{4,5},{5,4},{6,7},{7,6},{8,9},{9,8},{10,11... | collective-permute-start | bytes 589832 | tf_op jit(solution)/shard_map/ppermute | solution.py:286
  42.2 8.4 %collective-permute-start.7 = (bf16[48,2048]{1,0:T(8,128)(2,1)S(1)}, bf16[48,2048]{1,0:T(8,128)(2,1)S(1)}, u32[]{:S(2)}, u32[]{:S(2)}) collective-permute-start(bf16[48,2048]{1,0:T(8,128)(2,1)S(1)} %collective-permute-done.6.refs_2_), channel_id=1, source_target_pairs={{0,1},{1,0},{2,3},{3,2},{4,5},{5,4},{6,7},{7,6},{8,9},{9,8},{10,11... | collective-permute-start | bytes 589832 | tf_op jit(solution)/shard_map/ppermute | solution.py:286
  43.2 8.8 %collective-permute-start.19 = (bf16[24,2048]{1,0:T(8,128)(2,1)S(1)}, bf16[24,2048]{1,0:T(8,128)(2,1)S(1)}, u32[]{:S(2)}, u32[]{:S(2)}) collective-permute-start(bf16[24,2048]{1,0:T(8,128)(2,1)S(1)} %get-tuple-element.56), channel_id=1, source_target_pairs={{0,8},{1,9},{2,10},{3,11},{4,12},{5,13},{6,14},{7,15},{8,0},{9,1},... | collective-permute-start | bytes 294920 | tf_op jit(solution)/shard_map/ppermute | solution.py:286
  46.6 10.5 %collective-permute-start.20 = (bf16[24,2048]{1,0:T(8,128)(2,1)S(1)}, bf16[24,2048]{1,0:T(8,128)(2,1)S(1)}, u32[]{:S(2)}, u32[]{:S(2)}) collective-permute-start(bf16[24,2048]{1,0:T(8,128)(2,1)S(1)} %get-tuple-element.57), channel_id=1, source_target_pairs={{0,16},{1,17},{2,18},{3,19},{4,20},{5,21},{6,22},{7,23},{8,24},{9,... | collective-permute-start | bytes 294920 | tf_op jit(solution)/shard_map/ppermute | solution.py:286
  47.1 10.0 %collective-permute-start.21 = (bf16[24,2048]{1,0:T(8,128)(2,1)S(1)}, bf16[24,2048]{1,0:T(8,128)(2,1)S(1)}, u32[]{:S(2)}, u32[]{:S(2)}) collective-permute-start(bf16[24,2048]{1,0:T(8,128)(2,1)S(1)} %get-tuple-element.58), channel_id=1, source_target_pairs={{0,24},{1,25},{2,26},{3,27},{4,28},{5,29},{6,30},{7,31},{8,16},{9,... | collective-permute-start | bytes 294920 | tf_op jit(solution)/shard_map/ppermute | solution.py:286

commit v3 on v2

--- a/solution.py
+++ b/solution.py
@@ -186,10 +186,6 @@
         out[...] = total.astype(out.dtype)
 
 
-def total_kernel(own, g1, g2, g3, out):
-    out[...] = own[...] + g1[...].astype(F32) + g2[...].astype(F32) + g3[...].astype(F32)
-
-
 def join_kernel(w0, w1, w2, w3, out, front, back):
     per = w0.shape[0]
     for k, piece in enumerate((w0, w1, w2, w3)):
@@ -242,8 +238,9 @@
     )
 
 
-def late_kernel(per, normed, cot, w0, w1, full_t1, grad, values_far, grad_far, *refs):
-    joined, full_t, values, out, sem = refs
+def late_kernel(per, normed, cot, w0, w1, full_t1, grad, *refs):
+    (own, g1, g2, g3), (values_far, grad_far, total_far) = refs[:4], refs[4:7]
+    joined, full_t, total, values, out, sem = refs[7:]
     rows = grad.shape[0]
     half = out.shape[1] // 2
     g = lax.axis_index("grp")
@@ -253,7 +250,12 @@
             out.at[:, pl.ds(i * half, half)], grad_far.at[:, pl.ds(i * half, half)], sem.at[i]
         )
         for i in range(2)
-    ] + [pltpu.make_async_copy(values, values_far, sem.at[2])]
+    ] + [
+        pltpu.make_async_copy(values, values_far, sem.at[2]),
+        pltpu.make_async_copy(total, total_far, sem.at[3]),
+    ]
+    total[...] = own[...] + g1[...].astype(F32) + g2[...].astype(F32) + g3[...].astype(F32)
+    stores[3].start()
     stack((w0, w1), joined)
     for i in range(2):
         part = slice(i * half, (i + 1) * half)
@@ -416,25 +418,27 @@
         scratch=[pltpu.VMEM((4 * per, width), BF16)],
     )
     v11b = move(w11b, swap_core())
-    values, input_grad = call(
+    values, input_grad, weight_grad = call(
         lambda *refs: late_kernel(per, *refs),
-        [plain(rows, height, BF16), plain(rows, width, BF16)],
+        [plain(rows, height, BF16), plain(rows, width, BF16), plain(per, width, F32)],
         normed,
         late,
         w11b,
         v11b,
         full_t,
         grad,
+        mine,
+        *others,
         scratch=[
             pltpu.VMEM((4 * per, width), BF16),
             pltpu.VMEM((height, rows), F32),
+            pltpu.VMEM((per, width), F32),
             pltpu.VMEM((rows, height), BF16),
             pltpu.VMEM((rows, width), BF16),
-            pltpu.SemaphoreType.DMA((3,)),
+            pltpu.SemaphoreType.DMA((4,)),
         ],
         far_outs=True,
     )
-    weight_grad = call(total_kernel, plain(per, width, F32), mine, *others)
     return (values, input_grad, weight_grad)
 
 

time: 58 us -> 56.2 us (0.969)
  Pallas kernels: 6.56 us -> 5.83 us
  starting transfers between devices: 23.1 us -> 22.4 us
    pallas_call x10 -> x9, Pallas kernels: 6.56 us -> 5.83 us  [call(): pl.pallas_call(kernel, out_shape=outs, in_specs=[FAR if i in far else VME...]
    ppermute x22, starting transfers between devices: 23.1 us -> 22.4 us  [move(): return lax.ppermute(array, AXES, pairs)]
  transfers between devices with their start and end apart: 22 -> 22, of which waited for: 6 -> 6; matrix products, arithmetic and copies ran while one was open for 0% -> 0% of each run, Pallas kernels for 10% -> 8%
where the time goes in v3:
time: 56.2 us; the launch traced here: 56 us
  waiting for transfers between devices  27 us (48%)
  starting transfers between devices  22.4 us (40%)
  Pallas kernels  5.83 us (10%)
  between operations  0.73 us (1%)
    ppermute x22, waiting for transfers between devices, move(): return lax.ppermute(array, AXES, pairs)  27 us
    ppermute x22, starting transfers between devices, move(): return lax.ppermute(array, AXES, pairs)  22.4 us
    pallas_call x9, Pallas kernels, call(): pl.pallas_call(kernel, out_shape=outs, in_specs=[FAR if i in far else VME...  5.83 us
  transfers between devices with their start and end apart: 22, of which 6 were waited for; matrix products, arithmetic and copies ran while one was open for 0% of the time, Pallas kernels for 8%

profile of v3, /device:TPU:0, one launch (start us, length us, event | category | flops | bytes accessed | tf_op | source)
XLA Modules:
  0.0 56.0 jit_solution(17065941128749020393)
XLA Ops:
  0.6 0.6 collective-permute-start
  1.2 0.1 collective-permute-start.1
  1.3 1.5 %shard_map.67 = (bf16[24,2048]{1,0:T(8,128)(2,1)S(1)}, bf16[128,2048]{1,0:T(8,128)(2,1)S(1)}, f32[576,128]{1,0:T(8,128)S(1)}, f32[96,128]{1,0:T(8,128)S(1)}, f32[96,128]{1,0:T(8,128)S(1)}) custom-call(bf16[128,2048]{1,0:T(8,128)(2,1)} %refs_0_.1, bf16[128,768]{1,0:T(8,128)(2,1)} %refs_1_.1, bf16[24,2048]{1,0:T(8,128)(2,1)} %refs_2_.1, f32[16,24]{1,0:T(8,128)} %bitcast.1), custom_call_target="tpu_custom_call" | custom-call | tf_op jit(solution)/shard_map/pallas_call | solution.py:296
  2.8 3.1 %collective-permute-start.2 = (bf16[24,2048]{1,0:T(8,128)(2,1)S(1)}, bf16[24,2048]{1,0:T(8,128)(2,1)S(1)}, u32[]{:S(2)}, u32[]{:S(2)}) collective-permute-start(bf16[24,2048]{1,0:T(8,128)(2,1)S(1)} %get-tuple-element.37.w0), channel_id=1, source_target_pairs={{0,8},{1,9},{2,10},{3,11},{4,12},{5,13},{6,14},{7,15},{8,0},{9,1},... | collective-permute-start | bytes 294920 | tf_op jit(solution)/shard_map/ppermute | solution.py:288
  5.8 2.6 %collective-permute-start.3 = (bf16[24,2048]{1,0:T(8,128)(2,1)S(1)}, bf16[24,2048]{1,0:T(8,128)(2,1)S(1)}, u32[]{:S(2)}, u32[]{:S(2)}) collective-permute-start(bf16[24,2048]{1,0:T(8,128)(2,1)S(1)} %get-tuple-element.37.w0), channel_id=1, source_target_pairs={{0,16},{1,17},{2,18},{3,19},{4,20},{5,21},{6,22},{7,23},{8,24},{9,... | collective-permute-start | bytes 294920 | tf_op jit(solution)/shard_map/ppermute | solution.py:288
  8.4 0.0 collective-permute-start.4
  8.4 0.0 collective-permute-done.1.refs_1_
  8.4 0.0 collective-permute-done.refs_0_
  8.4 0.6 %shard_map.68 = (bf16[96,2048]{1,0:T(8,128)(2,1)S(1)}, bf16[96,256]{1,0:T(8,128)(2,1)S(1)}, bf16[192,256]{1,0:T(8,128)(2,1)S(1)}, bf16[256,2048]{1,0:T(8,128)(2,1)S(1)}) custom-call(bf16[128,2048]{1,0:T(8,128)(2,1)S(1)} %collective-permute-done.refs_0_, bf16[128,768]{1,0:T(8,128)(2,1)S(1)} %collective-permute-done.1.refs_1_, ...), custom_call_target="tpu_custom_call" | custom-call | tf_op jit(solution)/shard_map/pallas_call | solution.py:296
  9.0 1.8 %collective-permute-start.17 = (bf16[96,2048]{1,0:T(8,128)(2,1)S(1)}, bf16[96,2048]{1,0:T(8,128)(2,1)S(1)}, u32[]{:S(2)}, u32[]{:S(2)}) collective-permute-start(bf16[96,2048]{1,0:T(8,128)(2,1)S(1)} %get-tuple-element.50), channel_id=1, source_target_pairs={{0,2},{1,5},{2,0},{3,7},{4,6},{5,1},{6,4},{7,3},{8,10},{9,13},{10,... | collective-permute-start | bytes 1179656 | tf_op jit(solution)/shard_map/ppermute | solution.py:288
  10.8 0.0 collective-permute-done.2.w1
  10.8 5.7 %collective-permute-done.3.w2 = bf16[24,2048]{1,0:T(8,128)(2,1)S(1)} collective-permute-done((bf16[24,2048]{1,0:T(8,128)(2,1)S(1)}, bf16[24,2048]{1,0:T(8,128)(2,1)S(1)}, u32[]{:S(2)}, u32[]{:S(2)}) %collective-permute-start.3) | collective-permute-done | bytes 98336 | tf_op jit(solution)/shard_map/ppermute | solution.py:288
  16.5 0.0 collective-permute-done.4.w3
  16.5 0.1 shard_map.70
  16.6 1.6 %collective-permute-start.11 = (bf16[96,2048]{1,0:T(8,128)(2,1)S(1)}, bf16[96,2048]{1,0:T(8,128)(2,1)S(1)}, u32[]{:S(2)}, u32[]{:S(2)}) collective-permute-start(bf16[96,2048]{1,0:T(8,128)(2,1)S(1)} %get-tuple-element.42.refs_2_), channel_id=1, source_target_pairs={{0,2},{1,5},{2,0},{3,7},{4,6},{5,1},{6,4},{7,3},{8,10},{9,13},{10,... | collective-permute-start | bytes 1179656 | tf_op jit(solution)/shard_map/ppermute | solution.py:288
  18.1 1.5 %collective-permute-start.8 = (bf16[48,2048]{1,0:T(8,128)(2,1)S(1)}, bf16[48,2048]{1,0:T(8,128)(2,1)S(1)}, u32[]{:S(2)}, u32[]{:S(2)}) collective-permute-start(bf16[48,2048]{1,0:T(8,128)(2,1)S(1)} %get-tuple-element.40), channel_id=1, source_target_pairs={{0,4},{1,3},{2,6},{3,1},{4,0},{5,7},{6,2},{7,5},{8,12},{9,11},{10,... | collective-permute-start | bytes 589832 | tf_op jit(solution)/shard_map/ppermute | solution.py:288
  19.6 0.5 collective-permute-start.5
  20.1 3.6 %collective-permute-done.8.refs_3_ = bf16[48,2048]{1,0:T(8,128)(2,1)S(1)} collective-permute-done((bf16[48,2048]{1,0:T(8,128)(2,1)S(1)}, bf16[48,2048]{1,0:T(8,128)(2,1)S(1)}, u32[]{:S(2)}, u32[]{:S(2)}) %collective-permute-start.8) | collective-permute-done | bytes 196640 | tf_op jit(solution)/shard_map/ppermute | solution.py:288
  23.8 0.0 collective-permute-start.13
  23.8 1.3 %collective-permute-start.9 = (bf16[48,2048]{1,0:T(8,128)(2,1)S(1)}, bf16[48,2048]{1,0:T(8,128)(2,1)S(1)}, u32[]{:S(2)}, u32[]{:S(2)}) collective-permute-start(bf16[48,2048]{1,0:T(8,128)(2,1)S(1)} %collective-permute-done.8.refs_3_), channel_id=1, source_target_pairs={{0,2},{1,5},{2,0},{3,7},{4,6},{5,1},{6,4},{7,3},{8,10},{9,13},{10,... | collective-permute-start | bytes 589832 | tf_op jit(solution)/shard_map/ppermute | solution.py:288
  25.1 0.5 shard_map.69
  25.7 0.0 collective-permute-done.17.got_a
  25.7 0.7 %collective-permute-start.16 = (bf16[96,2048]{1,0:T(8,128)(2,1)S(1)}, bf16[96,2048]{1,0:T(8,128)(2,1)S(1)}, u32[]{:S(2)}, u32[]{:S(2)}) collective-permute-start(bf16[96,2048]{1,0:T(8,128)(2,1)S(1)} %get-tuple-element.48), channel_id=1, source_target_pairs={{0,2},{1,5},{2,0},{3,7},{4,6},{5,1},{6,4},{7,3},{8,10},{9,13},{10,... | collective-permute-start | bytes 1179656 | tf_op jit(solution)/shard_map/ppermute | solution.py:288
  26.4 0.1 shard_map.73
  26.5 0.0 collective-permute-done.5.refs_4_
  26.5 1.6 %collective-permute-start.18 = (bf16[96,2048]{1,0:T(8,128)(2,1)S(1)}, bf16[96,2048]{1,0:T(8,128)(2,1)S(1)}, u32[]{:S(2)}, u32[]{:S(2)}) collective-permute-start(bf16[96,2048]{1,0:T(8,128)(2,1)S(1)} %shard_map.73), channel_id=1, source_target_pairs={{0,4},{1,3},{2,6},{3,1},{4,0},{5,7},{6,2},{7,5},{8,12},{9,11},{10,... | collective-permute-start | bytes 1179656 | tf_op jit(solution)/shard_map/ppermute | solution.py:288
  28.1 0.0 collective-permute-done.11.refs_5_
  28.1 1.4 %collective-permute-start.6 = (bf16[48,2048]{1,0:T(8,128)(2,1)S(1)}, bf16[48,2048]{1,0:T(8,128)(2,1)S(1)}, u32[]{:S(2)}, u32[]{:S(2)}) collective-permute-start(bf16[48,2048]{1,0:T(8,128)(2,1)S(1)} %collective-permute-done.5.refs_4_), channel_id=1, source_target_pairs={{0,2},{1,5},{2,0},{3,7},{4,6},{5,1},{6,4},{7,3},{8,10},{9,13},{10,... | collective-permute-start | bytes 589832 | tf_op jit(solution)/shard_map/ppermute | solution.py:288
  29.4 0.0 collective-permute-done.13.refs_7_
  29.4 0.0 collective-permute-start.12
  29.5 0.3 collective-permute-done.9.refs_2_
  29.8 0.2 collective-permute-start.15
  30.0 10.0 %collective-permute-done.6.refs_2_ = bf16[48,2048]{1,0:T(8,128)(2,1)S(1)} collective-permute-done((bf16[48,2048]{1,0:T(8,128)(2,1)S(1)}, bf16[48,2048]{1,0:T(8,128)(2,1)S(1)}, u32[]{:S(2)}, u32[]{:S(2)}) %collective-permute-start.6) | collective-permute-done | bytes 196640 | tf_op jit(solution)/shard_map/ppermute | solution.py:288
  40.0 0.0 collective-permute-start.14
  40.0 0.0 collective-permute-done.16.got_b
  40.0 0.5 collective-permute-start.10
  40.5 0.0 collective-permute-done.18.got2
  40.5 0.1 collective-permute-start.7
  40.6 0.1 shard_map.74
  40.7 0.7 %collective-permute-done.14.refs_8_ = bf16[48,2048]{1,0:T(8,128)(2,1)S(1)} collective-permute-done((bf16[48,2048]{1,0:T(8,128)(2,1)S(1)}, bf16[48,2048]{1,0:T(8,128)(2,1)S(1)}, u32[]{:S(2)}, u32[]{:S(2)}) %collective-permute-start.14) | collective-permute-done | bytes 196640 | tf_op jit(solution)/shard_map/ppermute | solution.py:288
  41.4 2.6 %collective-permute-start.19 = (bf16[24,2048]{1,0:T(8,128)(2,1)S(1)}, bf16[24,2048]{1,0:T(8,128)(2,1)S(1)}, u32[]{:S(2)}, u32[]{:S(2)}) collective-permute-start(bf16[24,2048]{1,0:T(8,128)(2,1)S(1)} %get-tuple-element.52), channel_id=1, source_target_pairs={{0,8},{1,9},{2,10},{3,11},{4,12},{5,13},{6,14},{7,15},{8,0},{9,1},... | collective-permute-start | bytes 294920 | tf_op jit(solution)/shard_map/ppermute | solution.py:288
  44.0 0.0 collective-permute-done.12.refs_6_
  44.0 0.9 %collective-permute-start.20 = (bf16[24,2048]{1,0:T(8,128)(2,1)S(1)}, bf16[24,2048]{1,0:T(8,128)(2,1)S(1)}, u32[]{:S(2)}, u32[]{:S(2)}) collective-permute-start(bf16[24,2048]{1,0:T(8,128)(2,1)S(1)} %get-tuple-element.53), channel_id=1, source_target_pairs={{0,16},{1,17},{2,18},{3,19},{4,20},{5,21},{6,22},{7,23},{8,24},{9,... | collective-permute-start | bytes 294920 | tf_op jit(solution)/shard_map/ppermute | solution.py:288
  44.9 0.0 collective-permute-done.15.refs_9_
  44.9 1.5 %collective-permute-start.21 = (bf16[24,2048]{1,0:T(8,128)(2,1)S(1)}, bf16[24,2048]{1,0:T(8,128)(2,1)S(1)}, u32[]{:S(2)}, u32[]{:S(2)}) collective-permute-start(bf16[24,2048]{1,0:T(8,128)(2,1)S(1)} %get-tuple-element.54), channel_id=1, source_target_pairs={{0,24},{1,25},{2,26},{3,27},{4,28},{5,29},{6,30},{7,31},{8,16},{9,... | collective-permute-start | bytes 294920 | tf_op jit(solution)/shard_map/ppermute | solution.py:288
  46.5 1.2 %shard_map.71 = (f32[768,128]{1,0:T(8,128)S(1)}, f32[128,2048]{1,0:T(8,128)S(1)}) custom-call(bf16[256,2048]{1,0:T(8,128)(2,1)S(1)} %get-tuple-element.33.refs_2_.refs_0_, bf16[576,128]{1,0:T(8,128)(2,1)S(1)} %get-tuple-element.41.refs_1_, bf16[96,2048]{1,0:T(8,128)(2,1)S(1)} %get-tuple-element.42.refs_2_, ...), custom_call_target="tpu_custom_call" | custom-call | tf_op jit(solution)/shard_map/pallas_call | solution.py:296
  47.6 0.0 collective-permute-done.10.refs_3_
  47.7 0.4 shard_map.72
  48.1 0.0 collective-permute-done.7.refs_3_
  48.1 0.0 collective-permute-done.19.refs_7_
  48.1 6.5 %collective-permute-done.20.refs_8_ = bf16[24,2048]{1,0:T(8,128)(2,1)S(1)} collective-permute-done((bf16[24,2048]{1,0:T(8,128)(2,1)S(1)}, bf16[24,2048]{1,0:T(8,128)(2,1)S(1)}, u32[]{:S(2)}, u32[]{:S(2)}) %collective-permute-start.20) | collective-permute-done | bytes 98336 | tf_op jit(solution)/shard_map/ppermute | solution.py:288
  54.7 0.0 collective-permute-done.21.refs_9_
  54.7 1.3 %shard_map.75 = (bf16[128,768]{1,0:T(8,128)(2,1)}, bf16[128,2048]{1,0:T(8,128)(2,1)}, f32[24,2048]{1,0:T(8,128)}) custom-call(bf16[256,2048]{1,0:T(8,128)(2,1)S(1)} %get-tuple-element.33.refs_2_.refs_0_, bf16[96,128]{1,0:T(8,128)(2,1)S(1)} %get-tuple-element.36.refs_1_, bf16[48,2048]{1,0:T(8,128)(2,1)S(1)} %collective-permute-done.6.refs_2_, ...), custom_call_target="tpu_custom_call" | custom-call | tf_op jit(solution)/shard_map/pallas_call | solution.py:296
Async XLA Ops:
  0.6 7.8 %collective-permute-start = (bf16[128,2048]{1,0:T(8,128)(2,1)}, bf16[128,2048]{1,0:T(8,128)(2,1)S(1)}, u32[]{:S(2)}, u32[]{:S(2)}) collective-permute-start(bf16[128,2048]{1,0:T(8,128)(2,1)} %refs_0_.1), channel_id=1, source_target_pairs={{0,1},{1,0},{2,3},{3,2},{4,5},{5,4},{6,7},{7,6},{8,9},{9,8},{10,11... | collective-permute-start | bytes 1572872 | tf_op jit(solution)/shard_map/ppermute | solution.py:288
  1.2 7.2 %collective-permute-start.1 = (bf16[128,768]{1,0:T(8,128)(2,1)}, bf16[128,768]{1,0:T(8,128)(2,1)S(1)}, u32[]{:S(2)}, u32[]{:S(2)}) collective-permute-start(bf16[128,768]{1,0:T(8,128)(2,1)} %refs_1_.1), channel_id=1, source_target_pairs={{0,1},{1,0},{2,3},{3,2},{4,5},{5,4},{6,7},{7,6},{8,9},{9,8},{10,11... | collective-permute-start | bytes 589832 | tf_op jit(solution)/shard_map/ppermute | solution.py:288
  2.8 8.0 %collective-permute-start.2 = (bf16[24,2048]{1,0:T(8,128)(2,1)S(1)}, bf16[24,2048]{1,0:T(8,128)(2,1)S(1)}, u32[]{:S(2)}, u32[]{:S(2)}) collective-permute-start(bf16[24,2048]{1,0:T(8,128)(2,1)S(1)} %get-tuple-element.37.w0), channel_id=1, source_target_pairs={{0,8},{1,9},{2,10},{3,11},{4,12},{5,13},{6,14},{7,15},{8,0},{9,1},... | collective-permute-start | bytes 294920 | tf_op jit(solution)/shard_map/ppermute | solution.py:288
  5.8 10.7 %collective-permute-start.3 = (bf16[24,2048]{1,0:T(8,128)(2,1)S(1)}, bf16[24,2048]{1,0:T(8,128)(2,1)S(1)}, u32[]{:S(2)}, u32[]{:S(2)}) collective-permute-start(bf16[24,2048]{1,0:T(8,128)(2,1)S(1)} %get-tuple-element.37.w0), channel_id=1, source_target_pairs={{0,16},{1,17},{2,18},{3,19},{4,20},{5,21},{6,22},{7,23},{8,24},{9,... | collective-permute-start | bytes 294920 | tf_op jit(solution)/shard_map/ppermute | solution.py:288
  8.4 8.1 %collective-permute-start.4 = (bf16[24,2048]{1,0:T(8,128)(2,1)S(1)}, bf16[24,2048]{1,0:T(8,128)(2,1)S(1)}, u32[]{:S(2)}, u32[]{:S(2)}) collective-permute-start(bf16[24,2048]{1,0:T(8,128)(2,1)S(1)} %get-tuple-element.37.w0), channel_id=1, source_target_pairs={{0,24},{1,25},{2,26},{3,27},{4,28},{5,29},{6,30},{7,31},{8,16},{9,... | collective-permute-start | bytes 294920 | tf_op jit(solution)/shard_map/ppermute | solution.py:288
  9.0 16.6 %collective-permute-start.17 = (bf16[96,2048]{1,0:T(8,128)(2,1)S(1)}, bf16[96,2048]{1,0:T(8,128)(2,1)S(1)}, u32[]{:S(2)}, u32[]{:S(2)}) collective-permute-start(bf16[96,2048]{1,0:T(8,128)(2,1)S(1)} %get-tuple-element.50), channel_id=1, source_target_pairs={{0,2},{1,5},{2,0},{3,7},{4,6},{5,1},{6,4},{7,3},{8,10},{9,13},{10,... | collective-permute-start | bytes 1179656 | tf_op jit(solution)/shard_map/ppermute | solution.py:288
  16.6 11.5 %collective-permute-start.11 = (bf16[96,2048]{1,0:T(8,128)(2,1)S(1)}, bf16[96,2048]{1,0:T(8,128)(2,1)S(1)}, u32[]{:S(2)}, u32[]{:S(2)}) collective-permute-start(bf16[96,2048]{1,0:T(8,128)(2,1)S(1)} %get-tuple-element.42.refs_2_), channel_id=1, source_target_pairs={{0,2},{1,5},{2,0},{3,7},{4,6},{5,1},{6,4},{7,3},{8,10},{9,13},{10,... | collective-permute-start | bytes 1179656 | tf_op jit(solution)/shard_map/ppermute | solution.py:288
  18.1 5.7 %collective-permute-start.8 = (bf16[48,2048]{1,0:T(8,128)(2,1)S(1)}, bf16[48,2048]{1,0:T(8,128)(2,1)S(1)}, u32[]{:S(2)}, u32[]{:S(2)}) collective-permute-start(bf16[48,2048]{1,0:T(8,128)(2,1)S(1)} %get-tuple-element.40), channel_id=1, source_target_pairs={{0,4},{1,3},{2,6},{3,1},{4,0},{5,7},{6,2},{7,5},{8,12},{9,11},{10,... | collective-permute-start | bytes 589832 | tf_op jit(solution)/shard_map/ppermute | solution.py:288
  19.6 6.9 %collective-permute-start.5 = (bf16[48,2048]{1,0:T(8,128)(2,1)S(1)}, bf16[48,2048]{1,0:T(8,128)(2,1)S(1)}, u32[]{:S(2)}, u32[]{:S(2)}) collective-permute-start(bf16[48,2048]{1,0:T(8,128)(2,1)S(1)} %get-tuple-element.38), channel_id=1, source_target_pairs={{0,4},{1,3},{2,6},{3,1},{4,0},{5,7},{6,2},{7,5},{8,12},{9,11},{10,... | collective-permute-start | bytes 589832 | tf_op jit(solution)/shard_map/ppermute | solution.py:288
  23.8 5.7 %collective-permute-start.13 = (bf16[48,2048]{1,0:T(8,128)(2,1)S(1)}, bf16[48,2048]{1,0:T(8,128)(2,1)S(1)}, u32[]{:S(2)}, u32[]{:S(2)}) collective-permute-start(bf16[48,2048]{1,0:T(8,128)(2,1)S(1)} %collective-permute-done.8.refs_3_), channel_id=1, source_target_pairs={{0,1},{1,0},{2,3},{3,2},{4,5},{5,4},{6,7},{7,6},{8,9},{9,8},{10,11... | collective-permute-start | bytes 589832 | tf_op jit(solution)/shard_map/ppermute | solution.py:288
  23.8 6.0 %collective-permute-start.9 = (bf16[48,2048]{1,0:T(8,128)(2,1)S(1)}, bf16[48,2048]{1,0:T(8,128)(2,1)S(1)}, u32[]{:S(2)}, u32[]{:S(2)}) collective-permute-start(bf16[48,2048]{1,0:T(8,128)(2,1)S(1)} %collective-permute-done.8.refs_3_), channel_id=1, source_target_pairs={{0,2},{1,5},{2,0},{3,7},{4,6},{5,1},{6,4},{7,3},{8,10},{9,13},{10,... | collective-permute-start | bytes 589832 | tf_op jit(solution)/shard_map/ppermute | solution.py:288
  25.7 14.3 %collective-permute-start.16 = (bf16[96,2048]{1,0:T(8,128)(2,1)S(1)}, bf16[96,2048]{1,0:T(8,128)(2,1)S(1)}, u32[]{:S(2)}, u32[]{:S(2)}) collective-permute-start(bf16[96,2048]{1,0:T(8,128)(2,1)S(1)} %get-tuple-element.48), channel_id=1, source_target_pairs={{0,2},{1,5},{2,0},{3,7},{4,6},{5,1},{6,4},{7,3},{8,10},{9,13},{10,... | collective-permute-start | bytes 1179656 | tf_op jit(solution)/shard_map/ppermute | solution.py:288
  26.5 14.0 %collective-permute-start.18 = (bf16[96,2048]{1,0:T(8,128)(2,1)S(1)}, bf16[96,2048]{1,0:T(8,128)(2,1)S(1)}, u32[]{:S(2)}, u32[]{:S(2)}) collective-permute-start(bf16[96,2048]{1,0:T(8,128)(2,1)S(1)} %shard_map.73), channel_id=1, source_target_pairs={{0,4},{1,3},{2,6},{3,1},{4,0},{5,7},{6,2},{7,5},{8,12},{9,11},{10,... | collective-permute-start | bytes 1179656 | tf_op jit(solution)/shard_map/ppermute | solution.py:288
  28.1 11.9 %collective-permute-start.6 = (bf16[48,2048]{1,0:T(8,128)(2,1)S(1)}, bf16[48,2048]{1,0:T(8,128)(2,1)S(1)}, u32[]{:S(2)}, u32[]{:S(2)}) collective-permute-start(bf16[48,2048]{1,0:T(8,128)(2,1)S(1)} %collective-permute-done.5.refs_4_), channel_id=1, source_target_pairs={{0,2},{1,5},{2,0},{3,7},{4,6},{5,1},{6,4},{7,3},{8,10},{9,13},{10,... | collective-permute-start | bytes 589832 | tf_op jit(solution)/shard_map/ppermute | solution.py:288
  29.4 14.5 %collective-permute-start.12 = (bf16[96,2048]{1,0:T(8,128)(2,1)S(1)}, bf16[96,2048]{1,0:T(8,128)(2,1)S(1)}, u32[]{:S(2)}, u32[]{:S(2)}) collective-permute-start(bf16[96,2048]{1,0:T(8,128)(2,1)S(1)} %get-tuple-element.42.refs_2_), channel_id=1, source_target_pairs={{0,1},{1,0},{2,3},{3,2},{4,5},{5,4},{6,7},{7,6},{8,9},{9,8},{10,11... | collective-permute-start | bytes 1179656 | tf_op jit(solution)/shard_map/ppermute | solution.py:288
  29.8 15.1 %collective-permute-start.15 = (bf16[96,2048]{1,0:T(8,128)(2,1)S(1)}, bf16[96,2048]{1,0:T(8,128)(2,1)S(1)}, u32[]{:S(2)}, u32[]{:S(2)}) collective-permute-start(bf16[96,2048]{1,0:T(8,128)(2,1)S(1)} %collective-permute-done.11.refs_5_), channel_id=1, source_target_pairs={{0,1},{1,0},{2,3},{3,2},{4,5},{5,4},{6,7},{7,6},{8,9},{9,8},{10,11... | collective-permute-start | bytes 1179656 | tf_op jit(solution)/shard_map/ppermute | solution.py:288
  40.0 1.4 %collective-permute-start.14 = (bf16[48,2048]{1,0:T(8,128)(2,1)S(1)}, bf16[48,2048]{1,0:T(8,128)(2,1)S(1)}, u32[]{:S(2)}, u32[]{:S(2)}) collective-permute-start(bf16[48,2048]{1,0:T(8,128)(2,1)S(1)} %collective-permute-done.5.refs_4_), channel_id=1, source_target_pairs={{0,1},{1,0},{2,3},{3,2},{4,5},{5,4},{6,7},{7,6},{8,9},{9,8},{10,11... | collective-permute-start | bytes 589832 | tf_op jit(solution)/shard_map/ppermute | solution.py:288
  40.0 7.7 %collective-permute-start.10 = (bf16[48,2048]{1,0:T(8,128)(2,1)S(1)}, bf16[48,2048]{1,0:T(8,128)(2,1)S(1)}, u32[]{:S(2)}, u32[]{:S(2)}) collective-permute-start(bf16[48,2048]{1,0:T(8,128)(2,1)S(1)} %collective-permute-done.9.refs_2_), channel_id=1, source_target_pairs={{0,1},{1,0},{2,3},{3,2},{4,5},{5,4},{6,7},{7,6},{8,9},{9,8},{10,11... | collective-permute-start | bytes 589832 | tf_op jit(solution)/shard_map/ppermute | solution.py:288
  40.5 7.6 %collective-permute-start.7 = (bf16[48,2048]{1,0:T(8,128)(2,1)S(1)}, bf16[48,2048]{1,0:T(8,128)(2,1)S(1)}, u32[]{:S(2)}, u32[]{:S(2)}) collective-permute-start(bf16[48,2048]{1,0:T(8,128)(2,1)S(1)} %collective-permute-done.6.refs_2_), channel_id=1, source_target_pairs={{0,1},{1,0},{2,3},{3,2},{4,5},{5,4},{6,7},{7,6},{8,9},{9,8},{10,11... | collective-permute-start | bytes 589832 | tf_op jit(solution)/shard_map/ppermute | solution.py:288
  41.4 6.7 %collective-permute-start.19 = (bf16[24,2048]{1,0:T(8,128)(2,1)S(1)}, bf16[24,2048]{1,0:T(8,128)(2,1)S(1)}, u32[]{:S(2)}, u32[]{:S(2)}) collective-permute-start(bf16[24,2048]{1,0:T(8,128)(2,1)S(1)} %get-tuple-element.52), channel_id=1, source_target_pairs={{0,8},{1,9},{2,10},{3,11},{4,12},{5,13},{6,14},{7,15},{8,0},{9,1},... | collective-permute-start | bytes 294920 | tf_op jit(solution)/shard_map/ppermute | solution.py:288
  44.0 10.7 %collective-permute-start.20 = (bf16[24,2048]{1,0:T(8,128)(2,1)S(1)}, bf16[24,2048]{1,0:T(8,128)(2,1)S(1)}, u32[]{:S(2)}, u32[]{:S(2)}) collective-permute-start(bf16[24,2048]{1,0:T(8,128)(2,1)S(1)} %get-tuple-element.53), channel_id=1, source_target_pairs={{0,16},{1,17},{2,18},{3,19},{4,20},{5,21},{6,22},{7,23},{8,24},{9,... | collective-permute-start | bytes 294920 | tf_op jit(solution)/shard_map/ppermute | solution.py:288
  44.9 9.7 %collective-permute-start.21 = (bf16[24,2048]{1,0:T(8,128)(2,1)S(1)}, bf16[24,2048]{1,0:T(8,128)(2,1)S(1)}, u32[]{:S(2)}, u32[]{:S(2)}) collective-permute-start(bf16[24,2048]{1,0:T(8,128)(2,1)S(1)} %get-tuple-element.54), channel_id=1, source_target_pairs={{0,24},{1,25},{2,26},{3,27},{4,28},{5,29},{6,30},{7,31},{8,16},{9,... | collective-permute-start | bytes 294920 | tf_op jit(solution)/shard_map/ppermute | solution.py:288

commit v4 on v3

--- a/solution.py
+++ b/solution.py
@@ -136,27 +136,28 @@
                 out[at : at + per, :] = cot_t[row_block(g, c, j, block, per), :]
 
 
-def term_kernel(
-    per, factor, tok2, cot2, normed1, early, mid, late, sent, going, kept_cot, normed, cot_t
-):
-    rows = tok2.shape[0]
+def pick_kernel(per, cot2, early, mid, late, last, going, kept_cot, cot_t):
     quarter = 4 * per
     g = lax.axis_index("grp")
     c = lax.axis_index("node")
-    normed[:rows, :] = normed1[...]
-    normed[rows:, :] = normalized(tok2)
     cot_t[...] = cot2[...].astype(F32).T
 
     def both(i, own):
         swapped = [cot_t[row_block(g, c, 0, (i, k), per), :] for k in range(4)]
         return jnp.concatenate([own, jnp.concatenate(swapped, axis=0)], axis=1).astype(BF16)
 
+    last[...] = both(3, jnp.concatenate([mid[: 2 * per, :], late[: 2 * per, :]], axis=0))
+    going[...] = both(1, early[2 * quarter : 3 * quarter, :])
     kept_cot[:quarter, :] = both(0, early[:quarter, :])
     kept_cot[quarter:, :] = both(2, early[quarter : 2 * quarter, :])
-    going[...] = both(1, early[2 * quarter : 3 * quarter, :])
-    last = jnp.concatenate([mid[: 2 * per, :], late[: 2 * per, :]], axis=0)
+
+
+def term_kernel(factor, tok2, normed1, last, sent, normed):
+    rows = tok2.shape[0]
+    normed[:rows, :] = normed1[...]
+    normed[rows:, :] = normalized(tok2)
     sent[...] = (
-        jnp.dot(both(3, last), normed[...], preferred_element_type=F32) * factor
+        jnp.dot(last[...], normed[...], preferred_element_type=F32) * factor
     ).astype(BF16)
 
 
@@ -339,19 +340,23 @@
         ],
         far=(0, 1, 2, 3),
     )
-    sent_a, going, kept_cot, normed = call(
-        lambda *refs: term_kernel(per, factor, *refs),
+    last, going, kept_cot = call(
+        lambda *refs: pick_kernel(per, *refs),
         [
-            held(quarter, width, BF16),
+            held(quarter, 2 * rows, BF16),
             held(quarter, 2 * rows, BF16),
             held(2 * quarter, 2 * rows, BF16),
-            held(2 * rows, width, BF16),
         ],
-        tokens2,
         cotangent2,
-        normed1,
         *cots,
         scratch=[pltpu.VMEM((height, rows), F32)],
+    )
+    sent_a, normed = call(
+        lambda *refs: term_kernel(factor, *refs),
+        [held(quarter, width, BF16), held(2 * rows, width, BF16)],
+        tokens2,
+        normed1,
+        last,
     )
     got_a = move(sent_a, swap_first())
     by_z = [own] + [move(own, swap_z(k)) for k in (1, 2, 3)]

time: 56.2 us -> 56.2 us (level)
    pallas_call x9 -> x10, Pallas kernels: 5.83 us -> 5.91 us  [call(): pl.pallas_call(kernel, out_shape=outs, in_specs=[FAR if i in far else VME...]
where the time goes in v4:
time: 56.2 us; the launch traced here: 56 us
  waiting for transfers between devices  26.9 us (48%)
  starting transfers between devices  22.4 us (40%)
  Pallas kernels  5.91 us (11%)
  between operations  0.74 us (1%)
    ppermute x22, waiting for transfers between devices, move(): return lax.ppermute(array, AXES, pairs)  26.9 us
    ppermute x22, starting transfers between devices, move(): return lax.ppermute(array, AXES, pairs)  22.4 us
    pallas_call x10, Pallas kernels, call(): pl.pallas_call(kernel, out_shape=outs, in_specs=[FAR if i in far else VME...  5.91 us
  transfers between devices with their start and end apart: 22, of which 6 were waited for; matrix products, arithmetic and copies ran while one was open for 0% of the time, Pallas kernels for 8%

profile of v4, /device:TPU:0, one launch (start us, length us, event | category | flops | bytes accessed | tf_op | source)
XLA Modules:
  0.0 56.0 jit_solution(794591152178576988)
XLA Ops:
  0.6 0.6 collective-permute-start
  1.2 0.1 collective-permute-start.1
  1.3 1.5 %shard_map.67 = (bf16[24,2048]{1,0:T(8,128)(2,1)S(1)}, bf16[128,2048]{1,0:T(8,128)(2,1)S(1)}, f32[576,128]{1,0:T(8,128)S(1)}, f32[96,128]{1,0:T(8,128)S(1)}, f32[96,128]{1,0:T(8,128)S(1)}) custom-call(bf16[128,2048]{1,0:T(8,128)(2,1)} %refs_0_.1, bf16[128,768]{1,0:T(8,128)(2,1)} %refs_1_.1, bf16[24,2048]{1,0:T(8,128)(2,1)} %refs_2_.1, f32[16,24]{1,0:T(8,128)} %bitcast.1), custom_call_target="tpu_custom_call" | custom-call | tf_op jit(solution)/shard_map/pallas_call | solution.py:297
  2.8 3.1 %collective-permute-start.2 = (bf16[24,2048]{1,0:T(8,128)(2,1)S(1)}, bf16[24,2048]{1,0:T(8,128)(2,1)S(1)}, u32[]{:S(2)}, u32[]{:S(2)}) collective-permute-start(bf16[24,2048]{1,0:T(8,128)(2,1)S(1)} %get-tuple-element.39.w0), channel_id=1, source_target_pairs={{0,8},{1,9},{2,10},{3,11},{4,12},{5,13},{6,14},{7,15},{8,0},{9,1},... | collective-permute-start | bytes 294920 | tf_op jit(solution)/shard_map/ppermute | solution.py:289
  5.8 2.6 %collective-permute-start.3 = (bf16[24,2048]{1,0:T(8,128)(2,1)S(1)}, bf16[24,2048]{1,0:T(8,128)(2,1)S(1)}, u32[]{:S(2)}, u32[]{:S(2)}) collective-permute-start(bf16[24,2048]{1,0:T(8,128)(2,1)S(1)} %get-tuple-element.39.w0), channel_id=1, source_target_pairs={{0,16},{1,17},{2,18},{3,19},{4,20},{5,21},{6,22},{7,23},{8,24},{9,... | collective-permute-start | bytes 294920 | tf_op jit(solution)/shard_map/ppermute | solution.py:289
  8.4 0.0 collective-permute-start.4
  8.4 0.0 collective-permute-done.1.refs_0_
  8.4 0.2 shard_map.68
  8.6 0.0 collective-permute-done.refs_0_
  8.6 0.5 shard_map.69
  9.1 1.8 %collective-permute-start.17 = (bf16[96,2048]{1,0:T(8,128)(2,1)S(1)}, bf16[96,2048]{1,0:T(8,128)(2,1)S(1)}, u32[]{:S(2)}, u32[]{:S(2)}) collective-permute-start(bf16[96,2048]{1,0:T(8,128)(2,1)S(1)} %get-tuple-element.52), channel_id=1, source_target_pairs={{0,2},{1,5},{2,0},{3,7},{4,6},{5,1},{6,4},{7,3},{8,10},{9,13},{10,... | collective-permute-start | bytes 1179656 | tf_op jit(solution)/shard_map/ppermute | solution.py:289
  10.9 0.0 collective-permute-done.2.w1
  10.9 5.6 %collective-permute-done.3.w2 = bf16[24,2048]{1,0:T(8,128)(2,1)S(1)} collective-permute-done((bf16[24,2048]{1,0:T(8,128)(2,1)S(1)}, bf16[24,2048]{1,0:T(8,128)(2,1)S(1)}, u32[]{:S(2)}, u32[]{:S(2)}) %collective-permute-start.3) | collective-permute-done | bytes 98336 | tf_op jit(solution)/shard_map/ppermute | solution.py:289
  16.5 0.0 collective-permute-done.4.w3
  16.5 0.1 shard_map.71
  16.6 1.6 %collective-permute-start.11 = (bf16[96,2048]{1,0:T(8,128)(2,1)S(1)}, bf16[96,2048]{1,0:T(8,128)(2,1)S(1)}, u32[]{:S(2)}, u32[]{:S(2)}) collective-permute-start(bf16[96,2048]{1,0:T(8,128)(2,1)S(1)} %get-tuple-element.44.refs_2_), channel_id=1, source_target_pairs={{0,2},{1,5},{2,0},{3,7},{4,6},{5,1},{6,4},{7,3},{8,10},{9,13},{10,... | collective-permute-start | bytes 1179656 | tf_op jit(solution)/shard_map/ppermute | solution.py:289
  18.1 1.5 %collective-permute-start.8 = (bf16[48,2048]{1,0:T(8,128)(2,1)S(1)}, bf16[48,2048]{1,0:T(8,128)(2,1)S(1)}, u32[]{:S(2)}, u32[]{:S(2)}) collective-permute-start(bf16[48,2048]{1,0:T(8,128)(2,1)S(1)} %get-tuple-element.42), channel_id=1, source_target_pairs={{0,4},{1,3},{2,6},{3,1},{4,0},{5,7},{6,2},{7,5},{8,12},{9,11},{10,... | collective-permute-start | bytes 589832 | tf_op jit(solution)/shard_map/ppermute | solution.py:289
  19.6 0.5 collective-permute-start.5
  20.1 3.6 %collective-permute-done.8.refs_3_ = bf16[48,2048]{1,0:T(8,128)(2,1)S(1)} collective-permute-done((bf16[48,2048]{1,0:T(8,128)(2,1)S(1)}, bf16[48,2048]{1,0:T(8,128)(2,1)S(1)}, u32[]{:S(2)}, u32[]{:S(2)}) %collective-permute-start.8) | collective-permute-done | bytes 196640 | tf_op jit(solution)/shard_map/ppermute | solution.py:289
  23.8 0.0 collective-permute-start.13
  23.8 1.3 %collective-permute-start.9 = (bf16[48,2048]{1,0:T(8,128)(2,1)S(1)}, bf16[48,2048]{1,0:T(8,128)(2,1)S(1)}, u32[]{:S(2)}, u32[]{:S(2)}) collective-permute-start(bf16[48,2048]{1,0:T(8,128)(2,1)S(1)} %collective-permute-done.8.refs_3_), channel_id=1, source_target_pairs={{0,2},{1,5},{2,0},{3,7},{4,6},{5,1},{6,4},{7,3},{8,10},{9,13},{10,... | collective-permute-start | bytes 589832 | tf_op jit(solution)/shard_map/ppermute | solution.py:289
  25.1 0.5 shard_map.70
  25.7 0.0 collective-permute-done.17.got_a
  25.7 0.7 %collective-permute-start.16 = (bf16[96,2048]{1,0:T(8,128)(2,1)S(1)}, bf16[96,2048]{1,0:T(8,128)(2,1)S(1)}, u32[]{:S(2)}, u32[]{:S(2)}) collective-permute-start(bf16[96,2048]{1,0:T(8,128)(2,1)S(1)} %get-tuple-element.50), channel_id=1, source_target_pairs={{0,2},{1,5},{2,0},{3,7},{4,6},{5,1},{6,4},{7,3},{8,10},{9,13},{10,... | collective-permute-start | bytes 1179656 | tf_op jit(solution)/shard_map/ppermute | solution.py:289
  26.4 0.1 shard_map.74
  26.5 0.0 collective-permute-done.5.refs_4_
  26.5 1.6 %collective-permute-start.18 = (bf16[96,2048]{1,0:T(8,128)(2,1)S(1)}, bf16[96,2048]{1,0:T(8,128)(2,1)S(1)}, u32[]{:S(2)}, u32[]{:S(2)}) collective-permute-start(bf16[96,2048]{1,0:T(8,128)(2,1)S(1)} %shard_map.74), channel_id=1, source_target_pairs={{0,4},{1,3},{2,6},{3,1},{4,0},{5,7},{6,2},{7,5},{8,12},{9,11},{10,... | collective-permute-start | bytes 1179656 | tf_op jit(solution)/shard_map/ppermute | solution.py:289
  28.1 0.0 collective-permute-done.11.refs_5_
  28.1 1.4 %collective-permute-start.6 = (bf16[48,2048]{1,0:T(8,128)(2,1)S(1)}, bf16[48,2048]{1,0:T(8,128)(2,1)S(1)}, u32[]{:S(2)}, u32[]{:S(2)}) collective-permute-start(bf16[48,2048]{1,0:T(8,128)(2,1)S(1)} %collective-permute-done.5.refs_4_), channel_id=1, source_target_pairs={{0,2},{1,5},{2,0},{3,7},{4,6},{5,1},{6,4},{7,3},{8,10},{9,13},{10,... | collective-permute-start | bytes 589832 | tf_op jit(solution)/shard_map/ppermute | solution.py:289
  29.4 0.0 collective-permute-done.13.refs_7_
  29.4 0.0 collective-permute-start.12
  29.5 0.3 collective-permute-done.9.refs_2_
  29.8 0.2 collective-permute-start.15
  30.0 10.0 %collective-permute-done.6.refs_2_ = bf16[48,2048]{1,0:T(8,128)(2,1)S(1)} collective-permute-done((bf16[48,2048]{1,0:T(8,128)(2,1)S(1)}, bf16[48,2048]{1,0:T(8,128)(2,1)S(1)}, u32[]{:S(2)}, u32[]{:S(2)}) %collective-permute-start.6) | collective-permute-done | bytes 196640 | tf_op jit(solution)/shard_map/ppermute | solution.py:289
  40.0 0.0 collective-permute-start.14
  40.0 0.0 collective-permute-done.16.got_b
  40.0 0.5 collective-permute-start.10
  40.5 0.0 collective-permute-done.18.got2
  40.5 0.1 collective-permute-start.7
  40.6 0.1 shard_map.75
  40.7 0.7 %collective-permute-done.14.refs_8_ = bf16[48,2048]{1,0:T(8,128)(2,1)S(1)} collective-permute-done((bf16[48,2048]{1,0:T(8,128)(2,1)S(1)}, bf16[48,2048]{1,0:T(8,128)(2,1)S(1)}, u32[]{:S(2)}, u32[]{:S(2)}) %collective-permute-start.14) | collective-permute-done | bytes 196640 | tf_op jit(solution)/shard_map/ppermute | solution.py:289
  41.4 2.6 %collective-permute-start.19 = (bf16[24,2048]{1,0:T(8,128)(2,1)S(1)}, bf16[24,2048]{1,0:T(8,128)(2,1)S(1)}, u32[]{:S(2)}, u32[]{:S(2)}) collective-permute-start(bf16[24,2048]{1,0:T(8,128)(2,1)S(1)} %get-tuple-element.54), channel_id=1, source_target_pairs={{0,8},{1,9},{2,10},{3,11},{4,12},{5,13},{6,14},{7,15},{8,0},{9,1},... | collective-permute-start | bytes 294920 | tf_op jit(solution)/shard_map/ppermute | solution.py:289
  44.0 0.0 collective-permute-done.12.refs_6_
  44.0 0.9 %collective-permute-start.20 = (bf16[24,2048]{1,0:T(8,128)(2,1)S(1)}, bf16[24,2048]{1,0:T(8,128)(2,1)S(1)}, u32[]{:S(2)}, u32[]{:S(2)}) collective-permute-start(bf16[24,2048]{1,0:T(8,128)(2,1)S(1)} %get-tuple-element.55), channel_id=1, source_target_pairs={{0,16},{1,17},{2,18},{3,19},{4,20},{5,21},{6,22},{7,23},{8,24},{9,... | collective-permute-start | bytes 294920 | tf_op jit(solution)/shard_map/ppermute | solution.py:289
  44.9 0.0 collective-permute-done.15.refs_9_
  44.9 1.5 %collective-permute-start.21 = (bf16[24,2048]{1,0:T(8,128)(2,1)S(1)}, bf16[24,2048]{1,0:T(8,128)(2,1)S(1)}, u32[]{:S(2)}, u32[]{:S(2)}) collective-permute-start(bf16[24,2048]{1,0:T(8,128)(2,1)S(1)} %get-tuple-element.56), channel_id=1, source_target_pairs={{0,24},{1,25},{2,26},{3,27},{4,28},{5,29},{6,30},{7,31},{8,16},{9,... | collective-permute-start | bytes 294920 | tf_op jit(solution)/shard_map/ppermute | solution.py:289
  46.5 1.2 %shard_map.72 = (f32[768,128]{1,0:T(8,128)S(1)}, f32[128,2048]{1,0:T(8,128)S(1)}) custom-call(bf16[256,2048]{1,0:T(8,128)(2,1)S(1)} %get-tuple-element.35.refs_2_.refs_0_, bf16[576,128]{1,0:T(8,128)(2,1)S(1)} %get-tuple-element.43.refs_1_, bf16[96,2048]{1,0:T(8,128)(2,1)S(1)} %get-tuple-element.44.refs_2_, ...), custom_call_target="tpu_custom_call" | custom-call | tf_op jit(solution)/shard_map/pallas_call | solution.py:297
  47.6 0.0 collective-permute-done.10.refs_3_
  47.7 0.4 shard_map.73
  48.1 0.0 collective-permute-done.7.refs_3_
  48.1 0.0 collective-permute-done.19.refs_7_
  48.1 6.5 %collective-permute-done.20.refs_8_ = bf16[24,2048]{1,0:T(8,128)(2,1)S(1)} collective-permute-done((bf16[24,2048]{1,0:T(8,128)(2,1)S(1)}, bf16[24,2048]{1,0:T(8,128)(2,1)S(1)}, u32[]{:S(2)}, u32[]{:S(2)}) %collective-permute-start.20) | collective-permute-done | bytes 98336 | tf_op jit(solution)/shard_map/ppermute | solution.py:289
  54.7 0.0 collective-permute-done.21.refs_9_
  54.7 1.3 %shard_map.76 = (bf16[128,768]{1,0:T(8,128)(2,1)}, bf16[128,2048]{1,0:T(8,128)(2,1)}, f32[24,2048]{1,0:T(8,128)}) custom-call(bf16[256,2048]{1,0:T(8,128)(2,1)S(1)} %get-tuple-element.35.refs_2_.refs_0_, bf16[96,128]{1,0:T(8,128)(2,1)S(1)} %get-tuple-element.38.refs_1_, bf16[48,2048]{1,0:T(8,128)(2,1)S(1)} %collective-permute-done.6.refs_2_, ...), custom_call_target="tpu_custom_call" | custom-call | tf_op jit(solution)/shard_map/pallas_call | solution.py:297
Async XLA Ops:
  0.6 8.0 %collective-permute-start = (bf16[128,2048]{1,0:T(8,128)(2,1)}, bf16[128,2048]{1,0:T(8,128)(2,1)S(1)}, u32[]{:S(2)}, u32[]{:S(2)}) collective-permute-start(bf16[128,2048]{1,0:T(8,128)(2,1)} %refs_0_.1), channel_id=1, source_target_pairs={{0,1},{1,0},{2,3},{3,2},{4,5},{5,4},{6,7},{7,6},{8,9},{9,8},{10,11... | collective-permute-start | bytes 1572872 | tf_op jit(solution)/shard_map/ppermute | solution.py:289
  1.2 7.2 %collective-permute-start.1 = (bf16[128,768]{1,0:T(8,128)(2,1)}, bf16[128,768]{1,0:T(8,128)(2,1)S(1)}, u32[]{:S(2)}, u32[]{:S(2)}) collective-permute-start(bf16[128,768]{1,0:T(8,128)(2,1)} %refs_1_.1), channel_id=1, source_target_pairs={{0,1},{1,0},{2,3},{3,2},{4,5},{5,4},{6,7},{7,6},{8,9},{9,8},{10,11... | collective-permute-start | bytes 589832 | tf_op jit(solution)/shard_map/ppermute | solution.py:289
  2.8 8.1 %collective-permute-start.2 = (bf16[24,2048]{1,0:T(8,128)(2,1)S(1)}, bf16[24,2048]{1,0:T(8,128)(2,1)S(1)}, u32[]{:S(2)}, u32[]{:S(2)}) collective-permute-start(bf16[24,2048]{1,0:T(8,128)(2,1)S(1)} %get-tuple-element.39.w0), channel_id=1, source_target_pairs={{0,8},{1,9},{2,10},{3,11},{4,12},{5,13},{6,14},{7,15},{8,0},{9,1},... | collective-permute-start | bytes 294920 | tf_op jit(solution)/shard_map/ppermute | solution.py:289
  5.8 10.7 %collective-permute-start.3 = (bf16[24,2048]{1,0:T(8,128)(2,1)S(1)}, bf16[24,2048]{1,0:T(8,128)(2,1)S(1)}, u32[]{:S(2)}, u32[]{:S(2)}) collective-permute-start(bf16[24,2048]{1,0:T(8,128)(2,1)S(1)} %get-tuple-element.39.w0), channel_id=1, source_target_pairs={{0,16},{1,17},{2,18},{3,19},{4,20},{5,21},{6,22},{7,23},{8,24},{9,... | collective-permute-start | bytes 294920 | tf_op jit(solution)/shard_map/ppermute | solution.py:289
  8.4 8.1 %collective-permute-start.4 = (bf16[24,2048]{1,0:T(8,128)(2,1)S(1)}, bf16[24,2048]{1,0:T(8,128)(2,1)S(1)}, u32[]{:S(2)}, u32[]{:S(2)}) collective-permute-start(bf16[24,2048]{1,0:T(8,128)(2,1)S(1)} %get-tuple-element.39.w0), channel_id=1, source_target_pairs={{0,24},{1,25},{2,26},{3,27},{4,28},{5,29},{6,30},{7,31},{8,16},{9,... | collective-permute-start | bytes 294920 | tf_op jit(solution)/shard_map/ppermute | solution.py:289
  9.1 16.6 %collective-permute-start.17 = (bf16[96,2048]{1,0:T(8,128)(2,1)S(1)}, bf16[96,2048]{1,0:T(8,128)(2,1)S(1)}, u32[]{:S(2)}, u32[]{:S(2)}) collective-permute-start(bf16[96,2048]{1,0:T(8,128)(2,1)S(1)} %get-tuple-element.52), channel_id=1, source_target_pairs={{0,2},{1,5},{2,0},{3,7},{4,6},{5,1},{6,4},{7,3},{8,10},{9,13},{10,... | collective-permute-start | bytes 1179656 | tf_op jit(solution)/shard_map/ppermute | solution.py:289
  16.6 11.5 %collective-permute-start.11 = (bf16[96,2048]{1,0:T(8,128)(2,1)S(1)}, bf16[96,2048]{1,0:T(8,128)(2,1)S(1)}, u32[]{:S(2)}, u32[]{:S(2)}) collective-permute-start(bf16[96,2048]{1,0:T(8,128)(2,1)S(1)} %get-tuple-element.44.refs_2_), channel_id=1, source_target_pairs={{0,2},{1,5},{2,0},{3,7},{4,6},{5,1},{6,4},{7,3},{8,10},{9,13},{10,... | collective-permute-start | bytes 1179656 | tf_op jit(solution)/shard_map/ppermute | solution.py:289
  18.1 5.7 %collective-permute-start.8 = (bf16[48,2048]{1,0:T(8,128)(2,1)S(1)}, bf16[48,2048]{1,0:T(8,128)(2,1)S(1)}, u32[]{:S(2)}, u32[]{:S(2)}) collective-permute-start(bf16[48,2048]{1,0:T(8,128)(2,1)S(1)} %get-tuple-element.42), channel_id=1, source_target_pairs={{0,4},{1,3},{2,6},{3,1},{4,0},{5,7},{6,2},{7,5},{8,12},{9,11},{10,... | collective-permute-start | bytes 589832 | tf_op jit(solution)/shard_map/ppermute | solution.py:289
  19.6 6.9 %collective-permute-start.5 = (bf16[48,2048]{1,0:T(8,128)(2,1)S(1)}, bf16[48,2048]{1,0:T(8,128)(2,1)S(1)}, u32[]{:S(2)}, u32[]{:S(2)}) collective-permute-start(bf16[48,2048]{1,0:T(8,128)(2,1)S(1)} %get-tuple-element.40), channel_id=1, source_target_pairs={{0,4},{1,3},{2,6},{3,1},{4,0},{5,7},{6,2},{7,5},{8,12},{9,11},{10,... | collective-permute-start | bytes 589832 | tf_op jit(solution)/shard_map/ppermute | solution.py:289
  23.8 5.7 %collective-permute-start.13 = (bf16[48,2048]{1,0:T(8,128)(2,1)S(1)}, bf16[48,2048]{1,0:T(8,128)(2,1)S(1)}, u32[]{:S(2)}, u32[]{:S(2)}) collective-permute-start(bf16[48,2048]{1,0:T(8,128)(2,1)S(1)} %collective-permute-done.8.refs_3_), channel_id=1, source_target_pairs={{0,1},{1,0},{2,3},{3,2},{4,5},{5,4},{6,7},{7,6},{8,9},{9,8},{10,11... | collective-permute-start | bytes 589832 | tf_op jit(solution)/shard_map/ppermute | solution.py:289
  23.8 6.0 %collective-permute-start.9 = (bf16[48,2048]{1,0:T(8,128)(2,1)S(1)}, bf16[48,2048]{1,0:T(8,128)(2,1)S(1)}, u32[]{:S(2)}, u32[]{:S(2)}) collective-permute-start(bf16[48,2048]{1,0:T(8,128)(2,1)S(1)} %collective-permute-done.8.refs_3_), channel_id=1, source_target_pairs={{0,2},{1,5},{2,0},{3,7},{4,6},{5,1},{6,4},{7,3},{8,10},{9,13},{10,... | collective-permute-start | bytes 589832 | tf_op jit(solution)/shard_map/ppermute | solution.py:289
  25.7 14.3 %collective-permute-start.16 = (bf16[96,2048]{1,0:T(8,128)(2,1)S(1)}, bf16[96,2048]{1,0:T(8,128)(2,1)S(1)}, u32[]{:S(2)}, u32[]{:S(2)}) collective-permute-start(bf16[96,2048]{1,0:T(8,128)(2,1)S(1)} %get-tuple-element.50), channel_id=1, source_target_pairs={{0,2},{1,5},{2,0},{3,7},{4,6},{5,1},{6,4},{7,3},{8,10},{9,13},{10,... | collective-permute-start | bytes 1179656 | tf_op jit(solution)/shard_map/ppermute | solution.py:289
  26.5 14.0 %collective-permute-start.18 = (bf16[96,2048]{1,0:T(8,128)(2,1)S(1)}, bf16[96,2048]{1,0:T(8,128)(2,1)S(1)}, u32[]{:S(2)}, u32[]{:S(2)}) collective-permute-start(bf16[96,2048]{1,0:T(8,128)(2,1)S(1)} %shard_map.74), channel_id=1, source_target_pairs={{0,4},{1,3},{2,6},{3,1},{4,0},{5,7},{6,2},{7,5},{8,12},{9,11},{10,... | collective-permute-start | bytes 1179656 | tf_op jit(solution)/shard_map/ppermute | solution.py:289
  28.1 11.9 %collective-permute-start.6 = (bf16[48,2048]{1,0:T(8,128)(2,1)S(1)}, bf16[48,2048]{1,0:T(8,128)(2,1)S(1)}, u32[]{:S(2)}, u32[]{:S(2)}) collective-permute-start(bf16[48,2048]{1,0:T(8,128)(2,1)S(1)} %collective-permute-done.5.refs_4_), channel_id=1, source_target_pairs={{0,2},{1,5},{2,0},{3,7},{4,6},{5,1},{6,4},{7,3},{8,10},{9,13},{10,... | collective-permute-start | bytes 589832 | tf_op jit(solution)/shard_map/ppermute | solution.py:289
  29.4 14.5 %collective-permute-start.12 = (bf16[96,2048]{1,0:T(8,128)(2,1)S(1)}, bf16[96,2048]{1,0:T(8,128)(2,1)S(1)}, u32[]{:S(2)}, u32[]{:S(2)}) collective-permute-start(bf16[96,2048]{1,0:T(8,128)(2,1)S(1)} %get-tuple-element.44.refs_2_), channel_id=1, source_target_pairs={{0,1},{1,0},{2,3},{3,2},{4,5},{5,4},{6,7},{7,6},{8,9},{9,8},{10,11... | collective-permute-start | bytes 1179656 | tf_op jit(solution)/shard_map/ppermute | solution.py:289
  29.8 15.1 %collective-permute-start.15 = (bf16[96,2048]{1,0:T(8,128)(2,1)S(1)}, bf16[96,2048]{1,0:T(8,128)(2,1)S(1)}, u32[]{:S(2)}, u32[]{:S(2)}) collective-permute-start(bf16[96,2048]{1,0:T(8,128)(2,1)S(1)} %collective-permute-done.11.refs_5_), channel_id=1, source_target_pairs={{0,1},{1,0},{2,3},{3,2},{4,5},{5,4},{6,7},{7,6},{8,9},{9,8},{10,11... | collective-permute-start | bytes 1179656 | tf_op jit(solution)/shard_map/ppermute | solution.py:289
  40.0 1.4 %collective-permute-start.14 = (bf16[48,2048]{1,0:T(8,128)(2,1)S(1)}, bf16[48,2048]{1,0:T(8,128)(2,1)S(1)}, u32[]{:S(2)}, u32[]{:S(2)}) collective-permute-start(bf16[48,2048]{1,0:T(8,128)(2,1)S(1)} %collective-permute-done.5.refs_4_), channel_id=1, source_target_pairs={{0,1},{1,0},{2,3},{3,2},{4,5},{5,4},{6,7},{7,6},{8,9},{9,8},{10,11... | collective-permute-start | bytes 589832 | tf_op jit(solution)/shard_map/ppermute | solution.py:289
  40.0 7.7 %collective-permute-start.10 = (bf16[48,2048]{1,0:T(8,128)(2,1)S(1)}, bf16[48,2048]{1,0:T(8,128)(2,1)S(1)}, u32[]{:S(2)}, u32[]{:S(2)}) collective-permute-start(bf16[48,2048]{1,0:T(8,128)(2,1)S(1)} %collective-permute-done.9.refs_2_), channel_id=1, source_target_pairs={{0,1},{1,0},{2,3},{3,2},{4,5},{5,4},{6,7},{7,6},{8,9},{9,8},{10,11... | collective-permute-start | bytes 589832 | tf_op jit(solution)/shard_map/ppermute | solution.py:289
  40.5 7.6 %collective-permute-start.7 = (bf16[48,2048]{1,0:T(8,128)(2,1)S(1)}, bf16[48,2048]{1,0:T(8,128)(2,1)S(1)}, u32[]{:S(2)}, u32[]{:S(2)}) collective-permute-start(bf16[48,2048]{1,0:T(8,128)(2,1)S(1)} %collective-permute-done.6.refs_2_), channel_id=1, source_target_pairs={{0,1},{1,0},{2,3},{3,2},{4,5},{5,4},{6,7},{7,6},{8,9},{9,8},{10,11... | collective-permute-start | bytes 589832 | tf_op jit(solution)/shard_map/ppermute | solution.py:289
  41.4 6.7 %collective-permute-start.19 = (bf16[24,2048]{1,0:T(8,128)(2,1)S(1)}, bf16[24,2048]{1,0:T(8,128)(2,1)S(1)}, u32[]{:S(2)}, u32[]{:S(2)}) collective-permute-start(bf16[24,2048]{1,0:T(8,128)(2,1)S(1)} %get-tuple-element.54), channel_id=1, source_target_pairs={{0,8},{1,9},{2,10},{3,11},{4,12},{5,13},{6,14},{7,15},{8,0},{9,1},... | collective-permute-start | bytes 294920 | tf_op jit(solution)/shard_map/ppermute | solution.py:289
  44.0 10.7 %collective-permute-start.20 = (bf16[24,2048]{1,0:T(8,128)(2,1)S(1)}, bf16[24,2048]{1,0:T(8,128)(2,1)S(1)}, u32[]{:S(2)}, u32[]{:S(2)}) collective-permute-start(bf16[24,2048]{1,0:T(8,128)(2,1)S(1)} %get-tuple-element.55), channel_id=1, source_target_pairs={{0,16},{1,17},{2,18},{3,19},{4,20},{5,21},{6,22},{7,23},{8,24},{9,... | collective-permute-start | bytes 294920 | tf_op jit(solution)/shard_map/ppermute | solution.py:289
  44.9 9.7 %collective-permute-start.21 = (bf16[24,2048]{1,0:T(8,128)(2,1)S(1)}, bf16[24,2048]{1,0:T(8,128)(2,1)S(1)}, u32[]{:S(2)}, u32[]{:S(2)}) collective-permute-start(bf16[24,2048]{1,0:T(8,128)(2,1)S(1)} %get-tuple-element.56), channel_id=1, source_target_pairs={{0,24},{1,25},{2,26},{3,27},{4,28},{5,29},{6,30},{7,31},{8,16},{9,... | collective-permute-start | bytes 294920 | tf_op jit(solution)/shard_map/ppermute | solution.py:289

commit v5 on v4

--- a/solution.py
+++ b/solution.py
@@ -239,9 +239,26 @@
     )
 
 
-def late_kernel(per, normed, cot, w0, w1, full_t1, grad, *refs):
+def more_kernel(per, normed, cot, weight, full_t1, grad1, full_t, grad):
+    rows = grad.shape[0]
+    count = weight.shape[0]
+    g = lax.axis_index("grp")
+    c = lax.axis_index("node")
+    values_t = lax.dot_general(
+        weight[...], normed[:rows, :], LAST, preferred_element_type=F32
+    )
+    full_t[...] = full_t1[...]
+    for n, block in enumerate(LATE):
+        full_t[row_block(g, c, 0, block, per), :] = values_t[n * per : (n + 1) * per, :]
+    grad[...] = grad1[...] + lax.dot_general(
+        cot[:count, :], weight[...], FIRST, preferred_element_type=F32
+    )
+
+
+def late_kernel(per, normed, cot, weight, full_t1, grad, *refs):
     (own, g1, g2, g3), (values_far, grad_far, total_far) = refs[:4], refs[4:7]
-    joined, full_t, total, values, out, sem = refs[7:]
+    full_t, total, values, out, sem = refs[7:]
+    count = weight.shape[0]
     rows = grad.shape[0]
     half = out.shape[1] // 2
     g = lax.axis_index("grp")
@@ -257,20 +274,21 @@
     ]
     total[...] = own[...] + g1[...].astype(F32) + g2[...].astype(F32) + g3[...].astype(F32)
     stores[3].start()
-    stack((w0, w1), joined)
     for i in range(2):
         part = slice(i * half, (i + 1) * half)
         out[:, part] = (
             grad[:, part]
-            + lax.dot_general(cot[...], joined[:, part], FIRST, preferred_element_type=F32)
+            + lax.dot_general(
+                cot[count:, :], weight[:, part], FIRST, preferred_element_type=F32
+            )
         ).astype(BF16)
         stores[i].start()
-    values_t = lax.dot_general(joined[...], normed[:rows, :], LAST, preferred_element_type=F32)
+    values_t = lax.dot_general(
+        weight[...], normed[:rows, :], LAST, preferred_element_type=F32
+    )
     full_t[...] = full_t1[...]
-    for j in range(2):
-        for n, block in enumerate(LATE):
-            at = (j * len(LATE) + n) * per
-            full_t[row_block(g, c, j, block, per), :] = values_t[at : at + per, :]
+    for n, block in enumerate(LATE):
+        full_t[row_block(g, c, 1, block, per), :] = values_t[n * per : (n + 1) * per, :]
     values[...] = full_t[...].T.astype(BF16)
     stores[2].start()
     for store in stores:
@@ -377,7 +395,9 @@
     )
     got_b = move(sent_b, swap_first())
     w00, front, back = call(
-        join_kernel, [held(quarter, width, BF16)] + [held(2 * per, width, BF16)] * 2, *by_z
+        join_kernel,
+        [held(quarter, width, BF16)] + [held(2 * per, width, BF16)] * 2,
+        *by_z,
     )
     sent2 = call(second_kernel, held(quarter, width, BF16), far, got_a)
     got2 = move(sent2, swap_second())
@@ -392,7 +412,11 @@
     v10 = move(w10, swap_core())
 
     mine, s1, s2, s3 = call(
-        spread_kernel, [held(per, width, F32)] + [held(per, width, BF16)] * 3, near, got_b, got2
+        spread_kernel,
+        [held(per, width, F32)] + [held(per, width, BF16)] * 3,
+        near,
+        got_b,
+        got2,
     )
     others = [move(s, swap_z(k)) for k, s in ((1, s1), (2, s2), (3, s3))]
     full_t, grad = call(
@@ -423,19 +447,26 @@
         scratch=[pltpu.VMEM((4 * per, width), BF16)],
     )
     v11b = move(w11b, swap_core())
+    full_t, grad = call(
+        lambda *refs: more_kernel(per, *refs),
+        [held(height, rows, F32), held(rows, width, F32)],
+        normed,
+        late,
+        w11b,
+        full_t,
+        grad,
+    )
     values, input_grad, weight_grad = call(
         lambda *refs: late_kernel(per, *refs),
         [plain(rows, height, BF16), plain(rows, width, BF16), plain(per, width, F32)],
         normed,
         late,
-        w11b,
         v11b,
         full_t,
         grad,
         mine,
         *others,
         scratch=[
-            pltpu.VMEM((4 * per, width), BF16),
             pltpu.VMEM((height, rows), F32),
             pltpu.VMEM((per, width), F32),
             pltpu.VMEM((rows, height), BF16),

time: 56.2 us -> 58.7 us (1.044)
  waiting for transfers between devices: 26.9 us -> 30.2 us
  starting transfers between devices: 22.4 us -> 21.2 us
    ppermute x22, waiting for transfers between devices: 26.9 us -> 30.2 us  [move(): return lax.ppermute(array, AXES, pairs)]
    ppermute x22, starting transfers between devices: 22.4 us -> 21.2 us  [move(): return lax.ppermute(array, AXES, pairs)]
    pallas_call x10 -> x11, Pallas kernels: 5.91 us -> 6.36 us  [call(): pl.pallas_call(kernel, out_shape=outs, in_specs=[FAR if i in far else VME...]
  transfers between devices with their start and end apart: 22 -> 22, of which waited for: 6 -> 6; matrix products, arithmetic and copies ran while one was open for 0% -> 0% of each run, Pallas kernels for 8% -> 9%
where the time goes in v5:
time: 58.7 us; the launch traced here: 58.5 us
  waiting for transfers between devices  30.2 us (51%)
  starting transfers between devices  21.2 us (36%)
  Pallas kernels  6.36 us (11%)
  between operations  0.75 us (1%)
    ppermute x22, waiting for transfers between devices, move(): return lax.ppermute(array, AXES, pairs)  30.2 us
    ppermute x22, starting transfers between devices, move(): return lax.ppermute(array, AXES, pairs)  21.2 us
    pallas_call x11, Pallas kernels, call(): pl.pallas_call(kernel, out_shape=outs, in_specs=[FAR if i in far else VME...  6.36 us
  transfers between devices with their start and end apart: 22, of which 6 were waited for; matrix products, arithmetic and copies ran while one was open for 0% of the time, Pallas kernels for 9%

profile of v5, /device:TPU:0, one launch (start us, length us, event | category | flops | bytes accessed | tf_op | source)
XLA Modules:
  0.0 58.5 jit_solution(3956624586216693929)
XLA Ops:
  0.6 0.6 collective-permute-start
  1.2 0.1 collective-permute-start.1
  1.3 1.5 %shard_map.67 = (bf16[24,2048]{1,0:T(8,128)(2,1)S(1)}, bf16[128,2048]{1,0:T(8,128)(2,1)S(1)}, f32[576,128]{1,0:T(8,128)S(1)}, f32[96,128]{1,0:T(8,128)S(1)}, f32[96,128]{1,0:T(8,128)S(1)}) custom-call(bf16[128,2048]{1,0:T(8,128)(2,1)} %refs_0_.1, bf16[128,768]{1,0:T(8,128)(2,1)} %refs_1_.1, bf16[24,2048]{1,0:T(8,128)(2,1)} %refs_2_.1, f32[16,24]{1,0:T(8,128)} %bitcast.1), custom_call_target="tpu_custom_call" | custom-call | tf_op jit(solution)/shard_map/pallas_call | solution.py:315
  2.8 3.1 %collective-permute-start.2 = (bf16[24,2048]{1,0:T(8,128)(2,1)S(1)}, bf16[24,2048]{1,0:T(8,128)(2,1)S(1)}, u32[]{:S(2)}, u32[]{:S(2)}) collective-permute-start(bf16[24,2048]{1,0:T(8,128)(2,1)S(1)} %get-tuple-element.41.w0), channel_id=1, source_target_pairs={{0,8},{1,9},{2,10},{3,11},{4,12},{5,13},{6,14},{7,15},{8,0},{9,1},... | collective-permute-start | bytes 294920 | tf_op jit(solution)/shard_map/ppermute | solution.py:307
  5.8 0.0 collective-permute-done.1.refs_0_
  5.8 0.2 shard_map.68
  6.0 0.0 collective-permute-done.refs_0_
  6.0 0.5 shard_map.69
  6.5 1.5 %collective-permute-start.17 = (bf16[96,2048]{1,0:T(8,128)(2,1)S(1)}, bf16[96,2048]{1,0:T(8,128)(2,1)S(1)}, u32[]{:S(2)}, u32[]{:S(2)}) collective-permute-start(bf16[96,2048]{1,0:T(8,128)(2,1)S(1)} %get-tuple-element.56), channel_id=1, source_target_pairs={{0,2},{1,5},{2,0},{3,7},{4,6},{5,1},{6,4},{7,3},{8,10},{9,13},{10,... | collective-permute-start | bytes 1179656 | tf_op jit(solution)/shard_map/ppermute | solution.py:307
  8.1 2.6 %collective-permute-start.3 = (bf16[24,2048]{1,0:T(8,128)(2,1)S(1)}, bf16[24,2048]{1,0:T(8,128)(2,1)S(1)}, u32[]{:S(2)}, u32[]{:S(2)}) collective-permute-start(bf16[24,2048]{1,0:T(8,128)(2,1)S(1)} %get-tuple-element.41.w0), channel_id=1, source_target_pairs={{0,16},{1,17},{2,18},{3,19},{4,20},{5,21},{6,22},{7,23},{8,24},{9,... | collective-permute-start | bytes 294920 | tf_op jit(solution)/shard_map/ppermute | solution.py:307
  10.7 0.2 collective-permute-start.4
  10.9 0.0 collective-permute-done.2.w1
  10.9 6.8 %collective-permute-done.3.w2 = bf16[24,2048]{1,0:T(8,128)(2,1)S(1)} collective-permute-done((bf16[24,2048]{1,0:T(8,128)(2,1)S(1)}, bf16[24,2048]{1,0:T(8,128)(2,1)S(1)}, u32[]{:S(2)}, u32[]{:S(2)}) %collective-permute-start.3) | collective-permute-done | bytes 98336 | tf_op jit(solution)/shard_map/ppermute | solution.py:307
  17.7 0.0 collective-permute-done.4.w3
  17.7 0.1 shard_map.71
  17.7 1.5 %collective-permute-start.11 = (bf16[96,2048]{1,0:T(8,128)(2,1)S(1)}, bf16[96,2048]{1,0:T(8,128)(2,1)S(1)}, u32[]{:S(2)}, u32[]{:S(2)}) collective-permute-start(bf16[96,2048]{1,0:T(8,128)(2,1)S(1)} %get-tuple-element.46.refs_2_), channel_id=1, source_target_pairs={{0,2},{1,5},{2,0},{3,7},{4,6},{5,1},{6,4},{7,3},{8,10},{9,13},{10,... | collective-permute-start | bytes 1179656 | tf_op jit(solution)/shard_map/ppermute | solution.py:307
  19.2 1.1 %collective-permute-start.8 = (bf16[48,2048]{1,0:T(8,128)(2,1)S(1)}, bf16[48,2048]{1,0:T(8,128)(2,1)S(1)}, u32[]{:S(2)}, u32[]{:S(2)}) collective-permute-start(bf16[48,2048]{1,0:T(8,128)(2,1)S(1)} %get-tuple-element.44), channel_id=1, source_target_pairs={{0,4},{1,3},{2,6},{3,1},{4,0},{5,7},{6,2},{7,5},{8,12},{9,11},{10,... | collective-permute-start | bytes 589832 | tf_op jit(solution)/shard_map/ppermute | solution.py:307
  20.3 0.9 %collective-permute-start.5 = (bf16[48,2048]{1,0:T(8,128)(2,1)S(1)}, bf16[48,2048]{1,0:T(8,128)(2,1)S(1)}, u32[]{:S(2)}, u32[]{:S(2)}) collective-permute-start(bf16[48,2048]{1,0:T(8,128)(2,1)S(1)} %get-tuple-element.42), channel_id=1, source_target_pairs={{0,4},{1,3},{2,6},{3,1},{4,0},{5,7},{6,2},{7,5},{8,12},{9,11},{10,... | collective-permute-start | bytes 589832 | tf_op jit(solution)/shard_map/ppermute | solution.py:307
  21.3 5.1 %collective-permute-done.8.refs_3_ = bf16[48,2048]{1,0:T(8,128)(2,1)S(1)} collective-permute-done((bf16[48,2048]{1,0:T(8,128)(2,1)S(1)}, bf16[48,2048]{1,0:T(8,128)(2,1)S(1)}, u32[]{:S(2)}, u32[]{:S(2)}) %collective-permute-start.8) | collective-permute-done | bytes 196640 | tf_op jit(solution)/shard_map/ppermute | solution.py:307
  26.3 0.0 collective-permute-start.13
  26.3 1.3 %collective-permute-start.9 = (bf16[48,2048]{1,0:T(8,128)(2,1)S(1)}, bf16[48,2048]{1,0:T(8,128)(2,1)S(1)}, u32[]{:S(2)}, u32[]{:S(2)}) collective-permute-start(bf16[48,2048]{1,0:T(8,128)(2,1)S(1)} %collective-permute-done.8.refs_3_), channel_id=1, source_target_pairs={{0,2},{1,5},{2,0},{3,7},{4,6},{5,1},{6,4},{7,3},{8,10},{9,13},{10,... | collective-permute-start | bytes 589832 | tf_op jit(solution)/shard_map/ppermute | solution.py:307
  27.6 0.5 shard_map.70
  28.1 0.0 collective-permute-done.17.got_a
  28.2 0.8 %collective-permute-start.16 = (bf16[96,2048]{1,0:T(8,128)(2,1)S(1)}, bf16[96,2048]{1,0:T(8,128)(2,1)S(1)}, u32[]{:S(2)}, u32[]{:S(2)}) collective-permute-start(bf16[96,2048]{1,0:T(8,128)(2,1)S(1)} %get-tuple-element.54), channel_id=1, source_target_pairs={{0,2},{1,5},{2,0},{3,7},{4,6},{5,1},{6,4},{7,3},{8,10},{9,13},{10,... | collective-permute-start | bytes 1179656 | tf_op jit(solution)/shard_map/ppermute | solution.py:307
  29.0 0.1 shard_map.75
  29.1 0.0 collective-permute-done.5.refs_4_
  29.1 0.4 collective-permute-start.18
  29.4 0.0 collective-permute-done.11.refs_5_
  29.4 1.6 %collective-permute-start.6 = (bf16[48,2048]{1,0:T(8,128)(2,1)S(1)}, bf16[48,2048]{1,0:T(8,128)(2,1)S(1)}, u32[]{:S(2)}, u32[]{:S(2)}) collective-permute-start(bf16[48,2048]{1,0:T(8,128)(2,1)S(1)} %collective-permute-done.5.refs_4_), channel_id=1, source_target_pairs={{0,2},{1,5},{2,0},{3,7},{4,6},{5,1},{6,4},{7,3},{8,10},{9,13},{10,... | collective-permute-start | bytes 589832 | tf_op jit(solution)/shard_map/ppermute | solution.py:307
  31.0 0.0 collective-permute-done.13.refs_7_
  31.0 0.0 collective-permute-start.12
  31.0 1.4 %collective-permute-done.9.refs_2_ = bf16[48,2048]{1,0:T(8,128)(2,1)S(1)} collective-permute-done((bf16[48,2048]{1,0:T(8,128)(2,1)S(1)}, bf16[48,2048]{1,0:T(8,128)(2,1)S(1)}, u32[]{:S(2)}, u32[]{:S(2)}) %collective-permute-start.9) | collective-permute-done | bytes 196640 | tf_op jit(solution)/shard_map/ppermute | solution.py:307
  32.4 0.0 collective-permute-start.15
  32.4 10.2 %collective-permute-done.6.refs_2_ = bf16[48,2048]{1,0:T(8,128)(2,1)S(1)} collective-permute-done((bf16[48,2048]{1,0:T(8,128)(2,1)S(1)}, bf16[48,2048]{1,0:T(8,128)(2,1)S(1)}, u32[]{:S(2)}, u32[]{:S(2)}) %collective-permute-start.6) | collective-permute-done | bytes 196640 | tf_op jit(solution)/shard_map/ppermute | solution.py:307
  42.5 0.0 collective-permute-start.14
  42.5 0.0 collective-permute-done.16.got_b
  42.6 0.5 collective-permute-start.10
  43.1 0.0 collective-permute-done.18.got2
  43.1 0.1 collective-permute-start.7
  43.1 0.1 shard_map.76
  43.3 0.7 %collective-permute-done.14.refs_8_ = bf16[48,2048]{1,0:T(8,128)(2,1)S(1)} collective-permute-done((bf16[48,2048]{1,0:T(8,128)(2,1)S(1)}, bf16[48,2048]{1,0:T(8,128)(2,1)S(1)}, u32[]{:S(2)}, u32[]{:S(2)}) %collective-permute-start.14) | collective-permute-done | bytes 196640 | tf_op jit(solution)/shard_map/ppermute | solution.py:307
  44.0 2.7 %collective-permute-start.19 = (bf16[24,2048]{1,0:T(8,128)(2,1)S(1)}, bf16[24,2048]{1,0:T(8,128)(2,1)S(1)}, u32[]{:S(2)}, u32[]{:S(2)}) collective-permute-start(bf16[24,2048]{1,0:T(8,128)(2,1)S(1)} %get-tuple-element.58), channel_id=1, source_target_pairs={{0,8},{1,9},{2,10},{3,11},{4,12},{5,13},{6,14},{7,15},{8,0},{9,1},... | collective-permute-start | bytes 294920 | tf_op jit(solution)/shard_map/ppermute | solution.py:307
  46.7 0.0 collective-permute-done.12.refs_6_
  46.7 0.5 collective-permute-start.20
  47.2 0.0 collective-permute-done.15.refs_9_
  47.2 1.8 %collective-permute-start.21 = (bf16[24,2048]{1,0:T(8,128)(2,1)S(1)}, bf16[24,2048]{1,0:T(8,128)(2,1)S(1)}, u32[]{:S(2)}, u32[]{:S(2)}) collective-permute-start(bf16[24,2048]{1,0:T(8,128)(2,1)S(1)} %get-tuple-element.60), channel_id=1, source_target_pairs={{0,24},{1,25},{2,26},{3,27},{4,28},{5,29},{6,30},{7,31},{8,16},{9,... | collective-permute-start | bytes 294920 | tf_op jit(solution)/shard_map/ppermute | solution.py:307
  49.0 1.2 %shard_map.72 = (f32[768,128]{1,0:T(8,128)S(1)}, f32[128,2048]{1,0:T(8,128)S(1)}) custom-call(bf16[256,2048]{1,0:T(8,128)(2,1)S(1)} %get-tuple-element.37.refs_2_.refs_0_, bf16[576,128]{1,0:T(8,128)(2,1)S(1)} %get-tuple-element.45.refs_1_, bf16[96,2048]{1,0:T(8,128)(2,1)S(1)} %get-tuple-element.46.refs_2_, ...), custom_call_target="tpu_custom_call" | custom-call | tf_op jit(solution)/shard_map/pallas_call | solution.py:315
  50.2 0.0 collective-permute-done.10.refs_3_
  50.2 0.5 shard_map.73
  50.7 0.5 shard_map.74
  51.2 0.0 collective-permute-done.7.refs_2_
  51.2 0.0 collective-permute-done.19.refs_6_
  51.2 6.0 %collective-permute-done.20.refs_7_ = bf16[24,2048]{1,0:T(8,128)(2,1)S(1)} collective-permute-done((bf16[24,2048]{1,0:T(8,128)(2,1)S(1)}, bf16[24,2048]{1,0:T(8,128)(2,1)S(1)}, u32[]{:S(2)}, u32[]{:S(2)}) %collective-permute-start.20) | collective-permute-done | bytes 98336 | tf_op jit(solution)/shard_map/ppermute | solution.py:307
  57.2 0.0 collective-permute-done.21.refs_8_
  57.2 1.3 %shard_map.77 = (bf16[128,768]{1,0:T(8,128)(2,1)}, bf16[128,2048]{1,0:T(8,128)(2,1)}, f32[24,2048]{1,0:T(8,128)}) custom-call(bf16[256,2048]{1,0:T(8,128)(2,1)S(1)} %get-tuple-element.37.refs_2_.refs_0_, bf16[96,128]{1,0:T(8,128)(2,1)S(1)} %get-tuple-element.40.refs_1_, bf16[48,2048]{1,0:T(8,128)(2,1)S(1)} %collective-permute-done.7.refs_2_, ...), custom_call_target="tpu_custom_call" | custom-call | tf_op jit(solution)/shard_map/pallas_call | solution.py:315
Async XLA Ops:
  0.6 5.4 %collective-permute-start = (bf16[128,2048]{1,0:T(8,128)(2,1)}, bf16[128,2048]{1,0:T(8,128)(2,1)S(1)}, u32[]{:S(2)}, u32[]{:S(2)}) collective-permute-start(bf16[128,2048]{1,0:T(8,128)(2,1)} %refs_0_.1), channel_id=1, source_target_pairs={{0,1},{1,0},{2,3},{3,2},{4,5},{5,4},{6,7},{7,6},{8,9},{9,8},{10,11... | collective-permute-start | bytes 1572872 | tf_op jit(solution)/shard_map/ppermute | solution.py:307
  1.2 4.7 %collective-permute-start.1 = (bf16[128,768]{1,0:T(8,128)(2,1)}, bf16[128,768]{1,0:T(8,128)(2,1)S(1)}, u32[]{:S(2)}, u32[]{:S(2)}) collective-permute-start(bf16[128,768]{1,0:T(8,128)(2,1)} %refs_1_.1), channel_id=1, source_target_pairs={{0,1},{1,0},{2,3},{3,2},{4,5},{5,4},{6,7},{7,6},{8,9},{9,8},{10,11... | collective-permute-start | bytes 589832 | tf_op jit(solution)/shard_map/ppermute | solution.py:307
  2.8 8.1 %collective-permute-start.2 = (bf16[24,2048]{1,0:T(8,128)(2,1)S(1)}, bf16[24,2048]{1,0:T(8,128)(2,1)S(1)}, u32[]{:S(2)}, u32[]{:S(2)}) collective-permute-start(bf16[24,2048]{1,0:T(8,128)(2,1)S(1)} %get-tuple-element.41.w0), channel_id=1, source_target_pairs={{0,8},{1,9},{2,10},{3,11},{4,12},{5,13},{6,14},{7,15},{8,0},{9,1},... | collective-permute-start | bytes 294920 | tf_op jit(solution)/shard_map/ppermute | solution.py:307
  6.5 21.6 %collective-permute-start.17 = (bf16[96,2048]{1,0:T(8,128)(2,1)S(1)}, bf16[96,2048]{1,0:T(8,128)(2,1)S(1)}, u32[]{:S(2)}, u32[]{:S(2)}) collective-permute-start(bf16[96,2048]{1,0:T(8,128)(2,1)S(1)} %get-tuple-element.56), channel_id=1, source_target_pairs={{0,2},{1,5},{2,0},{3,7},{4,6},{5,1},{6,4},{7,3},{8,10},{9,13},{10,... | collective-permute-start | bytes 1179656 | tf_op jit(solution)/shard_map/ppermute | solution.py:307
  8.1 9.6 %collective-permute-start.3 = (bf16[24,2048]{1,0:T(8,128)(2,1)S(1)}, bf16[24,2048]{1,0:T(8,128)(2,1)S(1)}, u32[]{:S(2)}, u32[]{:S(2)}) collective-permute-start(bf16[24,2048]{1,0:T(8,128)(2,1)S(1)} %get-tuple-element.41.w0), channel_id=1, source_target_pairs={{0,16},{1,17},{2,18},{3,19},{4,20},{5,21},{6,22},{7,23},{8,24},{9,... | collective-permute-start | bytes 294920 | tf_op jit(solution)/shard_map/ppermute | solution.py:307
  10.7 7.0 %collective-permute-start.4 = (bf16[24,2048]{1,0:T(8,128)(2,1)S(1)}, bf16[24,2048]{1,0:T(8,128)(2,1)S(1)}, u32[]{:S(2)}, u32[]{:S(2)}) collective-permute-start(bf16[24,2048]{1,0:T(8,128)(2,1)S(1)} %get-tuple-element.41.w0), channel_id=1, source_target_pairs={{0,24},{1,25},{2,26},{3,27},{4,28},{5,29},{6,30},{7,31},{8,16},{9,... | collective-permute-start | bytes 294920 | tf_op jit(solution)/shard_map/ppermute | solution.py:307
  17.7 11.7 %collective-permute-start.11 = (bf16[96,2048]{1,0:T(8,128)(2,1)S(1)}, bf16[96,2048]{1,0:T(8,128)(2,1)S(1)}, u32[]{:S(2)}, u32[]{:S(2)}) collective-permute-start(bf16[96,2048]{1,0:T(8,128)(2,1)S(1)} %get-tuple-element.46.refs_2_), channel_id=1, source_target_pairs={{0,2},{1,5},{2,0},{3,7},{4,6},{5,1},{6,4},{7,3},{8,10},{9,13},{10,... | collective-permute-start | bytes 1179656 | tf_op jit(solution)/shard_map/ppermute | solution.py:307
  19.2 7.1 %collective-permute-start.8 = (bf16[48,2048]{1,0:T(8,128)(2,1)S(1)}, bf16[48,2048]{1,0:T(8,128)(2,1)S(1)}, u32[]{:S(2)}, u32[]{:S(2)}) collective-permute-start(bf16[48,2048]{1,0:T(8,128)(2,1)S(1)} %get-tuple-element.44), channel_id=1, source_target_pairs={{0,4},{1,3},{2,6},{3,1},{4,0},{5,7},{6,2},{7,5},{8,12},{9,11},{10,... | collective-permute-start | bytes 589832 | tf_op jit(solution)/shard_map/ppermute | solution.py:307
  20.3 8.7 %collective-permute-start.5 = (bf16[48,2048]{1,0:T(8,128)(2,1)S(1)}, bf16[48,2048]{1,0:T(8,128)(2,1)S(1)}, u32[]{:S(2)}, u32[]{:S(2)}) collective-permute-start(bf16[48,2048]{1,0:T(8,128)(2,1)S(1)} %get-tuple-element.42), channel_id=1, source_target_pairs={{0,4},{1,3},{2,6},{3,1},{4,0},{5,7},{6,2},{7,5},{8,12},{9,11},{10,... | collective-permute-start | bytes 589832 | tf_op jit(solution)/shard_map/ppermute | solution.py:307
  26.3 4.6 %collective-permute-start.13 = (bf16[48,2048]{1,0:T(8,128)(2,1)S(1)}, bf16[48,2048]{1,0:T(8,128)(2,1)S(1)}, u32[]{:S(2)}, u32[]{:S(2)}) collective-permute-start(bf16[48,2048]{1,0:T(8,128)(2,1)S(1)} %collective-permute-done.8.refs_3_), channel_id=1, source_target_pairs={{0,1},{1,0},{2,3},{3,2},{4,5},{5,4},{6,7},{7,6},{8,9},{9,8},{10,11... | collective-permute-start | bytes 589832 | tf_op jit(solution)/shard_map/ppermute | solution.py:307
  26.3 6.0 %collective-permute-start.9 = (bf16[48,2048]{1,0:T(8,128)(2,1)S(1)}, bf16[48,2048]{1,0:T(8,128)(2,1)S(1)}, u32[]{:S(2)}, u32[]{:S(2)}) collective-permute-start(bf16[48,2048]{1,0:T(8,128)(2,1)S(1)} %collective-permute-done.8.refs_3_), channel_id=1, source_target_pairs={{0,2},{1,5},{2,0},{3,7},{4,6},{5,1},{6,4},{7,3},{8,10},{9,13},{10,... | collective-permute-start | bytes 589832 | tf_op jit(solution)/shard_map/ppermute | solution.py:307
  28.2 14.4 %collective-permute-start.16 = (bf16[96,2048]{1,0:T(8,128)(2,1)S(1)}, bf16[96,2048]{1,0:T(8,128)(2,1)S(1)}, u32[]{:S(2)}, u32[]{:S(2)}) collective-permute-start(bf16[96,2048]{1,0:T(8,128)(2,1)S(1)} %get-tuple-element.54), channel_id=1, source_target_pairs={{0,2},{1,5},{2,0},{3,7},{4,6},{5,1},{6,4},{7,3},{8,10},{9,13},{10,... | collective-permute-start | bytes 1179656 | tf_op jit(solution)/shard_map/ppermute | solution.py:307
  29.1 14.0 %collective-permute-start.18 = (bf16[96,2048]{1,0:T(8,128)(2,1)S(1)}, bf16[96,2048]{1,0:T(8,128)(2,1)S(1)}, u32[]{:S(2)}, u32[]{:S(2)}) collective-permute-start(bf16[96,2048]{1,0:T(8,128)(2,1)S(1)} %shard_map.75), channel_id=1, source_target_pairs={{0,4},{1,3},{2,6},{3,1},{4,0},{5,7},{6,2},{7,5},{8,12},{9,11},{10,... | collective-permute-start | bytes 1179656 | tf_op jit(solution)/shard_map/ppermute | solution.py:307
  29.4 13.1 %collective-permute-start.6 = (bf16[48,2048]{1,0:T(8,128)(2,1)S(1)}, bf16[48,2048]{1,0:T(8,128)(2,1)S(1)}, u32[]{:S(2)}, u32[]{:S(2)}) collective-permute-start(bf16[48,2048]{1,0:T(8,128)(2,1)S(1)} %collective-permute-done.5.refs_4_), channel_id=1, source_target_pairs={{0,2},{1,5},{2,0},{3,7},{4,6},{5,1},{6,4},{7,3},{8,10},{9,13},{10,... | collective-permute-start | bytes 589832 | tf_op jit(solution)/shard_map/ppermute | solution.py:307
  31.0 15.7 %collective-permute-start.12 = (bf16[96,2048]{1,0:T(8,128)(2,1)S(1)}, bf16[96,2048]{1,0:T(8,128)(2,1)S(1)}, u32[]{:S(2)}, u32[]{:S(2)}) collective-permute-start(bf16[96,2048]{1,0:T(8,128)(2,1)S(1)} %get-tuple-element.46.refs_2_), channel_id=1, source_target_pairs={{0,1},{1,0},{2,3},{3,2},{4,5},{5,4},{6,7},{7,6},{8,9},{9,8},{10,11... | collective-permute-start | bytes 1179656 | tf_op jit(solution)/shard_map/ppermute | solution.py:307
  32.4 14.8 %collective-permute-start.15 = (bf16[96,2048]{1,0:T(8,128)(2,1)S(1)}, bf16[96,2048]{1,0:T(8,128)(2,1)S(1)}, u32[]{:S(2)}, u32[]{:S(2)}) collective-permute-start(bf16[96,2048]{1,0:T(8,128)(2,1)S(1)} %collective-permute-done.11.refs_5_), channel_id=1, source_target_pairs={{0,1},{1,0},{2,3},{3,2},{4,5},{5,4},{6,7},{7,6},{8,9},{9,8},{10,11... | collective-permute-start | bytes 1179656 | tf_op jit(solution)/shard_map/ppermute | solution.py:307
  42.5 1.4 %collective-permute-start.14 = (bf16[48,2048]{1,0:T(8,128)(2,1)S(1)}, bf16[48,2048]{1,0:T(8,128)(2,1)S(1)}, u32[]{:S(2)}, u32[]{:S(2)}) collective-permute-start(bf16[48,2048]{1,0:T(8,128)(2,1)S(1)} %collective-permute-done.5.refs_4_), channel_id=1, source_target_pairs={{0,1},{1,0},{2,3},{3,2},{4,5},{5,4},{6,7},{7,6},{8,9},{9,8},{10,11... | collective-permute-start | bytes 589832 | tf_op jit(solution)/shard_map/ppermute | solution.py:307
  42.6 7.7 %collective-permute-start.10 = (bf16[48,2048]{1,0:T(8,128)(2,1)S(1)}, bf16[48,2048]{1,0:T(8,128)(2,1)S(1)}, u32[]{:S(2)}, u32[]{:S(2)}) collective-permute-start(bf16[48,2048]{1,0:T(8,128)(2,1)S(1)} %collective-permute-done.9.refs_2_), channel_id=1, source_target_pairs={{0,1},{1,0},{2,3},{3,2},{4,5},{5,4},{6,7},{7,6},{8,9},{9,8},{10,11... | collective-permute-start | bytes 589832 | tf_op jit(solution)/shard_map/ppermute | solution.py:307
  43.1 8.1 %collective-permute-start.7 = (bf16[48,2048]{1,0:T(8,128)(2,1)S(1)}, bf16[48,2048]{1,0:T(8,128)(2,1)S(1)}, u32[]{:S(2)}, u32[]{:S(2)}) collective-permute-start(bf16[48,2048]{1,0:T(8,128)(2,1)S(1)} %collective-permute-done.6.refs_2_), channel_id=1, source_target_pairs={{0,1},{1,0},{2,3},{3,2},{4,5},{5,4},{6,7},{7,6},{8,9},{9,8},{10,11... | collective-permute-start | bytes 589832 | tf_op jit(solution)/shard_map/ppermute | solution.py:307
  44.0 7.2 %collective-permute-start.19 = (bf16[24,2048]{1,0:T(8,128)(2,1)S(1)}, bf16[24,2048]{1,0:T(8,128)(2,1)S(1)}, u32[]{:S(2)}, u32[]{:S(2)}) collective-permute-start(bf16[24,2048]{1,0:T(8,128)(2,1)S(1)} %get-tuple-element.58), channel_id=1, source_target_pairs={{0,8},{1,9},{2,10},{3,11},{4,12},{5,13},{6,14},{7,15},{8,0},{9,1},... | collective-permute-start | bytes 294920 | tf_op jit(solution)/shard_map/ppermute | solution.py:307
  46.7 10.5 %collective-permute-start.20 = (bf16[24,2048]{1,0:T(8,128)(2,1)S(1)}, bf16[24,2048]{1,0:T(8,128)(2,1)S(1)}, u32[]{:S(2)}, u32[]{:S(2)}) collective-permute-start(bf16[24,2048]{1,0:T(8,128)(2,1)S(1)} %get-tuple-element.59), channel_id=1, source_target_pairs={{0,16},{1,17},{2,18},{3,19},{4,20},{5,21},{6,22},{7,23},{8,24},{9,... | collective-permute-start | bytes 294920 | tf_op jit(solution)/shard_map/ppermute | solution.py:307
  47.2 10.0 %collective-permute-start.21 = (bf16[24,2048]{1,0:T(8,128)(2,1)S(1)}, bf16[24,2048]{1,0:T(8,128)(2,1)S(1)}, u32[]{:S(2)}, u32[]{:S(2)}) collective-permute-start(bf16[24,2048]{1,0:T(8,128)(2,1)S(1)} %get-tuple-element.60), channel_id=1, source_target_pairs={{0,24},{1,25},{2,26},{3,27},{4,28},{5,29},{6,30},{7,31},{8,16},{9,... | collective-permute-start | bytes 294920 | tf_op jit(solution)/shard_map/ppermute | solution.py:307
